TPU v7x, 32 devices: a whole 2x2x4 slice. The times are simulated.
32 devices in a mesh: fsdp: 8 (over z, x), ctx: 2 (over y), tp: 2 (over core).
Axes of the slice: x: 2, y: 2, z: 4, core: 2. Of those that a mesh axis runs over, the one named last changes fastest.
Arguments:
- hidden_in: bfloat16 [4096, 2048], P(('fsdp', 'ctx', 'tp')), may hold values from -6 to 6
- cotangent: bfloat16 [4096, 2048], P(('fsdp', 'ctx', 'tp')), may hold values from -6 to 6
- segments: int32 [4096], P('fsdp'), may hold values from 0 to 31, never falling along the last dimension, each value on 1 to 512 neighbouring positions
- w_query: bfloat16 [2048, 2048], P(('fsdp', 'ctx'), 'tp'), may hold values from -0.125 to 0.125
- key_projection_weight: bfloat16 [2048, 1024], P(('fsdp', 'ctx'), 'tp'), may hold values from -0.125 to 0.125
- value_projection_weight: bfloat16 [2048, 1024], P(('fsdp', 'ctx'), 'tp'), may hold values from -0.125 to 0.125
- w_out: bfloat16 [2048, 2048], P('tp', ('fsdp', 'ctx')), may hold values from -0.5 to 0.5
- w_gate: bfloat16 [2048, 6144], P('fsdp', ('ctx', 'tp')), may hold values from -0.125 to 0.125
- w_up: bfloat16 [2048, 6144], P('fsdp', ('ctx', 'tp')), may hold values from -0.125 to 0.125
- w_down: bfloat16 [6144, 2048], P(('ctx', 'tp'), 'fsdp'), may hold values from -0.078125 to 0.078125
- gain_attn: float32 [2048], replicated, may hold values from 0.5 to 1.5
- gain_mlp: float32 [2048], replicated, may hold values from 0.5 to 1.5
- gain_query: float32 [128], replicated, may hold values from 0.6 to 1.6
- key_norm_gain: float32 [128], replicated, may hold values from 0.6 to 1.6
Outputs:
- hidden_out: float32 [4096, 2048], P(('fsdp', 'ctx', 'tp'))
- grad_input: float32 [4096, 2048], P(('fsdp', 'ctx', 'tp'))
- grad_w_query: float32 [2048, 2048], P(('fsdp', 'ctx'), 'tp')
- grad_w_key: float32 [2048, 1024], P(('fsdp', 'ctx'), 'tp')
- grad_w_value: float32 [2048, 1024], P(('fsdp', 'ctx'), 'tp')
- grad_w_out: float32 [2048, 2048], P('tp', ('fsdp', 'ctx'))
- grad_w_gate: float32 [2048, 6144], P('fsdp', ('ctx', 'tp'))
- grad_w_up: float32 [2048, 6144], P('fsdp', ('ctx', 'tp'))
- grad_w_down: float32 [6144, 2048], P(('ctx', 'tp'), 'fsdp')
- grad_gain_attn: float32 [2048], replicated
- grad_gain_mlp: float32 [2048], replicated
- grad_gain_query: float32 [128], replicated
- grad_gain_key: float32 [128], replicated
Inputs may be any that keep to these rules, and one draw needn't show every extreme that they name: `segments`: segment numbers never fall along the tokens, and every number up to the largest names a run of 1 to 512 tokens.
All inputs are finite; a program needn't handle non-finite values.
Results may differ from a plain program's by a relative error of at most 0.014.
Values may be sent and summed in bfloat16 or wider, within the bound.
A program may use at most 256 MiB of HBM per device.

v0:
```python
import jax
import jax.numpy as jnp
from jax import lax
from jax.sharding import PartitionSpec as P

EPS = 1e-06
THETA = 1000000.0


def norm_moments(hidden):
    row_scale = lax.rsqrt(jnp.mean(hidden * hidden, axis=-1, keepdims=True) + EPS)
    return (hidden * row_scale, row_scale)


def norm_backward_step(grad_norm, unit_rows, row_scale, gain):
    scaled = grad_norm * gain
    return row_scale * (scaled - unit_rows * jnp.mean(scaled * unit_rows, axis=-1, keepdims=True))


def positions_of(segments):
    count = segments.shape[0]
    token_index = jnp.arange(count, dtype=jnp.int32)
    starts_here = jnp.concatenate([jnp.ones((1,), dtype=bool), segments[1:] != segments[:-1]])
    seg_start = lax.cummax(jnp.where(starts_here, token_index, jnp.zeros_like(token_index)), axis=0)
    return token_index - seg_start


def rotary_tables(positions, head_dim):
    half_dim = head_dim // 2
    freqs = THETA ** (-2.0 * jnp.arange(half_dim, dtype=jnp.float32) / head_dim)
    angles = positions.astype(jnp.float32)[:, None] * freqs[None, :]
    return (jnp.cos(angles)[:, None, :], jnp.sin(angles)[:, None, :])


def rotate(values_in, cosine, sine):
    half_dim = values_in.shape[-1] // 2
    first_half = values_in[..., :half_dim]
    second_half = values_in[..., half_dim:]
    return jnp.concatenate(
        [first_half * cosine - second_half * sine, second_half * cosine + first_half * sine],
        axis=-1,
    )


def rotate_back(grads_in, cosine, sine):
    half_dim = grads_in.shape[-1] // 2
    first_half = grads_in[..., :half_dim]
    second_half = grads_in[..., half_dim:]
    return jnp.concatenate(
        [first_half * cosine + second_half * sine, second_half * cosine - first_half * sine],
        axis=-1,
    )


def contract_rows(left, right):
    return lax.dot_general(
        left, right, (((0,), (0,)), ((), ())), preferred_element_type=jnp.float32
    )


def contract_cols(left, right):
    return lax.dot_general(
        left, right, (((1,), (1,)), ((), ())), preferred_element_type=jnp.float32
    )


def gather_rows(local_rows):
    return lax.all_gather(local_rows, "tp", axis=0, tiled=True)


def sum_rows(product, rows_out):
    return lax.psum_scatter(
        product(jnp.int32(0), rows_out * lax.axis_size("tp")), "tp", scatter_dimension=0, tiled=True
    )


def gather_wide(local_rows):
    return lax.all_gather(local_rows, ("ctx", "tp"), axis=0, tiled=True)


def sum_wide(product, rows_out):
    return lax.psum_scatter(
        product(jnp.int32(0), rows_out * lax.axis_size(("ctx", "tp"))),
        ("ctx", "tp"),
        scatter_dimension=0,
        tiled=True,
    )


def reduce_attn_grads(product, rows_out):
    return lax.psum_scatter(
        product(jnp.int32(0), rows_out * lax.axis_size(("fsdp", "ctx"))),
        ("fsdp", "ctx"),
        scatter_dimension=0,
        tiled=True,
    )


def block_mask(segments, token_index, row_start, row_end):
    same_segment = segments[row_start:row_end, None] == segments[None, :row_end]
    not_after = token_index[row_start:row_end, None] >= token_index[None, :row_end]
    return same_segment & not_after


def block_scores(query_block, key_block, allowed, score_scale):
    scores = (
        jnp.einsum("qgid,kgd->giqk", query_block, key_block, preferred_element_type=jnp.float32)
        * score_scale
    )
    return jnp.where(allowed, scores, -jnp.inf)


def attend_forward(rotated_query, key_rot, value_heads, segments, score_scale):
    packed_length = rotated_query.shape[0]
    block_rows = min(512, packed_length)
    token_index = jnp.arange(packed_length, dtype=jnp.int32)
    allowed = block_mask(segments, token_index, 0, block_rows)
    scores = block_scores(rotated_query, key_rot, allowed, score_scale)
    row_peak = jnp.max(scores, axis=-1, keepdims=True)
    log_total = row_peak + jnp.log(jnp.sum(jnp.exp(scores - row_peak), axis=-1, keepdims=True))
    soft_weights = jnp.exp(scores - log_total).astype(jnp.bfloat16)
    block_out = jnp.einsum(
        "giqk,kgd->qgid", soft_weights, value_heads, preferred_element_type=jnp.float32
    )
    outputs = block_out.astype(jnp.bfloat16)
    log_sums = [log_total]
    return (outputs, log_sums)


def attend_backward(
    rotated_query, key_rot, value_heads, attended, attention_grad, log_sums, segments, score_scale
):
    packed_length = rotated_query.shape[0]
    block_rows = min(512, packed_length)
    token_index = jnp.arange(packed_length, dtype=jnp.int32)
    grad_keys = jnp.zeros(key_rot.shape, jnp.float32)
    grad_values = jnp.zeros(value_heads.shape, jnp.float32)
    allowed = block_mask(segments, token_index, 0, block_rows)
    soft_exact = jnp.exp(block_scores(rotated_query, key_rot, allowed, score_scale) - log_sums[0])
    rounded_softmax = soft_exact.astype(jnp.bfloat16)
    delta = jnp.sum(attention_grad.astype(jnp.float32) * attended.astype(jnp.float32), axis=-1)
    delta_heads = jnp.transpose(delta, (1, 2, 0))[..., None]
    grad_soft = jnp.einsum(
        "qgid,kgd->giqk", attention_grad, value_heads, preferred_element_type=jnp.float32
    )
    score_gradient = (soft_exact * (grad_soft - delta_heads) * score_scale).astype(jnp.bfloat16)
    grad_queries = jnp.einsum(
        "giqk,kgd->qgid", score_gradient, key_rot, preferred_element_type=jnp.float32
    )
    grad_keys = grad_keys.at[:block_rows].add(
        jnp.einsum(
            "giqk,qgid->kgd", score_gradient, rotated_query, preferred_element_type=jnp.float32
        )
    )
    grad_values = grad_values.at[:block_rows].add(
        jnp.einsum(
            "giqk,qgid->kgd", rounded_softmax, attention_grad, preferred_element_type=jnp.float32
        )
    )
    return (grad_queries, grad_keys, grad_values)


def body(
    hidden_in,
    cotangent,
    segments,
    w_query,
    key_projection_weight,
    value_projection_weight,
    w_out,
    w_gate,
    w_up,
    w_down,
    gain_attn,
    gain_mlp,
    gain_query,
    key_norm_gain,
):
    full_query, full_key, full_value, full_out = (
        lax.all_gather(w_query, ("fsdp", "ctx"), axis=0, tiled=True),
        lax.all_gather(key_projection_weight, ("fsdp", "ctx"), axis=0, tiled=True),
        lax.all_gather(value_projection_weight, ("fsdp", "ctx"), axis=0, tiled=True),
        lax.all_gather(w_out, ("fsdp", "ctx"), axis=1, tiled=True),
    )
    full_gate, full_up, full_down = (
        lax.all_gather(w_gate, "fsdp", axis=0, tiled=True),
        lax.all_gather(w_up, "fsdp", axis=0, tiled=True),
        lax.all_gather(w_down, "fsdp", axis=1, tiled=True),
    )
    own_rows = hidden_in.shape[0]
    attn_shard_rows = w_query.shape[0]
    head_dim = gain_query.shape[0]
    score_scale = head_dim ** (-0.5)
    residual_in = hidden_in.astype(jnp.float32)
    unit_one, scale_one = norm_moments(residual_in)
    normed_one = gather_rows((unit_one * gain_attn).astype(jnp.bfloat16))
    query_tok = jnp.dot(normed_one, full_query, preferred_element_type=jnp.float32).astype(
        jnp.bfloat16
    )
    key_tok = jnp.dot(normed_one, full_key, preferred_element_type=jnp.float32).astype(jnp.bfloat16)
    value_tok = jnp.dot(normed_one, full_value, preferred_element_type=jnp.float32).astype(
        jnp.bfloat16
    )
    query_heads, key_heads, value_heads = (
        lax.all_to_all(query_tok, "ctx", split_axis=1, concat_axis=0, tiled=True),
        lax.all_to_all(key_tok, "ctx", split_axis=1, concat_axis=0, tiled=True),
        lax.all_to_all(value_tok, "ctx", split_axis=1, concat_axis=0, tiled=True),
    )
    packed_length = query_heads.shape[0]
    query_count = query_heads.shape[1] // head_dim
    kv_count = key_heads.shape[1] // head_dim
    query_group_width = query_count // kv_count
    cosine, sine = rotary_tables(positions_of(segments), head_dim)
    unit_q, scale_q = norm_moments(
        query_heads.astype(jnp.float32).reshape(packed_length, query_count, head_dim)
    )
    unit_key_rows, key_norm_scale = norm_moments(
        key_heads.astype(jnp.float32).reshape(packed_length, kv_count, head_dim)
    )
    rotated_query = (
        rotate(unit_q * gain_query, cosine, sine)
        .astype(jnp.bfloat16)
        .reshape(packed_length, kv_count, query_group_width, head_dim)
    )
    key_rot = rotate(unit_key_rows * key_norm_gain, cosine, sine).astype(jnp.bfloat16)
    value_split = value_heads.reshape(packed_length, kv_count, head_dim)
    attended, log_sums = attend_forward(rotated_query, key_rot, value_split, segments, score_scale)
    attended_tok = lax.all_to_all(
        attended.reshape(packed_length, query_count * head_dim),
        "ctx",
        split_axis=0,
        concat_axis=1,
        tiled=True,
    )

    def out_product(row_start, row_count):
        return jnp.dot(attended_tok, full_out, preferred_element_type=jnp.float32)

    residual_mid = residual_in + sum_rows(out_product, own_rows)
    unit_two, scale_two = norm_moments(residual_mid)
    normed_two = gather_wide((unit_two * gain_mlp).astype(jnp.bfloat16))
    gate_pre = jnp.dot(normed_two, full_gate, preferred_element_type=jnp.float32)
    up_pre = jnp.dot(normed_two, full_up, preferred_element_type=jnp.float32)
    gate_sig = jax.nn.sigmoid(gate_pre)
    gate_act = gate_pre * gate_sig
    mixed = (gate_act * up_pre).astype(jnp.bfloat16)

    def down_product(row_start, row_count):
        return jnp.dot(mixed, full_down, preferred_element_type=jnp.float32)

    hidden_out = residual_mid + sum_wide(down_product, own_rows)
    grad_rows = gather_wide(cotangent)
    grad_mixed = contract_cols(grad_rows, full_down)
    grad_gate = (grad_mixed * up_pre * gate_sig * (1.0 + gate_pre * (1.0 - gate_sig))).astype(
        jnp.bfloat16
    )
    grad_up = (grad_mixed * gate_act).astype(jnp.bfloat16)

    def mlp_input(row_start, row_count):
        return contract_cols(grad_gate, full_gate) + contract_cols(grad_up, full_up)

    grad_norm_two = sum_wide(mlp_input, own_rows)
    local_gain_mlp = jnp.sum(grad_norm_two * unit_two, axis=0)
    grad_mid = cotangent.astype(jnp.float32) + norm_backward_step(
        grad_norm_two, unit_two, scale_two, gain_mlp
    )
    mlp_grads = lax.psum_scatter(
        jnp.concatenate(
            [
                contract_rows(normed_two, grad_gate),
                contract_rows(normed_two, grad_up),
                contract_rows(grad_rows, mixed),
            ],
            axis=1,
        ),
        "fsdp",
        scatter_dimension=0,
        tiled=True,
    )
    hidden_part = w_gate.shape[1]
    grad_w_gate = mlp_grads[:, :hidden_part]
    grad_w_up = mlp_grads[:, hidden_part : 2 * hidden_part]
    grad_w_down = mlp_grads[:, 2 * hidden_part :].T
    grad_mid_rows = gather_rows(grad_mid.astype(jnp.bfloat16))
    grad_att_tok = contract_cols(grad_mid_rows, full_out).astype(jnp.bfloat16)
    attention_grad = lax.all_to_all(grad_att_tok, "ctx", split_axis=1, concat_axis=0, tiled=True)
    grad_att_split = attention_grad.reshape(packed_length, kv_count, query_group_width, head_dim)
    grad_query_rot, rotated_key_grad, value_grad_total = attend_backward(
        rotated_query,
        key_rot,
        value_split,
        attended,
        grad_att_split,
        log_sums,
        segments,
        score_scale,
    )
    grad_unit_q = rotate_back(
        grad_query_rot.reshape(packed_length, query_count, head_dim), cosine, sine
    )
    unit_key_grad = rotate_back(rotated_key_grad, cosine, sine)
    local_gain_query = jnp.sum(grad_unit_q * unit_q, axis=(0, 1))
    local_gain_key = jnp.sum(unit_key_grad * unit_key_rows, axis=(0, 1))
    grad_query = (
        norm_backward_step(grad_unit_q, unit_q, scale_q, gain_query)
        .astype(jnp.bfloat16)
        .reshape(packed_length, query_count * head_dim)
    )
    key_gradient = (
        norm_backward_step(unit_key_grad, unit_key_rows, key_norm_scale, key_norm_gain)
        .astype(jnp.bfloat16)
        .reshape(packed_length, kv_count * head_dim)
    )
    value_gradient = value_grad_total.astype(jnp.bfloat16).reshape(
        packed_length, kv_count * head_dim
    )
    grad_query_tok, grad_key_tok, grad_value_tok = (
        lax.all_to_all(grad_query, "ctx", split_axis=0, concat_axis=1, tiled=True),
        lax.all_to_all(key_gradient, "ctx", split_axis=0, concat_axis=1, tiled=True),
        lax.all_to_all(value_gradient, "ctx", split_axis=0, concat_axis=1, tiled=True),
    )

    def attn_input(row_start, row_count):
        return (
            contract_cols(grad_query_tok, full_query)
            + contract_cols(grad_key_tok, full_key)
            + contract_cols(grad_value_tok, full_value)
        )

    grad_norm_one = sum_rows(attn_input, own_rows)
    local_gain_attn = jnp.sum(grad_norm_one * unit_one, axis=0)
    grad_input = grad_mid + norm_backward_step(grad_norm_one, unit_one, scale_one, gain_attn)

    def attn_weight_terms(row_start, row_count):
        return jnp.concatenate(
            [
                contract_rows(normed_one, grad_query_tok),
                contract_rows(normed_one, grad_key_tok),
                contract_rows(normed_one, grad_value_tok),
                contract_rows(grad_mid_rows, attended_tok),
            ],
            axis=1,
        )

    attn_grads = reduce_attn_grads(attn_weight_terms, attn_shard_rows)
    query_cols = w_query.shape[1]
    key_cols = key_projection_weight.shape[1]
    grad_w_query = attn_grads[:, :query_cols]
    grad_w_key = attn_grads[:, query_cols : query_cols + key_cols]
    grad_w_value = attn_grads[:, query_cols + key_cols : query_cols + 2 * key_cols]
    grad_w_out = attn_grads[:, query_cols + 2 * key_cols :].T
    grad_gain_attn, grad_gain_mlp, grad_gain_query, grad_gain_key = lax.psum(
        (local_gain_attn, local_gain_mlp, local_gain_query, local_gain_key), ("fsdp", "ctx", "tp")
    )
    return (
        hidden_out,
        grad_input,
        grad_w_query,
        grad_w_key,
        grad_w_value,
        grad_w_out,
        grad_w_gate,
        grad_w_up,
        grad_w_down,
        grad_gain_attn,
        grad_gain_mlp,
        grad_gain_query,
        grad_gain_key,
    )


def solution(mesh):
    placed = (
        P(("fsdp", "ctx", "tp"), None),
        P(("fsdp", "ctx", "tp"), None),
        P("fsdp"),
        P(("fsdp", "ctx"), "tp"),
        P(("fsdp", "ctx"), "tp"),
        P(("fsdp", "ctx"), "tp"),
        P("tp", ("fsdp", "ctx")),
        P("fsdp", ("ctx", "tp")),
        P("fsdp", ("ctx", "tp")),
        P(("ctx", "tp"), "fsdp"),
        P(),
        P(),
        P(),
        P(),
    )
    return jax.shard_map(
        body,
        mesh=mesh,
        in_specs=placed,
        out_specs=(
            P(("fsdp", "ctx", "tp"), None),
            P(("fsdp", "ctx", "tp"), None),
            P(("fsdp", "ctx"), "tp"),
            P(("fsdp", "ctx"), "tp"),
            P(("fsdp", "ctx"), "tp"),
            P("tp", ("fsdp", "ctx")),
            P("fsdp", ("ctx", "tp")),
            P("fsdp", ("ctx", "tp")),
            P(("ctx", "tp"), "fsdp"),
            P(),
            P(),
            P(),
            P(),
        ),
        check_vma=False,
    )
```

profile of v0, /device:TPU:0, one launch (start us, length us, event | category | flops | bytes accessed | tf_op | source)
XLA Modules:
  0.0 1894.7 jit_solution(11246895614089492385)
XLA Ops:
  16.6 6.7 all-gather.12.cloned.1.call-done
  23.2 64.6 %all-gather.14.cloned.1.call-done = bf16[2048,512]{1,0:T(8,128)(2,1)} async-done(((bf16[128,512]{1,0:T(8,128)(2,1)}), bf16[2048,512]{1,0:T(8,128)(2,1)}) %all-gather.14.cloned.1.call-update) | async-done | bytes 2097168 | tf_op jit(solution)/shard_map/all_gather | solution.py:182
  87.8 2.6 convolution_convert_fusion.4
  91.2 3.4 all-to-all-start
  94.6 55.3 %all-gather.16.cloned.1.call-done = bf16[2048,512]{1,0:T(8,128)(2,1)} async-done(((bf16[128,512]{1,0:T(8,128)(2,1)}), bf16[2048,512]{1,0:T(8,128)(2,1)}) %all-gather.16.cloned.1.call-update) | async-done | bytes 2097168 | tf_op jit(solution)/shard_map/all_gather | solution.py:181
  149.9 2.3 convolution_convert_fusion.3
  152.9 3.4 all-to-all-start.1
  158.3 3.3 all-to-all-done.1
  162.8 64.3 %all-gather.18.cloned.1.call-done = bf16[2048,1024]{1,0:T(8,128)(2,1)} async-done(((bf16[128,1024]{1,0:T(8,128)(2,1)}), bf16[2048,1024]{1,0:T(8,128)(2,1)}) %all-gather.18.cloned.1.call-update) | async-done | bytes 4194320 | tf_op jit(solution)/shard_map/all_gather | solution.py:180
  227.2 3.4 convolution_convert_fusion.2
  231.4 3.6 all-to-all-start.2
  236.1 8.8 all-to-all-done.2
  255.9 3.5 all-to-all-start.3
  259.6 61.2 %all-gather.20.cloned.1.call-done = bf16[1024,2048]{1,0:T(8,128)(2,1)} async-done(((bf16[1024,128]{1,0:T(8,128)(2,1)}), bf16[1024,2048]{1,0:T(8,128)(2,1)}) %all-gather.20.cloned.1.call-update) | async-done | bytes 4194320 | tf_op jit(solution)/shard_map/all_gather | solution.py:183
  320.9 5.0 fusion.35
  326.5 7.3 reduce-scatter.7.cloned.1.call-done
  338.5 87.2 %all-gather.26.cloned.1.call-done = bf16[2048,1536]{1,0:T(8,128)(2,1)} async-done(((bf16[256,1536]{1,0:T(8,128)(2,1)}), bf16[2048,1536]{1,0:T(8,128)(2,1)}) %all-gather.26.cloned.1.call-update) | async-done | bytes 6291472 | tf_op jit(solution)/shard_map/all_gather | solution.py:187
  425.7 22.7 %all-gather.22.cloned.1.call-done = bf16[512,2048]{1,0:T(8,128)(2,1)} async-done(((bf16[128,2048]{1,0:T(8,128)(2,1)}), bf16[512,2048]{1,0:T(8,128)(2,1)}) %all-gather.22.cloned.1.call-update) | async-done | bytes 2097168 | tf_op jit(solution)/shard_map/all_gather | solution.py:78
  448.5 8.5 fusion.37
  457.0 92.5 %all-gather.24.cloned.1.call-done = bf16[2048,1536]{1,0:T(8,128)(2,1)} async-done(((bf16[256,1536]{1,0:T(8,128)(2,1)}), bf16[2048,1536]{1,0:T(8,128)(2,1)}) %all-gather.24.cloned.1.call-update) | async-done | bytes 6291472 | tf_op jit(solution)/shard_map/all_gather | solution.py:186
  549.5 8.5 fusion.36
  558.0 13.8 all-gather.30.cloned.1.call-done
  571.8 101.8 %all-gather.28.cloned.1.call-done = bf16[1536,2048]{1,0:T(8,128)(2,1)} async-done(((bf16[1536,256]{1,0:T(8,128)(2,1)}), bf16[1536,2048]{1,0:T(8,128)(2,1)}) %all-gather.28.cloned.1.call-update) | async-done | bytes 6291472 | tf_op jit(solution)/shard_map/all_gather | solution.py:188
  673.6 11.2 multiply_convert_fusion
  684.9 3.4 fusion.39
  688.4 5.0 convolution_add_fusion
  693.9 42.3 %reduce-scatter.11.cloned.1.call-done = f32[128,2048]{1,0:T(8,128)} async-done(((f32[512,2048]{1,0:T(8,128)}), f32[128,2048]{1,0:T(8,128)}) %reduce-scatter.11.cloned.1.call-update) | async-done | bytes 1048592 | tf_op jit(solution)/shard_map/reduce_scatter | solution.py:82
  737.8 2.3 fusion.32
  740.1 9.2 all-gather.32.cloned.1.call-done
  749.3 4.6 convolution_convert_fusion.1
  756.0 4.2 all-to-all-start.4
  761.8 2.3 mul.460
  765.6 2.7 mul.441
  769.0 2.4 copy.216
  774.8 4.1 fusion.2
  782.2 2.4 copy.259
  797.6 4.3 all-to-all-start.6
  801.9 2.4 copy.258
  806.4 2.9 multiply_reduce_fusion.2
  810.9 2.7 mul.457
  813.6 2.7 concatenate.45
  816.3 2.7 multiply_reduce_fusion
  819.0 3.5 all-to-all-start.5
  822.5 3.4 fusion.12
  827.8 2.6 all-to-all-done.5
  830.4 4.1 all-to-all-start.7
  834.8 3.7 fusion.40
  839.8 3.8 convolution_add_fusion.1
  843.7 8.7 fusion.38
  852.6 2.8 fusion.46
  855.5 3.7 fusion.45
  859.2 2.7 fusion.44
  861.9 5.5 fusion.43
  867.3 16.0 pad_maximum_fusion.1
  883.4 10.3 convolution_bitcast_fusion
  893.7 6.4 fusion.42
  900.1 6.5 fusion.41
  906.6 25.2 %pad_maximum_fusion = f32[2048,4608]{0,1:T(8,128)} fusion(f32[2048,1536]{0,1:T(8,128)} %convolution_bitcast_fusion, f32[2048,1536]{0,1:T(8,128)} %fusion.42, f32[2048,1536]{0,1:T(8,128)} %fusion.41), kind=kLoop, calls=%fused_computation | loop fusion | flops 18874368 | bytes 75497472 | tf_op jit(solution)/shard_map/concatenate | solution.py:268
  934.5 44.3 %all-reduce = (f32[2048]{0:T(1024)}, f32[2048]{0:T(1024)}, f32[128]{0:T(128)}, f32[128]{0:T(128)}) all-reduce(f32[2048]{0:T(1024)S(1)} %get-tuple-element.146, f32[2048]{0:T(1024)S(1)} %get-tuple-element.144, f32[128]{0:T(128)S(1)} %bitcast_reduce_fusion, ...), channel_id=1, replica_groups=mesh['fsdp'=8,'ctx'=2,'tp'=2] {'fsdp','ctx','tp'}, use_global_device_ids=true, to_apply=%region_20.21 | all-reduce | flops 4352 | bytes 34816 | tf_op jit(solution)/shard_map/psum | solution.py:352
  978.8 3.3 fusion.17
  982.1 289.0 %reduce-scatter.15.cloned.1.call-done = f32[128,3072]{0,1:T(8,128)} async-done(((f32[2048,3072]{0,1:T(8,128)}), f32[128,3072]{0,1:T(8,128)}) %reduce-scatter.15.cloned.1.call-update) | async-done | bytes 1572880 | tf_op jit(solution)/shard_map/reduce_scatter | solution.py:91
  1276.9 601.3 %reduce-scatter.17.cloned.1.call-done = f32[256,4608]{0,1:T(8,128)} async-done(((f32[2048,4608]{0,1:T(8,128)}), f32[256,4608]{0,1:T(8,128)}) %reduce-scatter.17.cloned.1.call-update) | async-done | bytes 4718608 | tf_op jit(solution)/shard_map/reduce_scatter | solution.py:267
  1878.2 4.3 slice_bitcast_fusion
  1882.5 3.0 copy.237
  (228 shorter events, 76.2 us)
Async XLA Ops:
  8.0 15.2 all-gather.12.cloned.1.call-start
  9.3 5.5 copy-start.40
  11.4 76.5 %all-gather.14.cloned.1.call-start = ((), (), s32[]{:S(2)}) async-start(), calls=%async_computation.15 | async-start | bytes 2228224 | tf_op jit(solution)/shard_map/all_gather | solution.py:182
  12.1 137.8 %all-gather.16.cloned.1.call-start = ((), (), s32[]{:S(2)}) async-start(), calls=%async_computation.16 | async-start | bytes 2228224 | tf_op jit(solution)/shard_map/all_gather | solution.py:181
  12.8 214.3 %all-gather.18.cloned.1.call-start = ((), (), s32[]{:S(2)}) async-start(), calls=%async_computation.17 | async-start | bytes 4456448 | tf_op jit(solution)/shard_map/all_gather | solution.py:180
  13.4 307.4 %all-gather.20.cloned.1.call-start = ((), (), s32[]{:S(2)}) async-start(), calls=%async_computation.18 | async-start | bytes 4456448 | tf_op jit(solution)/shard_map/all_gather | solution.py:183
  16.5 232.6 %copy-start.6 = (f32[512,64]{1,0:T(8,128)}, f32[512,64]{1,0:T(8,128)S(1)}, u32[]{:S(2)}) copy-start(f32[512,64]{1,0:T(8,128)S(1)} %get-tuple-element.185) | copy-start | bytes 393220
  16.5 139.9 %copy-start.39 = (s32[512]{0:T(512)S(1)}, s32[512]{0:T(512)}, u32[]{:S(2)}) copy-start(s32[512]{0:T(512)} %param.24) | copy-start | bytes 6148
  23.2 126.7 %copy-start.4 = (bf16[256,2048]{1,0:T(8,128)(2,1)S(1)}, bf16[256,2048]{1,0:T(8,128)(2,1)}, u32[]{:S(2)}) copy-start(bf16[256,2048]{1,0:T(8,128)(2,1)} %all-gather.12.cloned.1.call-done) | copy-start | bytes 3145732
  91.2 61.8 %all-to-all-start = ((bf16[256,2,256]{2,0,1:T(8,128)(2,1)}), bf16[256,2,256]{2,0,1:T(8,128)(2,1)S(1)}, u32[]{:S(2)}, u32[]{:S(2)}) async-start(bf16[256,2,256]{2,0,1:T(8,128)(2,1)} %bitcast.170), calls=%async_computation | async-start | bytes 524288 | tf_op jit(solution)/shard_map/all_to_all | solution.py:207
  94.6 68.0 %copy-start.43 = (f32[128]{0:T(128)S(1)}, f32[128]{0:T(128)}, u32[]{:S(2)}) copy-start(f32[128]{0:T(128)} %param.35) | copy-start | bytes 1540
  152.9 8.6 all-to-all-start.1
  157.4 4.2 copy-start.35
  161.6 69.0 %copy-start.29 = (bf16[256,2,256]{2,0,1:T(8,128)(2,1)}, bf16[256,2,256]{2,0,1:T(8,128)(2,1)S(1)}, u32[]{:S(2)}) copy-start(bf16[256,2,256]{2,0,1:T(8,128)(2,1)S(1)} %all-to-all-done.1) | copy-start | bytes 786436
  231.4 16.9 copy-start.42
  231.4 13.5 all-to-all-start.2
  250.1 3.4 copy-start.36
  254.8 66.0 %copy-start.32 = (bf16[512,2,2,128]{0,3,2,1:T(8,128)(2,1)}, bf16[512,2,2,128]{0,3,2,1:T(8,128)(2,1)S(1)}, u32[]{:S(2)}) copy-start(bf16[512,2,2,128]{0,3,2,1:T(8,128)(2,1)S(1)} %fusion.10) | copy-start | bytes 1572868
  255.9 65.0 %all-to-all-start.3 = ((bf16[2,256,512]{1,2,0:T(8,128)(2,1)}), bf16[2,256,512]{1,2,0:T(8,128)(2,1)S(1)}, u32[]{:S(2)}, u32[]{:S(2)}) async-start(bf16[2,256,512]{1,2,0:T(8,128)(2,1)} %copy.214), calls=%async_computation.3 | async-start | bytes 1048576 | tf_op jit(solution)/shard_map/all_to_all | solution.py:228
  259.4 74.5 %reduce-scatter.7.cloned.1.call-start = ((), (), s32[]{:S(2)}) async-start(), calls=%async_computation.19 | async-start | bytes 3145728 | tf_op jit(solution)/shard_map/reduce_scatter | solution.py:72
  320.8 5.1 copy-start.22
  320.8 13.0 copy-start.1
  325.9 9.5 copy-start.37
  325.9 99.8 %all-gather.26.cloned.1.call-start = ((), (), s32[]{:S(2)}) async-start(), calls=%async_computation.22 | async-start | bytes 7077888 | tf_op jit(solution)/shard_map/all_gather | solution.py:187
  326.5 122.0 %all-gather.22.cloned.1.call-start = ((), (), s32[]{:S(2)}) async-start(), calls=%async_computation.20 | async-start | bytes 2621440 | tf_op jit(solution)/shard_map/all_gather | solution.py:78
  336.4 213.1 %all-gather.24.cloned.1.call-start = ((), (), s32[]{:S(2)}) async-start(), calls=%async_computation.21 | async-start | bytes 7077888 | tf_op jit(solution)/shard_map/all_gather | solution.py:186
  337.0 234.8 %all-gather.30.cloned.1.call-start = ((), (), s32[]{:S(2)}) async-start(), calls=%async_computation.25 | async-start | bytes 2621440 | tf_op jit(solution)/shard_map/all_gather | solution.py:78
  337.7 335.9 %all-gather.28.cloned.1.call-start = ((), (), s32[]{:S(2)}) async-start(), calls=%async_computation.23 | async-start | bytes 7077888 | tf_op jit(solution)/shard_map/all_gather | solution.py:188
  338.5 397.7 %reduce-scatter.11.cloned.1.call-start = ((), (), s32[]{:S(2)}) async-start(), calls=%async_computation.26 | async-start | bytes 5242880 | tf_op jit(solution)/shard_map/reduce_scatter | solution.py:82
  673.6 11.2 copy-start.44
  673.6 14.7 slice-start
  684.8 3.5 copy-start.46
  684.9 3.5 copy-start.48
  684.9 3.5 slice-start.1
  693.4 44.3 %copy-start.14 = (bf16[128,2048]{1,0:T(8,128)(2,1)S(1)}, bf16[128,2048]{1,0:T(8,128)(2,1)}, u32[]{:S(2)}) copy-start(bf16[128,2048]{1,0:T(8,128)(2,1)} %param.23) | copy-start | bytes 1572868
  693.4 55.9 %all-gather.32.cloned.1.call-start = ((), (), s32[]{:S(2)}) async-start(), calls=%async_computation.27 | async-start | bytes 1572864 | tf_op jit(solution)/shard_map/all_gather | solution.py:68
  740.1 23.9 %copy-start.19 = (f32[512,4]{1,0:T(8,128)S(1)}, f32[512,4]{1,0:T(8,128)}, u32[]{:S(2)}) copy-start(f32[512,4]{1,0:T(8,128)} %copy-done.18) | copy-start | bytes 24580
  756.0 13.0 all-to-all-start.4
  765.6 7.9 copy-start.33
  774.7 4.1 copy-start.11
  774.8 4.1 copy-start.13
  774.8 5.7 copy-start.26
  774.8 5.7 copy-start.28
  780.5 4.1 copy-start.7
  787.1 8.3 copy-start.31
  795.5 10.9 copy-start.20
  797.6 21.3 %all-to-all-start.6 = ((bf16[2,256,256]{2,1,0:T(8,128)(2,1)}), bf16[2,256,256]{2,1,0:T(8,128)(2,1)}, u32[]{:S(2)}, u32[]{:S(2)}) async-start(bf16[2,256,256]{2,1,0:T(8,128)(2,1)} %get-tuple-element.175), calls=%async_computation.9 | async-start | bytes 524288 | tf_op jit(solution)/shard_map/all_to_all | solution.py:319
  809.3 7.0 copy-start.9
  809.3 7.0 copy-start.21
  813.6 8.9 copy-start.17
  813.6 8.9 copy-start.34
  819.0 11.5 all-to-all-start.5
  830.4 9.4 all-to-all-start.7
  834.6 97.4 %reduce-scatter.13.cloned.1.call-start = ((), (), s32[]{:S(2)}) async-start(), calls=%async_computation.28 | async-start | bytes 3145728 | tf_op jit(solution)/shard_map/reduce_scatter | solution.py:72
  834.8 3.7 copy-start.23
  834.8 3.7 copy-start.30
  843.6 135.2 %reduce-scatter.9.cloned.1.call-start = ((), (), s32[]{:S(2)}) async-start(), calls=%async_computation.24 | async-start | bytes 5242880 | tf_op jit(solution)/shard_map/reduce_scatter | solution.py:82
  852.4 418.7 %reduce-scatter.15.cloned.1.call-start = ((), (), s32[]{:S(2)}) async-start(), calls=%async_computation.29 | async-start | bytes 26738688 | tf_op jit(solution)/shard_map/reduce_scatter | solution.py:91
  883.4 10.3 copy-start.45
  883.4 994.8 %reduce-scatter.17.cloned.1.call-start = ((), (), s32[]{:S(2)}) async-start(), calls=%async_computation.30 | async-start | bytes 42467328 | tf_op jit(solution)/shard_map/reduce_scatter | solution.py:267
  883.4 10.3 copy-start.49
  893.7 6.4 copy-start.47
  931.9 46.9 %copy-start.3 = (f32[128,2048]{1,0:T(8,128)S(1)}, f32[128,2048]{1,0:T(8,128)}, u32[]{:S(2)}) copy-start(f32[128,2048]{1,0:T(8,128)} %reduce-scatter.11.cloned.1.call-done) | copy-start | bytes 3145732
  931.9 46.9 %copy-start.15 = (bf16[128,2048]{1,0:T(8,128)(2,1)S(1)}, bf16[128,2048]{1,0:T(8,128)(2,1)}, u32[]{:S(2)}) copy-start(bf16[128,2048]{1,0:T(8,128)(2,1)} %param.23) | copy-start | bytes 1572868
  (13 other events, 25.4 us)
Sparse Core Ops, SparseCore 0:
  11.5 11.7 all-gather.11
  26.0 61.8 all-gather.13
  90.6 59.3 all-gather.15
  152.5 74.5 all-gather.17
  229.7 91.0 all-gather.19
  326.0 7.7 reduce-scatter.6
  740.2 9.0 all-gather.31
  843.7 10.7 reduce-scatter.12
  857.3 45.6 reduce-scatter.8
  908.6 362.4 reduce-scatter.14
  1275.0 603.1 reduce-scatter.16
Sparse Core Ops, SparseCore 1:
  328.8 96.9 all-gather.25
  427.8 20.6 all-gather.21
  450.8 98.7 all-gather.23
  551.2 20.6 all-gather.29
  574.1 99.5 all-gather.27
  693.5 42.6 reduce-scatter.10
where the time goes:
time: 1910 us; the launch traced here: 1890 us
  waiting for transfers between devices  1540 us (81%)
  matrix products  122 us (6%)
  other arithmetic  78.8 us (4%)
  local copies, waits for them, and re-layouts  61.3 us (3%)
  blocking collectives  44.3 us (2%)
  starting transfers between devices  31.6 us (2%)
    reduce_scatter x1, waiting for transfers between devices, body(): lax.psum_scatter(jnp.concatenate([contract_rows(normed_two, grad_gate), c...  601 us
    reduce_scatter x1, waiting for transfers between devices, reduce_attn_grads(): lax.psum_scatter(product(jnp.int32(0), rows_out * lax.axis_size(('fsdp',...  289 us
    all_gather x1, waiting for transfers between devices, body(): lax.all_gather(w_down, 'fsdp', axis=1, tiled=True)  102 us
    all_gather x1, waiting for transfers between devices, body(): lax.all_gather(w_gate, 'fsdp', axis=0, tiled=True)  92.5 us
    all_gather x1, waiting for transfers between devices, body(): lax.all_gather(w_up, 'fsdp', axis=0, tiled=True)  87.2 us
    all_gather x1, waiting for transfers between devices, body(): lax.all_gather(value_projection_weight, ('fsdp', 'ctx'), axis=0, tiled=True)  64.6 us
    all_gather x1, waiting for transfers between devices, body(): lax.all_gather(w_query, ('fsdp', 'ctx'), axis=0, tiled=True)  64.3 us
    all_gather x1, waiting for transfers between devices, body(): lax.all_gather(w_out, ('fsdp', 'ctx'), axis=1, tiled=True)  61.2 us
  transfers between devices with their start and end apart: 25, of which 20 were waited for; matrix products, arithmetic and copies ran while one was open for 9% of the time, Pallas kernels for 0%

commit v1 on v0

v1 whole, which is shorter than its diff:
```python
import functools

import jax
import jax.numpy as jnp
from jax import lax
from jax.experimental import pallas as pl
from jax.experimental.pallas import tpu as pltpu
from jax.sharding import PartitionSpec as P

EPS = 1e-06
THETA = 1000000.0
AXES = ("fsdp", "ctx", "tp")
MESH = pl.DeviceIdType.MESH
BF16 = jnp.bfloat16
F32 = jnp.float32
TP_BIT, CTX_BIT = 1, 2
PAIR = 2
PAIR_BIT = PAIR * 4


def dot_rows(left, right):
    return lax.dot_general(left, right, (((0,), (0,)), ((), ())), preferred_element_type=F32)


def dot_cols(left, right):
    return lax.dot_general(left, right, (((1,), (1,)), ((), ())), preferred_element_type=F32)


def dot(left, right):
    return lax.dot_general(left, right, (((1,), (0,)), ((), ())), preferred_element_type=F32)


def places():
    f, c, t = lax.axis_index("fsdp"), lax.axis_index("ctx"), lax.axis_index("tp")
    pair = (f // PAIR) % 2
    other_f, other_c, other_t = f + PAIR - 2 * PAIR * pair, 1 - c, 1 - t
    mine = pair * 4 + c * 2
    blocks = [mine, pair * 4 + other_c * 2, (1 - pair) * 4 + c * 2, (1 - pair) * 4 + other_c * 2]
    chips = [None, {"ctx": other_c}, {"fsdp": other_f}, {"fsdp": other_f, "ctx": other_c}]
    return t, other_t, blocks, chips, {"tp": other_t}


def greet(chips, sibling):
    barrier = pltpu.get_barrier_semaphore()
    for device in [*chips[1:], sibling]:
        pl.semaphore_signal(barrier, inc=1, device_id=device, device_id_type=MESH)
    pl.semaphore_wait(barrier, 4)


def remote(src, dst, send, recv, device):
    return pltpu.make_async_remote_copy(
        src_ref=src, dst_ref=dst, send_sem=send, recv_sem=recv, device_id=device, device_id_type=MESH
    )


def spread(own, out, sems):
    send, recv, local = sems
    t, other_t, blocks, chips, sibling = places()
    here = pltpu.make_async_copy(own, out.at[blocks[0] + t], local)
    here.start()
    copies = [None] + [
        remote(own, out.at[blocks[0] + t], send.at[j], recv.at[j], chips[j]) for j in (1, 2, 3)
    ]
    for j in (3, 1, 2):
        copies[j].start()
    beside = remote(own, out.at[blocks[0] + t], send.at[0], recv.at[0], sibling)
    beside.start()
    forwards = []
    for j in (1, 2, 3):
        remote(own, out.at[blocks[j] + t], send.at[j], recv.at[j], chips[j]).wait_recv()
        hand = remote(
            out.at[blocks[j] + t], out.at[blocks[j] + t], send.at[j + 4], recv.at[j + 4], sibling
        )
        hand.start()
        forwards.append(hand)
    here.wait()
    beside.wait_send()
    remote(own, out.at[blocks[0] + other_t], send.at[0], recv.at[0], sibling).wait_recv()
    for j in (1, 2, 3):
        copies[j].wait_send()
        forwards[j - 1].wait_send()
        remote(
            own, out.at[blocks[j] + other_t], send.at[j + 4], recv.at[j + 4], sibling
        ).wait_recv()


def collect(partial, held, first, second, sending, sems):
    send, recv, local = sems
    t, other_t, blocks, chips, sibling = places()
    order = (3, 1, 2, 0)
    loads, hands = {}, {}
    for j in order:
        hands[j] = remote(
            partial.at[blocks[j] + other_t], first.at[j], send.at[j], recv.at[j], sibling
        )
        hands[j].start()
        loads[j] = pltpu.make_async_copy(partial.at[blocks[j] + t], held.at[j], local.at[j])
        loads[j].start()
    rows = held.shape[1]
    step = 16
    across = {}
    for j in order:
        loads[j].wait()
        hands[j].wait()
        if j == 0:
            continue

        @pl.loop(0, rows // step)
        def _(i):
            at = pl.ds(pl.multiple_of(i * step, step), step)
            sending[j - 1, at] = (held[j, at].astype(F32) + first[j, at].astype(F32)).astype(BF16)

        across[j] = remote(
            sending.at[j - 1], second.at[j - 1], send.at[j + 3], recv.at[j + 3], chips[j]
        )
        across[j].start()
    for j in (3, 1, 2):
        across[j].wait()


def collected(held, first, second, at):
    return (held[0, at].astype(F32) + first[0, at].astype(F32)) + (
        second[0, at].astype(F32) + second[1, at].astype(F32) + second[2, at].astype(F32)
    )


def row_loop(rows, body):
    step = 16

    @pl.loop(0, rows // step)
    def _(i):
        body(pl.ds(pl.multiple_of(i * step, step), step))


def unit_and_scale(x):
    scale = lax.rsqrt(jnp.mean(x * x, axis=-1, keepdims=True) + EPS)
    return x * scale, scale


def first_kernel(hidden, gain, out, own, send, recv, local):
    def norm(at):
        unit, _ = unit_and_scale(hidden[at].astype(F32))
        own[at] = (unit * gain[...]).astype(BF16)

    row_loop(hidden.shape[0], norm)
    _, _, _, chips, sibling = places()
    greet(chips, sibling)
    spread(own, out, (send, recv, local.at[0]))


def middle_kernel(
    partial, hidden, gain, mid, out, own, held, first, second, sending, s1, r1, l1, s2, r2, l2
):
    _, _, _, chips, sibling = places()
    greet(chips, sibling)
    collect(partial, held, first, second, sending, (s1, r1, l1))

    def norm(at):
        x = hidden[at].astype(F32) + collected(held, first, second, at)
        mid[at] = x
        unit, _ = unit_and_scale(x)
        own[at] = (unit * gain[...]).astype(BF16)

    row_loop(hidden.shape[0], norm)
    spread(own, out, (s2, r2, l2.at[0]))


def norm_back(grad, x, gain, gain_grad):
    unit, scale = unit_and_scale(x)
    gain_grad[...] += jnp.sum((grad * unit).reshape(-1, 8, grad.shape[-1]), axis=0)
    e = grad * gain
    return scale * (e - unit * jnp.mean(e * unit, axis=-1, keepdims=True))


def turn_kernel(
    partial, mid, cot, gain, grad_mid, gain_grad, out,
    own, held, first, second, sending, s1, r1, l1, s2, r2, l2,
):
    _, _, _, chips, sibling = places()
    greet(chips, sibling)
    collect(partial, held, first, second, sending, (s1, r1, l1))
    gain_grad[...] = jnp.zeros_like(gain_grad)

    def back(at):
        grad = collected(held, first, second, at)
        g = cot[at].astype(F32) + norm_back(grad, mid[at], gain[...], gain_grad)
        grad_mid[at] = g
        own[at] = g.astype(BF16)

    row_loop(mid.shape[0], back)
    spread(own, out, (s2, r2, l2.at[0]))


def last_kernel(
    partial, hidden, grad_mid, gain, grad_in, gain_grad, held, first, second, sending, s1, r1, l1
):
    _, _, _, chips, sibling = places()
    greet(chips, sibling)
    collect(partial, held, first, second, sending, (s1, r1, l1))
    gain_grad[...] = jnp.zeros_like(gain_grad)

    def back(at):
        grad = collected(held, first, second, at)
        grad_in[at] = grad_mid[at] + norm_back(
            grad, hidden[at].astype(F32), gain[...], gain_grad
        )

    row_loop(hidden.shape[0], back)


VMEM_SPEC = pl.BlockSpec(memory_space=pltpu.VMEM)
ANY_SPEC = pl.BlockSpec(memory_space=pl.ANY)


def comm_call(kernel, collective_id, operands, in_specs, outs, out_specs, scratch, nbytes):
    return pl.pallas_call(
        kernel,
        out_shape=outs,
        in_specs=in_specs,
        out_specs=out_specs,
        scratch_shapes=scratch,
        compiler_params=pltpu.CompilerParams(
            collective_id=collective_id, has_side_effects=True, vmem_limit_bytes=32 << 20
        ),
        cost_estimate=pl.CostEstimate(flops=nbytes * 20, bytes_accessed=nbytes, transcendentals=0),
        name=kernel.__name__,
    )(*operands)


def spread_scratch():
    return [
        pltpu.SemaphoreType.DMA((8,)),
        pltpu.SemaphoreType.DMA((8,)),
        pltpu.SemaphoreType.DMA((1,)),
    ]


def collect_buffers(rows, width):
    return [
        pltpu.VMEM((4, rows, width), BF16),
        pltpu.VMEM((4, rows, width), BF16),
        pltpu.VMEM((3, rows, width), BF16),
        pltpu.VMEM((3, rows, width), BF16),
    ]


def collect_sems():
    return [
        pltpu.SemaphoreType.DMA((8,)),
        pltpu.SemaphoreType.DMA((8,)),
        pltpu.SemaphoreType.DMA((4,)),
    ]


def head_unit(x):
    scale = lax.rsqrt(jnp.mean(x * x, axis=-1, keepdims=True) + EPS)
    return x * scale, scale


def rot(a, cos, sin):
    return a * cos + pltpu.roll(a, a.shape[-1] // 2, 1) * sin


def rot_back(b, cos, sin):
    return b * cos - pltpu.roll(b, b.shape[-1] // 2, 1) * sin


def allowed_keys(seg_col, seg_row):
    length = seg_col.shape[0]
    row = lax.broadcasted_iota(jnp.int32, (length, length), 0)
    col = lax.broadcasted_iota(jnp.int32, (length, length), 1)
    return (seg_col == seg_row) & (row >= col)


def soft_of(scores):
    peak = jnp.max(scores, axis=-1, keepdims=True)
    lse = peak + jnp.log(jnp.sum(jnp.exp(scores - peak), axis=-1, keepdims=True))
    return jnp.exp(scores - lse)


def attend_kernel(groups, qkv, seg_col, seg_row, cos_ref, sin_ref, gain_q, gain_k, out):
    d = gain_q.shape[-1]
    cos, sin = cos_ref[0], sin_ref[0]
    allowed = allowed_keys(seg_col[0], seg_row[0])
    unit_k, _ = head_unit(qkv[0, :, groups * d : (groups + 1) * d].astype(F32))
    key = rot(unit_k * gain_k[...], cos, sin).astype(BF16)
    value = qkv[0, :, (groups + 1) * d : (groups + 2) * d]
    for g in range(groups):
        unit_q, _ = head_unit(qkv[0, :, g * d : (g + 1) * d].astype(F32))
        query = rot(unit_q * gain_q[...], cos, sin).astype(BF16)
        scores = jnp.where(allowed, dot_cols(query, key) * d**-0.5, -jnp.inf)
        soft = soft_of(scores).astype(BF16)
        out[0, :, g * d : (g + 1) * d] = dot(soft, value).astype(BF16)


def attend_back_kernel(
    groups, qkv, att, datt, seg_col, seg_row, cos_ref, sin_ref, gain_q, gain_k, grad, gains
):
    d = gain_q.shape[-1]
    cos, sin = cos_ref[0], sin_ref[0]
    scale = d**-0.5
    allowed = allowed_keys(seg_col[0], seg_row[0])
    unit_k, scale_k = head_unit(qkv[0, :, groups * d : (groups + 1) * d].astype(F32))
    key = rot(unit_k * gain_k[...], cos, sin).astype(BF16)
    value = qkv[0, :, (groups + 1) * d : (groups + 2) * d]
    key_grad = jnp.zeros(unit_k.shape, F32)
    value_grad = jnp.zeros(unit_k.shape, F32)
    gq = jnp.zeros((8, d), F32)

    def through_norm(b, unit, scale_, gain):
        e = b * gain
        return scale_ * (e - unit * jnp.mean(e * unit, axis=-1, keepdims=True))

    for g in range(groups):
        at = slice(g * d, (g + 1) * d)
        unit_q, scale_q = head_unit(qkv[0, :, at].astype(F32))
        query = rot(unit_q * gain_q[...], cos, sin).astype(BF16)
        scores = jnp.where(allowed, dot_cols(query, key) * scale, -jnp.inf)
        soft = soft_of(scores)
        up = datt[0, :, at]
        delta = jnp.sum(up.astype(F32) * att[0, :, at].astype(F32), axis=-1, keepdims=True)
        ds = (soft * (dot_cols(up, value) - delta) * scale).astype(BF16)
        value_grad += dot_rows(soft.astype(BF16), up)
        key_grad += dot_rows(ds, query)
        b = rot_back(dot(ds, key), cos, sin)
        gq += jnp.sum((b * unit_q).reshape(-1, 8, d), axis=0)
        grad[0, :, at] = through_norm(b, unit_q, scale_q, gain_q[...]).astype(BF16)
    b = rot_back(key_grad, cos, sin)
    gk = jnp.sum((b * unit_k).reshape(-1, 8, d), axis=0)
    grad[0, :, groups * d : (groups + 1) * d] = through_norm(b, unit_k, scale_k, gain_k[...]).astype(BF16)
    grad[0, :, (groups + 1) * d : (groups + 2) * d] = value_grad.astype(BF16)
    gains[0, 0] = gq
    gains[0, 1] = gk


def per_sequence(*shape):
    return pl.BlockSpec((1, *shape), lambda s: (s,) + (0,) * len(shape))


def attention_specs(length, d):
    return [
        per_sequence(length, 1),
        per_sequence(1, length),
        per_sequence(length, d),
        per_sequence(length, d),
        pl.BlockSpec((1, d), lambda s: (0, 0)),
        pl.BlockSpec((1, d), lambda s: (0, 0)),
    ]


def attend(groups, qkv, common):
    n, length, width = qkv.shape
    d = width // (groups + 2)
    return pl.pallas_call(
        functools.partial(attend_kernel, groups),
        grid=(n,),
        out_shape=jax.ShapeDtypeStruct((n, length, groups * d), BF16),
        in_specs=[per_sequence(length, width), *attention_specs(length, d)],
        out_specs=per_sequence(length, groups * d),
        compiler_params=pltpu.CompilerParams(vmem_limit_bytes=40 << 20),
        cost_estimate=pl.CostEstimate(
            flops=n * groups * length * length * (4 * d + 20),
            bytes_accessed=n * length * width * 4,
            transcendentals=n * groups * length * length * 2,
        ),
        name="attend",
    )(qkv, *common)


def attend_back(groups, qkv, att, datt, common):
    n, length, width = qkv.shape
    d = width // (groups + 2)
    return pl.pallas_call(
        functools.partial(attend_back_kernel, groups),
        grid=(n,),
        out_shape=(
            jax.ShapeDtypeStruct((n, length, width), BF16),
            jax.ShapeDtypeStruct((n, 2, 8, d), F32),
        ),
        in_specs=[
            per_sequence(length, width),
            per_sequence(length, groups * d),
            per_sequence(length, groups * d),
            *attention_specs(length, d),
        ],
        out_specs=(per_sequence(length, width), per_sequence(2, 8, d)),
        compiler_params=pltpu.CompilerParams(vmem_limit_bytes=40 << 20),
        cost_estimate=pl.CostEstimate(
            flops=n * groups * length * length * (10 * d + 30),
            bytes_accessed=n * length * width * 8,
            transcendentals=n * groups * length * length * 2,
        ),
        name="attend_back",
    )(qkv, att, datt, *common)


def build(mesh):
    n = mesh.size
    n_f = mesh.shape["fsdp"]
    spread_bits = [b for b in (1 << i for i in range(n_f.bit_length() - 2, -1, -1)) if b != PAIR]
    all_bits = sorted([*spread_bits, PAIR], reverse=True)

    def swap(v, bit):
        return lax.ppermute(v, AXES, [(i, i ^ bit) for i in range(n)])

    def bit_of(f, b):
        return (f // b) % 2

    def in_order(bit, own, other, axis):
        low = jnp.where(bit == 0, own, other)
        high = jnp.where(bit == 0, other, own)
        return jnp.stack([low, high], axis=axis)

    def pick(v, index, axis):
        return lax.dynamic_index_in_dim(v, index, axis, keepdims=False)

    def gather(v, f):
        have = [PAIR]
        for b in spread_bits:
            have = sorted([*have, b], reverse=True)
            v = in_order(bit_of(f, b), v, swap(v, b * 4), have.index(b))
        return v.reshape(n_f, *v.shape[len(have) :])

    def halves(f, b, width):
        return [n_f // (2 * b), 2, b * width]

    def scatter(keep, got, f, width):
        v = keep + got.astype(F32)
        have = [b for b in all_bits if b != 1]
        v = v.reshape(*([2] * len(have)), width, v.shape[-1])
        for b in [b for b in reversed(spread_bits) if b != 1]:
            axis = have.index(b)
            bit = bit_of(f, b)
            v = pick(v, bit, axis) + swap(pick(v, 1 - bit, axis).astype(BF16), b * 4).astype(F32)
            have.remove(b)
        return v

    def body(
        hidden_in,
        cotangent,
        segments,
        w_query,
        key_projection_weight,
        value_projection_weight,
        w_out,
        w_gate,
        w_up,
        w_down,
        gain_attn,
        gain_mlp,
        gain_query,
        key_norm_gain,
    ):
        rows, width = hidden_in.shape
        d = gain_query.shape[0]
        length = segments.shape[0]
        f, c = lax.axis_index("fsdp"), lax.axis_index("ctx")
        pair = bit_of(f, PAIR)
        at_rows = w_query.shape[0]
        ff_rows = w_gate.shape[0]
        ff_cols = w_gate.shape[1] // 2
        q_cols, kv_cols = w_query.shape[1] // 4, key_projection_weight.shape[1] // 4
        groups = q_cols // kv_cols

        def chunks4(w):
            return jnp.moveaxis(w.reshape(at_rows, 4, w.shape[1] // 4), 1, 0)

        def attn_weights(chunks):
            cols = chunks.shape[-1]
            chunks = chunks.reshape(2, 2, at_rows, cols)
            mine = pick(pick(chunks, c, 0), pair, 0)
            by_ctx = swap(pick(pick(chunks, 1 - c, 0), pair, 0), CTX_BIT)
            by_pair = swap(pick(pick(chunks, c, 0), 1 - pair, 0), PAIR_BIT)
            by_both = swap(pick(pick(chunks, 1 - c, 0), 1 - pair, 0), CTX_BIT | PAIR_BIT)
            near = in_order(c, mine, by_ctx, 0)
            far = in_order(c, by_pair, by_both, 0)
            both = in_order(pair, near, far, 0)
            return gather(both.reshape(2, 2 * at_rows, cols), f).reshape(-1, cols)

        full_qkv = attn_weights(
            jnp.concatenate(
                [chunks4(w_query), chunks4(key_projection_weight), chunks4(value_projection_weight)], axis=2
            )
        )
        full_out = attn_weights(chunks4(w_out.T))

        def ff_weights(w):
            w = w.reshape(ff_rows, 2, ff_cols)
            other = swap(pick(w, 1 - pair, 1), PAIR_BIT)
            return gather(in_order(pair, pick(w, pair, 1), other, 0), f).reshape(-1, ff_cols)

        full_gate = ff_weights(w_gate)
        full_up = ff_weights(w_up)
        full_down = ff_weights(w_down.T)

        seg = in_order(pair, segments, swap(segments, PAIR_BIT), 0)
        before = jnp.sum((seg[:, None, :] < seg[:, :, None]).astype(jnp.int32), axis=-1)
        positions = jnp.arange(length, dtype=jnp.int32)[None] - before
        freqs = THETA ** (-2.0 * jnp.arange(d // 2, dtype=F32) / d)
        angles = positions.astype(F32)[..., None] * freqs
        cos, sin = jnp.cos(angles), jnp.sin(angles)
        common = (
            seg[:, :, None],
            seg[:, None, :],
            jnp.concatenate([cos, cos], axis=-1),
            jnp.concatenate([-sin, sin], axis=-1),
            gain_query[None],
            key_norm_gain[None],
        )

        all_rows = jax.ShapeDtypeStruct((8, rows, width), BF16)
        own_rows = jax.ShapeDtypeStruct((rows, width), F32)
        gain_rows = jax.ShapeDtypeStruct((8, width), F32)
        block = pltpu.VMEM((rows, width), BF16)
        nbytes = rows * width * 16

        normed_one = comm_call(
            first_kernel, 0, (hidden_in, gain_attn[None]), [VMEM_SPEC] * 2,
            all_rows, ANY_SPEC, [block, *spread_scratch()], nbytes,
        ).reshape(8 * rows, width)
        qkv = dot(normed_one, full_qkv).astype(BF16)
        qkv3 = qkv.reshape(2, length, qkv.shape[1])
        attended3 = attend(groups, qkv3, common)
        attended = attended3.reshape(8 * rows, q_cols)
        out_part = dot_cols(attended, full_out).astype(BF16).reshape(8, rows, width)
        residual_mid, normed_two = comm_call(
            middle_kernel, 1, (out_part, hidden_in, gain_mlp[None]),
            [ANY_SPEC, VMEM_SPEC, VMEM_SPEC], (own_rows, all_rows), (VMEM_SPEC, ANY_SPEC),
            [block, *collect_buffers(rows, width), *collect_sems(), *spread_scratch()], 2 * nbytes,
        )
        normed_two = normed_two.reshape(8 * rows, width)

        teams = sorted(
            sorted(i ^ b ^ p for b in range(4) for p in (0, PAIR_BIT))
            for i in range(0, n, 4)
            if not i & PAIR_BIT
        )
        grad_rows = lax.all_gather(cotangent, AXES, axis_index_groups=teams, tiled=True)

        gate_pre = dot(normed_two, full_gate)
        up_pre = dot(normed_two, full_up)
        gate_sig = jax.nn.sigmoid(gate_pre)
        gate_act = gate_pre * gate_sig
        mixed = (gate_act * up_pre).astype(BF16)
        grad_mixed = dot(grad_rows, full_down)
        grad_gate = (grad_mixed * up_pre * gate_sig * (1.0 + gate_pre * (1.0 - gate_sig))).astype(BF16)
        grad_up = (grad_mixed * gate_act).astype(BF16)
        norm_two_part = (dot_cols(grad_gate, full_gate) + dot_cols(grad_up, full_up)).astype(BF16)
        grad_mid, gain_mlp_part, grad_mid_rows = comm_call(
            turn_kernel, 2, (norm_two_part.reshape(8, rows, width), residual_mid, cotangent, gain_mlp[None]),
            [ANY_SPEC, VMEM_SPEC, VMEM_SPEC, VMEM_SPEC], (own_rows, gain_rows, all_rows),
            (VMEM_SPEC, VMEM_SPEC, ANY_SPEC),
            [block, *collect_buffers(rows, width), *collect_sems(), *spread_scratch()], 2 * nbytes,
        )
        grad_mid_rows = grad_mid_rows.reshape(8 * rows, width)

        down_part = dot_cols(mixed, full_down).astype(BF16)
        hidden_out = residual_mid + lax.psum_scatter(
            down_part, AXES, scatter_dimension=0, axis_index_groups=teams, tiled=True
        ).astype(F32)

        low = bit_of(f, 1)

        def weight_grad(acts, grads):
            split = acts.reshape(acts.shape[0], n_f // 2, 2, width // n_f)
            mine = pick(split, low, 2).reshape(acts.shape[0], -1)
            theirs = pick(split, 1 - low, 2).reshape(acts.shape[0], -1)
            got = swap(dot_rows(theirs, grads).astype(BF16), 4)
            return scatter(dot_rows(mine, grads), got, f, width // n_f)

        def ff_grad(acts, grads):
            v = weight_grad(acts, grads)
            other = swap(pick(v, 1 - pair, 0).astype(BF16), PAIR_BIT).astype(F32)
            return in_order(pair, pick(v, pair, 0), other, 1).reshape(ff_rows, 2 * ff_cols)

        grad_w_gate = ff_grad(normed_two, grad_gate)
        grad_w_up = ff_grad(normed_two, grad_up)
        grad_w_down = ff_grad(grad_rows, mixed).T

        def attn_grad(acts, grads):
            v = weight_grad(acts, grads)
            v = v.reshape(2, 2, at_rows, v.shape[-1])
            mine = pick(pick(v, pair, 0), c, 0)
            by_ctx = swap(pick(pick(v, pair, 0), 1 - c, 0).astype(BF16), CTX_BIT).astype(F32)
            by_pair = swap(pick(pick(v, 1 - pair, 0), c, 0).astype(BF16), PAIR_BIT).astype(F32)
            by_both = swap(pick(pick(v, 1 - pair, 0), 1 - c, 0).astype(BF16), CTX_BIT | PAIR_BIT).astype(F32)
            near = in_order(pair, mine, by_pair, 1)
            far = in_order(pair, by_ctx, by_both, 1)
            return in_order(c, near, far, 1)

        grad_w_out = attn_grad(grad_mid_rows, attended).reshape(at_rows, 4 * q_cols).T

        datt = dot(grad_mid_rows, full_out).astype(BF16).reshape(attended3.shape)
        grad_qkv, head_gains = attend_back(groups, qkv3, attended3, datt, common)
        grad_qkv = grad_qkv.reshape(8 * rows, -1)
        norm_one_part = dot_cols(grad_qkv, full_qkv).astype(BF16)
        grad_input, gain_attn_part = comm_call(
            last_kernel, 3, (norm_one_part.reshape(8, rows, width), hidden_in, grad_mid, gain_attn[None]),
            [ANY_SPEC, VMEM_SPEC, VMEM_SPEC, VMEM_SPEC], (own_rows, gain_rows), (VMEM_SPEC, VMEM_SPEC),
            [*collect_buffers(rows, width), *collect_sems()], nbytes,
        )
        grad_qkv_w = attn_grad(normed_one, grad_qkv)
        grad_w_query = grad_qkv_w[..., :q_cols].reshape(at_rows, -1)
        grad_w_key = grad_qkv_w[..., q_cols : q_cols + kv_cols].reshape(at_rows, -1)
        grad_w_value = grad_qkv_w[..., q_cols + kv_cols :].reshape(at_rows, -1)

        head_gains = jnp.sum(head_gains, axis=(0, 2))
        gains = jnp.concatenate(
            [jnp.sum(gain_attn_part, axis=0), jnp.sum(gain_mlp_part, axis=0), head_gains[0], head_gains[1]]
        ).reshape(-1, d)
        for i in range(n.bit_length() - 1):
            gains = gains + swap(gains, 1 << i)
        gains = gains.reshape(-1)
        return (
            hidden_out,
            grad_input,
            grad_w_query,
            grad_w_key,
            grad_w_value,
            grad_w_out,
            grad_w_gate,
            grad_w_up,
            grad_w_down,
            gains[:width],
            gains[width : 2 * width],
            gains[2 * width : 2 * width + d],
            gains[2 * width + d :],
        )

    return body


def solution(mesh):
    everyone = P(("fsdp", "ctx", "tp"), None)
    attn = P(("fsdp", "ctx"), "tp")
    attn_out = P("tp", ("fsdp", "ctx"))
    ff_in = P("fsdp", ("ctx", "tp"))
    ff_out = P(("ctx", "tp"), "fsdp")
    same = P()
    return jax.shard_map(
        build(mesh),
        mesh=mesh,
        in_specs=(
            everyone, everyone, P("fsdp"), attn, attn, attn, attn_out, ff_in, ff_in, ff_out,
            same, same, same, same,
        ),
        out_specs=(
            everyone, everyone, attn, attn, attn, attn_out, ff_in, ff_in, ff_out,
            same, same, same, same,
        ),
        check_vma=False,
    )
```

time: 1910 us -> 847 us (0.44)
  waiting for transfers between devices: 1540 us -> 243 us
  Pallas kernels: 0 us -> 222 us
  local copies, waits for them, and re-layouts: 61.3 us -> 187 us
  matrix products: 122 us -> 77.2 us
  blocking collectives: 44.3 us -> 0 us
  other arithmetic: 78.8 us -> 34.7 us
  starting transfers between devices: 31.6 us -> 55 us
    reduce_scatter x6 -> x1, waiting for transfers between devices: 940 us -> 0.01 us  [body(): lax.psum_scatter(down_part, AXES, scatter_dimension=0, axis_index_groups=...]
    all_gather x11 -> x1, waiting for transfers between devices: 579 us -> 0.01 us  [body(): lax.all_gather(cotangent, AXES, axis_index_groups=teams, tiled=True)]
    ppermute x0 -> x44, waiting for transfers between devices: none -> 243 us  [swap(): return lax.ppermute(v, AXES, [(i, i ^ bit) for i in range(n)])]
    pallas_call x0 -> x6, Pallas kernels: none -> 222 us  [the longest x4 203 us: comm_call(): pl.pallas_call(kernel, out_shape=outs, in_specs=in_specs, out_specs=out_s...]
    unnamed x112 -> x151, local copies, waits for them, and re-layouts: 14.4 us -> 96.5 us
    ppermute x0 -> x44, starting transfers between devices: none -> 55 us  [swap(): return lax.ppermute(v, AXES, [(i, i ^ bit) for i in range(n)])]
    dot_general x27 -> x20, matrix products: 122 us -> 77.2 us  [the longest x10 28.9 us: dot_rows(): lax.dot_general(left, right, (((0,), (0,)), ((), ())), preferred_element_...]
    psum x1 -> x0, blocking collectives: 44.3 us -> none  [body(): lax.psum((local_gain_attn, local_gain_mlp, local_gain_query, local_gain_k...]
  transfers between devices with their start and end apart: 25 -> 46, of which waited for: 20 -> 17; matrix products, arithmetic and copies ran while one was open for 9% -> 31% of each run, Pallas kernels for 0% -> 27%
where the time goes in v1:
time: 847 us; the launch traced here: 835 us
  waiting for transfers between devices  243 us (29%)
  Pallas kernels  222 us (26%)
  local copies, waits for them, and re-layouts  187 us (22%)
  matrix products  77.2 us (9%)
  starting transfers between devices  55 us (6%)
  other arithmetic  34.7 us (4%)
  between operations  16 us (2%)
    ppermute x44, waiting for transfers between devices, swap(): return lax.ppermute(v, AXES, [(i, i ^ bit) for i in range(n)])  243 us
    pallas_call x4, Pallas kernels, comm_call(): pl.pallas_call(kernel, out_shape=outs, in_specs=in_specs, out_specs=out_s...  203 us
    unnamed x151, local copies, waits for them, and re-layouts  96.5 us
    ppermute x44, starting transfers between devices, swap(): return lax.ppermute(v, AXES, [(i, i ^ bit) for i in range(n)])  55 us
    dynamic_slice x14, local copies, waits for them, and re-layouts, pick(): return lax.dynamic_index_in_dim(v, index, axis, keepdims=False)  42.4 us
    dot_general x10, matrix products, dot_rows(): lax.dot_general(left, right, (((0,), (0,)), ((), ())), preferred_element_...  28.9 us
    dot_general x5, matrix products, dot(): lax.dot_general(left, right, (((1,), (0,)), ((), ())), preferred_element_...  28 us
    another operation x3, local copies, waits for them, and re-layouts, weight_grad(): split = acts.reshape(acts.shape[0], n_f // 2, 2, width // n_f)  23.5 us
  transfers between devices with their start and end apart: 46, of which 17 were waited for; matrix products, arithmetic and copies ran while one was open for 31% of the time, Pallas kernels for 27%

profile of v1, /device:TPU:0, one launch (start us, length us, event | category | flops | bytes accessed | tf_op | source)
XLA Modules:
  0.0 835.3 jit_solution(15159375781620489683)
XLA Ops:
  7.3 3.1 collective-permute-start.5
  25.0 37.7 %first_kernel.1 = bf16[8,128,2048]{2,1,0:T(8,128)(2,1)S(1)} custom-call(bf16[128,2048]{1,0:T(8,128)(2,1)S(1)} %copy-done.4, f32[1,2048]{1,0:T(1,128)S(1)} %bitcast.367), custom_call_target="tpu_custom_call" | custom-call | flops 83886080 | bytes 4194304 | tf_op jit(solution)/shard_map/first_kernel/pallas_call | solution.py:216
  62.8 2.1 copy-done.2
  64.8 7.8 reshape_reshape.30
  72.7 11.6 %constant_dynamic-slice_fusion.10 = (bf16[1024,4,1,256]{3,2,1,0:T(2,128)(2,1)}, bf16[1024,4,1,256]{3,2,1,0:T(2,128)(2,1)}) fusion(bf16[1024,4,2,256]{3,2,1,0:T(2,128)(2,1)} %reshape_reshape.30, s32[]{:T(128)S(6)} %select_n.609, s32[]{:T(128)S(6)} %select_n.608), kind=kLoop, calls=%fused_computation.196 | loop fusion | bytes 8388616 | tf_op jit(solution)/shard_map/jit(dynamic_index_in_dim)/dynamic_slice | solution.py:415
  91.8 10.6 %copy.151 = bf16[1024,4,1,256]{0,3,1,2:T(8,128)(2,1)} copy(bf16[1024,4,1,256]{3,2,1,0:T(2,128)(2,1)} %get-tuple-element.66) | data formatting | bytes 4194304
  102.4 10.6 %copy.150 = bf16[1024,4,1,256]{0,3,1,2:T(8,128)(2,1)} copy(bf16[1024,4,1,256]{3,2,1,0:T(2,128)(2,1)} %get-tuple-element.67) | data formatting | bytes 4194304
  117.6 4.0 collective-permute-start.1
  125.8 2.6 collective-permute-start.9
  130.9 25.8 %collective-permute-done.9 = bf16[2,256,256]{2,1,0:T(8,128)(2,1)S(1)} collective-permute-done((bf16[2,256,256]{2,1,0:T(8,128)(2,1)S(1)}, bf16[2,256,256]{2,1,0:T(8,128)(2,1)S(1)}, u32[]{:S(2)}, u32[]{:S(2)}) %collective-permute-start.9) | collective-permute-done | bytes 262176 | tf_op jit(solution)/shard_map/ppermute | solution.py:404
  160.1 7.6 collective-permute-done.17
  175.2 64.1 %collective-permute-done.15 = bf16[2,256,768]{2,1,0:T(8,128)(2,1)S(1)} collective-permute-done((bf16[2,256,768]{2,1,0:T(8,128)(2,1)S(1)}, bf16[2,256,768]{2,1,0:T(8,128)(2,1)S(1)}, u32[]{:S(2)}, u32[]{:S(2)}) %collective-permute-start.15) | collective-permute-done | bytes 786464 | tf_op jit(solution)/shard_map/ppermute | solution.py:404
  242.3 13.8 %collective-permute-done.18 = bf16[2,256,768]{2,1,0:T(8,128)(2,1)S(1)} collective-permute-done((bf16[2,256,768]{2,1,0:T(8,128)(2,1)S(1)}, bf16[2,256,768]{2,1,0:T(8,128)(2,1)S(1)}, u32[]{:S(2)}, u32[]{:S(2)}) %collective-permute-start.18) | collective-permute-done | bytes 786464 | tf_op jit(solution)/shard_map/ppermute | solution.py:404
  259.2 12.6 %collective-permute-done.12 = bf16[2,256,768]{2,1,0:T(8,128)(2,1)S(1)} collective-permute-done((bf16[2,256,768]{2,1,0:T(8,128)(2,1)S(1)}, bf16[2,256,768]{2,1,0:T(8,128)(2,1)S(1)}, u32[]{:S(2)}, u32[]{:S(2)}) %collective-permute-start.12) | collective-permute-done | bytes 786464 | tf_op jit(solution)/shard_map/ppermute | solution.py:404
  276.0 2.7 copy-done.3
  278.7 2.3 convolution_convert_fusion.7
  281.1 10.0 %attend.1.att = bf16[2,512,256]{2,1,0:T(8,128)(2,1)S(1)} custom-call(bf16[2,512,512]{2,1,0:T(8,128)(2,1)S(1)} %bitcast.376, s32[2,512,1]{2,1,0:T(8,128)S(1)} %copy.112.seg_col, s32[2,1,512]{2,1,0:T(1,128)S(1)} %broadcast_in_dim.27.seg_row, f32[2,512,128]{2,1,0:T(8,128)S(1)} %get-tuple-element.161.cos_ref, f32[2,512,128]{2,1,0:T(8,128)S(1)} %get-tuple-element.162.sin_ref, ...), custom_call_target="tpu_custom_call" | custom-call | flops 557842432 | bytes 2097152 | tf_op jit(solution)/shard_map/attend/pallas_call | solution.py:354
  292.4 57.1 %middle_kernel.1 = (f32[128,2048]{1,0:T(8,128)S(1)}, bf16[8,128,2048]{2,1,0:T(8,128)(2,1)S(1)}) custom-call(bf16[8,128,2048]{2,1,0:T(8,128)(2,1)S(1)} %bitcast.355, bf16[128,2048]{1,0:T(8,128)(2,1)S(1)} %copy-done.4, f32[1,2048]{1,0:T(1,128)S(1)} %bitcast.365), custom_call_target="tpu_custom_call" | custom-call | flops 167772160 | bytes 8388608 | tf_op jit(solution)/shard_map/middle_kernel/pallas_call | solution.py:216
  349.6 2.1 copy-done.5
  351.7 7.8 reshape_reshape.32
  359.5 11.6 %constant_dynamic-slice_fusion.2 = (bf16[1024,4,1,256]{3,2,1,0:T(2,128)(2,1)}, bf16[1024,4,1,256]{3,2,1,0:T(2,128)(2,1)}) fusion(bf16[1024,4,2,256]{3,2,1,0:T(2,128)(2,1)} %reshape_reshape.32, s32[]{:T(128)S(6)} %select_n.609, s32[]{:T(128)S(6)} %select_n.608), kind=kLoop, calls=%fused_computation.188 | loop fusion | bytes 8388616 | tf_op jit(solution)/shard_map/jit(dynamic_index_in_dim)/dynamic_slice | solution.py:415
  371.1 10.6 %copy.158 = bf16[1024,4,1,256]{0,3,1,2:T(8,128)(2,1)} copy(bf16[1024,4,1,256]{3,2,1,0:T(2,128)(2,1)} %get-tuple-element.62) | data formatting | bytes 4194304
  381.6 10.5 %copy.157 = bf16[1024,4,1,256]{0,3,1,2:T(8,128)(2,1)} copy(bf16[1024,4,1,256]{3,2,1,0:T(2,128)(2,1)} %get-tuple-element.63) | data formatting | bytes 4194304
  402.5 3.1 copy-done.6
  405.6 5.1 fusion.47
  410.7 5.1 fusion.46
  415.8 11.6 %fusion.3 = (bf16[1024,768]{1,0:T(8,128)(2,1)}, bf16[1024,768]{1,0:T(8,128)(2,1)}, bf16[1024,768]{1,0:T(8,128)(2,1)S(1)}) fusion(f32[1024,768]{1,0:T(8,128)} %fusion.46, f32[1024,768]{1,0:T(8,128)} %fusion.47, bf16[2048,768]{1,0:T(8,128)(2,1)} %bitcast.386, bf16[1024,2048]{0,1:T(8,128)(2,1)} %all-gather.2.cloned.1.call-done), kind=kOutput, calls=%fused_computation.12 | convolution fusion | flops 3233021952 | bytes 18350080 | tf_op jit(solution)/shard_map/dot_general | solution.py:30
  428.6 5.0 convolution_convert_fusion.2
  433.7 6.0 fusion.48
  439.7 2.9 convolution_convert_fusion.5
  442.6 3.0 convolution_convert_fusion.4
  447.7 3.7 add_convert_fusion
  451.3 77.9 %turn_kernel.1 = (f32[128,2048]{1,0:T(8,128)S(1)}, f32[8,2048]{1,0:T(8,128)S(1)}, bf16[8,128,2048]{2,1,0:T(8,128)(2,1)S(1)}) custom-call(bf16[8,128,2048]{2,1,0:T(8,128)(2,1)S(1)} %bitcast.359, f32[128,2048]{1,0:T(8,128)S(1)} %get-tuple-element.22.mid, bf16[128,2048]{1,0:T(8,128)(2,1)S(1)} %copy-done.8, f32[1,2048]{1,0:T(1,128)S(1)} %bitcast.366), custom_call_target="tpu_custom_call" | custom-call | flops 167772160 | bytes 8388608 | tf_op jit(solution)/shard_map/turn_kernel/pallas_call | solution.py:216
  532.2 7.8 reshape_reshape.31
  540.0 3.9 convolution_convert_fusion.9
  544.0 8.6 %attend_back.1 = (bf16[2,512,512]{2,1,0:T(8,128)(2,1)S(1)}, f32[2,2,8,128]{3,2,1,0:T(8,128)S(1)}) custom-call(bf16[2,512,512]{2,1,0:T(8,128)(2,1)S(1)} %bitcast.377, bf16[2,512,256]{2,1,0:T(8,128)(2,1)S(1)} %attend.1.att, bf16[2,512,256]{2,1,0:T(8,128)(2,1)S(1)} %bitcast.378, s32[2,512,1]{2,1,0:T(8,128)S(1)} %copy-done.16, ...), custom_call_target="tpu_custom_call" | custom-call | flops 1373634560 | bytes 4194304 | tf_op jit(solution)/shard_map/attend_back/pallas_call | solution.py:373
  553.7 4.4 convolution_convert_fusion
  558.0 30.4 %last_kernel.1 = (f32[128,2048]{1,0:T(8,128)S(1)}, f32[8,2048]{1,0:T(8,128)S(1)}) custom-call(bf16[8,128,2048]{2,1,0:T(8,128)(2,1)S(1)} %bitcast.361, bf16[128,2048]{1,0:T(8,128)(2,1)S(1)} %copy-done.4, f32[128,2048]{1,0:T(8,128)S(1)} %copy-done.12, f32[1,2048]{1,0:T(1,128)S(1)} %bitcast.368), custom_call_target="tpu_custom_call" | custom-call | flops 83886080 | bytes 4194304 | tf_op jit(solution)/shard_map/last_kernel/pallas_call | solution.py:216
  589.6 4.2 convolution_convert_fusion.6
  596.8 9.8 %constant_dynamic-slice_fusion.8 = (bf16[1024,4,1,256]{3,2,1,0:T(2,128)(2,1)}, bf16[1024,4,1,256]{3,2,1,0:T(2,128)(2,1)}) fusion(bf16[1024,4,2,256]{3,2,1,0:T(2,128)(2,1)S(1)} %copy-done.25, s32[]{:T(128)S(6)} %select_n.609, s32[]{:T(128)S(6)} %select_n.608), kind=kLoop, calls=%fused_computation.194 | loop fusion | bytes 8388616 | tf_op jit(solution)/shard_map/jit(dynamic_index_in_dim)/dynamic_slice | solution.py:415
  606.6 10.6 %copy.153 = bf16[1024,4,1,256]{0,3,1,2:T(8,128)(2,1)} copy(bf16[1024,4,1,256]{3,2,1,0:T(2,128)(2,1)} %get-tuple-element.64) | data formatting | bytes 4194304
  617.8 2.4 convolution_convert_fusion.8
  625.6 2.4 collective-permute-start.43
  628.1 3.0 convolution_convert_fusion.3
  631.0 10.8 %copy.152 = bf16[1024,4,1,256]{0,3,1,2:T(8,128)(2,1)} copy(bf16[1024,4,1,256]{3,2,1,0:T(2,128)(2,1)} %get-tuple-element.65) | data formatting | bytes 4194304
  641.9 2.3 convert_add_fusion.4
  645.9 11.3 %collective-permute-done.26 = bf16[2,256,256]{2,1,0:T(8,128)(2,1)S(1)} collective-permute-done((bf16[2,256,256]{2,1,0:T(8,128)(2,1)S(1)}, bf16[2,256,256]{2,1,0:T(8,128)(2,1)S(1)}, u32[]{:S(2)}, u32[]{:S(2)}) %collective-permute-start.26) | collective-permute-done | bytes 262176 | tf_op jit(solution)/shard_map/ppermute | solution.py:404
  657.9 2.1 collective-permute-start.29
  663.5 2.6 collective-permute-done.28
  667.1 2.6 convert_add_fusion.3
  669.9 3.3 convert_add_fusion.2
  674.3 2.9 collective-permute-start.31
  677.2 3.2 convert_add_fusion.1
  681.7 45.2 %collective-permute-done.21 = bf16[2,256,512]{2,1,0:T(8,128)(2,1)S(1)} collective-permute-done((bf16[2,256,512]{2,1,0:T(8,128)(2,1)S(1)}, bf16[2,256,512]{2,1,0:T(8,128)(2,1)S(1)}, u32[]{:S(2)}, u32[]{:S(2)}) %collective-permute-start.21) | collective-permute-done | bytes 524320 | tf_op jit(solution)/shard_map/ppermute | solution.py:404
  727.2 2.4 collective-permute-start.24
  733.6 29.8 %collective-permute-done.22 = bf16[128,512]{1,0:T(8,128)(2,1)S(1)} collective-permute-done((bf16[128,512]{1,0:T(8,128)(2,1)S(1)}, bf16[128,512]{1,0:T(8,128)(2,1)S(1)}, u32[]{:S(2)}, u32[]{:S(2)}) %collective-permute-start.22) | collective-permute-done | bytes 131104 | tf_op jit(solution)/shard_map/ppermute | solution.py:404
  764.0 2.4 collective-permute-done.24
  777.0 22.9 %collective-permute-done.37 = bf16[2,256,768]{2,1,0:T(8,128)(2,1)} collective-permute-done((bf16[2,256,768]{2,1,0:T(8,128)(2,1)}, bf16[2,256,768]{2,1,0:T(8,128)(2,1)}, u32[]{:S(2)}, u32[]{:S(2)}) %collective-permute-start.37) | collective-permute-done | bytes 786464 | tf_op jit(solution)/shard_map/ppermute | solution.py:404
  804.1 3.0 copy.142
  807.2 3.0 copy.145
  813.2 3.1 copy.143
  816.2 3.0 copy.146
  821.8 3.1 copy.144
  824.8 2.2 convert_add_fusion.5
  (328 shorter events, 118.4 us)
Async XLA Ops:
  7.2 12.8 %copy-start.8 = (bf16[128,2048]{1,0:T(8,128)(2,1)S(1)}, bf16[128,2048]{1,0:T(8,128)(2,1)}, u32[]{:S(2)}) copy-start(bf16[128,2048]{1,0:T(8,128)(2,1)} %cot.1) | copy-start | bytes 1572868
  7.2 408.6 %all-gather.2.cloned.1.call-start = ((), (), s32[]{:S(2)}) async-start(), calls=%async_computation.2 | async-start | bytes 4718592 | tf_op jit(solution)/shard_map/all_gather | solution.py:538
  7.3 105.7 %collective-permute-start.5 = (s32[512]{0:T(512)}, s32[512]{0:T(512)S(1)}, u32[]{:S(2)}, u32[]{:S(2)}) collective-permute-start(s32[512]{0:T(512)} %param.16), channel_id=1, source_target_pairs={{0,8},{1,9},{2,10},{3,11},{4,12},{5,13},{6,14},{7,15},{8,0},{9,1},... | collective-permute-start | bytes 6152 | tf_op jit(solution)/shard_map/ppermute | solution.py:404
  12.1 105.4 %collective-permute-start.6 = (bf16[128,256]{1,0:T(8,128)(2,1)}, bf16[128,256]{1,0:T(8,128)(2,1)}, u32[]{:S(2)}, u32[]{:S(2)}) collective-permute-start(bf16[128,256]{1,0:T(8,128)(2,1)} %get-tuple-element.133), channel_id=1, source_target_pairs={{0,2},{1,3},{2,0},{3,1},{4,6},{5,7},{6,4},{7,5},{8,10},{9,11},{10,... | collective-permute-start | bytes 196616 | tf_op jit(solution)/shard_map/ppermute | solution.py:404
  13.7 108.8 %collective-permute-start.8 = (bf16[128,256]{1,0:T(8,128)(2,1)}, bf16[128,256]{1,0:T(8,128)(2,1)}, u32[]{:S(2)}, u32[]{:S(2)}) collective-permute-start(bf16[128,256]{1,0:T(8,128)(2,1)} %get-tuple-element.134), channel_id=1, source_target_pairs={{0,10},{1,11},{2,8},{3,9},{4,14},{5,15},{6,12},{7,13},{8,2},{9,3},... | collective-permute-start | bytes 196616 | tf_op jit(solution)/shard_map/ppermute | solution.py:404
  13.7 109.0 %collective-permute-start.7 = (bf16[128,256]{1,0:T(8,128)(2,1)}, bf16[128,256]{1,0:T(8,128)(2,1)}, u32[]{:S(2)}, u32[]{:S(2)}) collective-permute-start(bf16[128,256]{1,0:T(8,128)(2,1)} %get-tuple-element.135), channel_id=1, source_target_pairs={{0,8},{1,9},{2,10},{3,11},{4,12},{5,13},{6,14},{7,15},{8,0},{9,1},... | collective-permute-start | bytes 196616 | tf_op jit(solution)/shard_map/ppermute | solution.py:404
  18.5 110.9 %collective-permute-start = (bf16[128,512]{1,0:T(8,128)(2,1)}, bf16[128,512]{1,0:T(8,128)(2,1)}, u32[]{:S(2)}, u32[]{:S(2)}) collective-permute-start(bf16[128,512]{1,0:T(8,128)(2,1)} %get-tuple-element.124), channel_id=1, source_target_pairs={{0,2},{1,3},{2,0},{3,1},{4,6},{5,7},{6,4},{7,5},{8,10},{9,11},{10,... | collective-permute-start | bytes 393224 | tf_op jit(solution)/shard_map/ppermute | solution.py:404
  21.0 803.8 %reduce-scatter.2.cloned.1.call-start = ((), (), s32[]{:S(2)}) async-start(), calls=%async_computation.1 | async-start | bytes 4718592 | tf_op jit(solution)/shard_map/reduce_scatter | solution.py:558
  102.4 12.3 %copy-start.59 = (s32[512]{0:T(512)S(1)}, s32[512]{0:T(512)}, u32[]{:S(2)}) copy-start(s32[512]{0:T(512)} %param.16) | copy-start | bytes 6148
  112.9 12.6 %collective-permute-start.2 = (bf16[128,512]{1,0:T(8,128)(2,1)}, bf16[128,512]{1,0:T(8,128)(2,1)}, u32[]{:S(2)}, u32[]{:S(2)}) collective-permute-start(bf16[128,512]{1,0:T(8,128)(2,1)} %get-tuple-element.125), channel_id=1, source_target_pairs={{0,10},{1,11},{2,8},{3,9},{4,14},{5,15},{6,12},{7,13},{8,2},{9,3},... | collective-permute-start | bytes 393224 | tf_op jit(solution)/shard_map/ppermute | solution.py:404
  117.3 163.8 %copy-start.13 = (f32[2,512,128]{2,1,0:T(8,128)}, f32[2,512,128]{2,1,0:T(8,128)S(1)}, u32[]{:S(2)}) copy-start(f32[2,512,128]{2,1,0:T(8,128)S(1)} %get-tuple-element.162.sin_ref) | copy-start | bytes 1572868
  117.6 163.5 %copy-start.15 = (s32[2,512,1]{2,1,0:T(8,128)}, s32[2,512,1]{2,1,0:T(8,128)S(1)}, u32[]{:S(2)}) copy-start(s32[2,512,1]{2,1,0:T(8,128)S(1)} %copy.112.seg_col) | copy-start | bytes 12292
  117.6 8.3 collective-permute-start.1
  122.5 48.6 %collective-permute-start.11 = (bf16[256,768]{1,0:T(8,128)(2,1)}, bf16[256,768]{1,0:T(8,128)(2,1)S(1)}, u32[]{:S(2)}, u32[]{:S(2)}) collective-permute-start(bf16[256,768]{1,0:T(8,128)(2,1)} %bitcast.434), channel_id=1, source_target_pairs={{0,8},{1,9},{2,10},{3,11},{4,12},{5,13},{6,14},{7,15},{8,0},{9,1},... | collective-permute-start | bytes 1179656 | tf_op jit(solution)/shard_map/ppermute | solution.py:404
  122.7 37.4 %collective-permute-start.14 = (bf16[256,768]{1,0:T(8,128)(2,1)}, bf16[256,768]{1,0:T(8,128)(2,1)S(1)}, u32[]{:S(2)}, u32[]{:S(2)}) collective-permute-start(bf16[256,768]{1,0:T(8,128)(2,1)} %bitcast.435), channel_id=1, source_target_pairs={{0,8},{1,9},{2,10},{3,11},{4,12},{5,13},{6,14},{7,15},{8,0},{9,1},... | collective-permute-start | bytes 1179656 | tf_op jit(solution)/shard_map/ppermute | solution.py:404
  125.6 42.1 %collective-permute-start.17 = (bf16[256,768]{1,0:T(8,128)(2,1)}, bf16[256,768]{1,0:T(8,128)(2,1)S(1)}, u32[]{:S(2)}, u32[]{:S(2)}) collective-permute-start(bf16[256,768]{1,0:T(8,128)(2,1)} %bitcast.436), channel_id=1, source_target_pairs={{0,8},{1,9},{2,10},{3,11},{4,12},{5,13},{6,14},{7,15},{8,0},{9,1},... | collective-permute-start | bytes 1179656 | tf_op jit(solution)/shard_map/ppermute | solution.py:404
  125.8 30.8 %collective-permute-start.9 = (bf16[2,256,256]{2,1,0:T(8,128)(2,1)S(1)}, bf16[2,256,256]{2,1,0:T(8,128)(2,1)S(1)}, u32[]{:S(2)}, u32[]{:S(2)}) collective-permute-start(bf16[2,256,256]{2,1,0:T(8,128)(2,1)S(1)} %pad_maximum_fusion.26), channel_id=1, source_target_pairs={{0,16},{1,17},{2,18},{3,19},{4,20},{5,21},{6,22},{7,23},{8,24},{9,... | collective-permute-start | bytes 786440 | tf_op jit(solution)/shard_map/ppermute | solution.py:404
  130.3 37.3 %copy-start.55 = (bf16[256,1,768]{2,0,1:T(8,128)(2,1)S(1)}, bf16[256,1,768]{2,0,1:T(8,128)(2,1)}, u32[]{:S(2)}) copy-start(bf16[256,1,768]{2,0,1:T(8,128)(2,1)} %copy.120) | copy-start | bytes 1179652
  130.3 37.3 %copy-start.56 = (bf16[256,1,768]{2,0,1:T(8,128)(2,1)S(1)}, bf16[256,1,768]{2,0,1:T(8,128)(2,1)}, u32[]{:S(2)}) copy-start(bf16[256,1,768]{2,0,1:T(8,128)(2,1)} %copy.148) | copy-start | bytes 1179652
  130.5 42.8 %collective-permute-start.3 = (bf16[2,256,512]{2,1,0:T(8,128)(2,1)S(1)}, bf16[2,256,512]{2,1,0:T(8,128)(2,1)S(1)}, u32[]{:S(2)}, u32[]{:S(2)}) collective-permute-start(bf16[2,256,512]{2,1,0:T(8,128)(2,1)S(1)} %pad_maximum_fusion.16), channel_id=1, source_target_pairs={{0,16},{1,17},{2,18},{3,19},{4,20},{5,21},{6,22},{7,23},{8,24},{9,... | collective-permute-start | bytes 1572872 | tf_op jit(solution)/shard_map/ppermute | solution.py:404
  156.7 18.2 %collective-permute-start.10 = (bf16[2,2,256,256]{3,2,1,0:T(8,128)(2,1)S(1)}, bf16[2,2,256,256]{3,2,1,0:T(8,128)(2,1)S(1)}, u32[]{:S(2)}, u32[]{:S(2)}) collective-permute-start(bf16[2,2,256,256]{3,2,1,0:T(8,128)(2,1)S(1)} %pad_maximum_fusion.19), channel_id=1, source_target_pairs={{0,4},{1,5},{2,6},{3,7},{4,0},{5,1},{6,2},{7,3},{8,12},{9,13},{10,... | collective-permute-start | bytes 1572872 | tf_op jit(solution)/shard_map/ppermute | solution.py:404
  167.9 71.4 %collective-permute-start.15 = (bf16[2,256,768]{2,1,0:T(8,128)(2,1)S(1)}, bf16[2,256,768]{2,1,0:T(8,128)(2,1)S(1)}, u32[]{:S(2)}, u32[]{:S(2)}) collective-permute-start(bf16[2,256,768]{2,1,0:T(8,128)(2,1)S(1)} %pad_maximum_fusion.13), channel_id=1, source_target_pairs={{0,16},{1,17},{2,18},{3,19},{4,20},{5,21},{6,22},{7,23},{8,24},{9,... | collective-permute-start | bytes 2359304 | tf_op jit(solution)/shard_map/ppermute | solution.py:404
  170.0 86.2 %collective-permute-start.18 = (bf16[2,256,768]{2,1,0:T(8,128)(2,1)S(1)}, bf16[2,256,768]{2,1,0:T(8,128)(2,1)S(1)}, u32[]{:S(2)}, u32[]{:S(2)}) collective-permute-start(bf16[2,256,768]{2,1,0:T(8,128)(2,1)S(1)} %pad_maximum_fusion.14), channel_id=1, source_target_pairs={{0,16},{1,17},{2,18},{3,19},{4,20},{5,21},{6,22},{7,23},{8,24},{9,... | collective-permute-start | bytes 2359304 | tf_op jit(solution)/shard_map/ppermute | solution.py:404
  171.2 100.6 %collective-permute-start.12 = (bf16[2,256,768]{2,1,0:T(8,128)(2,1)S(1)}, bf16[2,256,768]{2,1,0:T(8,128)(2,1)S(1)}, u32[]{:S(2)}, u32[]{:S(2)}) collective-permute-start(bf16[2,256,768]{2,1,0:T(8,128)(2,1)S(1)} %pad_maximum_fusion.12), channel_id=1, source_target_pairs={{0,16},{1,17},{2,18},{3,19},{4,20},{5,21},{6,22},{7,23},{8,24},{9,... | collective-permute-start | bytes 2359304 | tf_op jit(solution)/shard_map/ppermute | solution.py:404
  173.4 102.2 %collective-permute-start.4 = (bf16[2,2,256,512]{3,2,1,0:T(8,128)(2,1)S(1)}, bf16[2,2,256,512]{3,2,1,0:T(8,128)(2,1)S(1)}, u32[]{:S(2)}, u32[]{:S(2)}) collective-permute-start(bf16[2,2,256,512]{3,2,1,0:T(8,128)(2,1)S(1)} %pad_maximum_fusion.10), channel_id=1, source_target_pairs={{0,4},{1,5},{2,6},{3,7},{4,0},{5,1},{6,2},{7,3},{8,12},{9,13},{10,... | collective-permute-start | bytes 3145736 | tf_op jit(solution)/shard_map/ppermute | solution.py:404
  175.2 115.9 %copy-start.38 = (bf16[2,2,2,256,256]{4,3,2,1,0:T(8,128)(2,1)}, bf16[2,2,2,256,256]{4,3,2,1,0:T(8,128)(2,1)S(1)}, u32[]{:S(2)}) copy-start(bf16[2,2,2,256,256]{4,3,2,1,0:T(8,128)(2,1)S(1)} %copy.114) | copy-start | bytes 3145732
  239.4 16.9 %copy-start.30 = (bf16[1,2,256,768]{3,2,1,0:T(8,128)(2,1)}, bf16[1,2,256,768]{3,2,1,0:T(8,128)(2,1)S(1)}, u32[]{:S(2)}) copy-start(bf16[1,2,256,768]{3,2,1,0:T(8,128)(2,1)S(1)} %get-tuple-element.86) | copy-start | bytes 2359300
  239.4 16.9 %copy-start.31 = (bf16[1,2,256,768]{3,2,1,0:T(8,128)(2,1)}, bf16[1,2,256,768]{3,2,1,0:T(8,128)(2,1)S(1)}, u32[]{:S(2)}) copy-start(bf16[1,2,256,768]{3,2,1,0:T(8,128)(2,1)S(1)} %get-tuple-element.87) | copy-start | bytes 2359300
  240.8 151.3 %collective-permute-start.16 = (bf16[2,2,256,768]{3,2,1,0:T(8,128)(2,1)}, bf16[2,2,256,768]{3,2,1,0:T(8,128)(2,1)}, u32[]{:S(2)}, u32[]{:S(2)}) collective-permute-start(bf16[2,2,256,768]{3,2,1,0:T(8,128)(2,1)} %pad_maximum_fusion.5), channel_id=1, source_target_pairs={{0,4},{1,5},{2,6},{3,7},{4,0},{5,1},{6,2},{7,3},{8,12},{9,13},{10,... | collective-permute-start | bytes 4718600 | tf_op jit(solution)/shard_map/ppermute | solution.py:404
  256.3 15.6 %copy-start.32 = (bf16[1,2,256,768]{3,2,1,0:T(8,128)(2,1)}, bf16[1,2,256,768]{3,2,1,0:T(8,128)(2,1)S(1)}, u32[]{:S(2)}) copy-start(bf16[1,2,256,768]{3,2,1,0:T(8,128)(2,1)S(1)} %get-tuple-element.82) | copy-start | bytes 2359300
  256.3 15.6 %copy-start.34 = (bf16[1,2,256,768]{3,2,1,0:T(8,128)(2,1)}, bf16[1,2,256,768]{3,2,1,0:T(8,128)(2,1)S(1)}, u32[]{:S(2)}) copy-start(bf16[1,2,256,768]{3,2,1,0:T(8,128)(2,1)S(1)} %get-tuple-element.83) | copy-start | bytes 2359300
  257.7 137.1 %collective-permute-start.19 = (bf16[2,2,256,768]{3,2,1,0:T(8,128)(2,1)}, bf16[2,2,256,768]{3,2,1,0:T(8,128)(2,1)}, u32[]{:S(2)}, u32[]{:S(2)}) collective-permute-start(bf16[2,2,256,768]{3,2,1,0:T(8,128)(2,1)} %pad_maximum_fusion.6), channel_id=1, source_target_pairs={{0,4},{1,5},{2,6},{3,7},{4,0},{5,1},{6,2},{7,3},{8,12},{9,13},{10,... | collective-permute-start | bytes 4718600 | tf_op jit(solution)/shard_map/ppermute | solution.py:404
  274.1 126.1 %collective-permute-start.13 = (bf16[2,2,256,768]{3,2,1,0:T(8,128)(2,1)}, bf16[2,2,256,768]{3,2,1,0:T(8,128)(2,1)}, u32[]{:S(2)}, u32[]{:S(2)}) collective-permute-start(bf16[2,2,256,768]{3,2,1,0:T(8,128)(2,1)} %pad_maximum_fusion.4), channel_id=1, source_target_pairs={{0,4},{1,5},{2,6},{3,7},{4,0},{5,1},{6,2},{7,3},{8,12},{9,13},{10,... | collective-permute-start | bytes 4718600 | tf_op jit(solution)/shard_map/ppermute | solution.py:404
  281.0 11.4 %copy-start.23 = (bf16[1024,512]{1,0:T(8,128)(2,1)}, bf16[1024,512]{1,0:T(8,128)(2,1)S(1)}, u32[]{:S(2)}) copy-start(bf16[1024,512]{1,0:T(8,128)(2,1)S(1)} %convolution_convert_fusion.7) | copy-start | bytes 3145732
  415.8 12.8 %copy-start.42 = (bf16[2,2,2,256,768]{4,3,2,1,0:T(8,128)(2,1)S(1)}, bf16[2,2,2,256,768]{4,3,2,1,0:T(8,128)(2,1)}, u32[]{:S(2)}) copy-start(bf16[2,2,2,256,768]{4,3,2,1,0:T(8,128)(2,1)} %copy.125) | copy-start | bytes 9437188
  445.6 224.2 %collective-permute-start.30 = (bf16[1024,768]{1,0:T(8,128)(2,1)}, bf16[1024,768]{1,0:T(8,128)(2,1)}, u32[]{:S(2)}, u32[]{:S(2)}) collective-permute-start(bf16[1024,768]{1,0:T(8,128)(2,1)} %convolution_convert_fusion.5), channel_id=1, source_target_pairs={{0,4},{1,5},{2,6},{3,7},{4,0},{5,1},{6,2},{7,3},{8,12},{9,13},{10,... | collective-permute-start | bytes 4718600 | tf_op jit(solution)/shard_map/ppermute | solution.py:404
  446.2 231.1 %collective-permute-start.33 = (bf16[1024,768]{1,0:T(8,128)(2,1)}, bf16[1024,768]{1,0:T(8,128)(2,1)}, u32[]{:S(2)}, u32[]{:S(2)}) collective-permute-start(bf16[1024,768]{1,0:T(8,128)(2,1)} %convolution_convert_fusion.4), channel_id=1, source_target_pairs={{0,4},{1,5},{2,6},{3,7},{4,0},{5,1},{6,2},{7,3},{8,12},{9,13},{10,... | collective-permute-start | bytes 4718600 | tf_op jit(solution)/shard_map/ppermute | solution.py:404
  589.4 6.3 collective-permute-start.39
  593.8 73.2 %collective-permute-start.20 = (bf16[1024,512]{1,0:T(8,128)(2,1)}, bf16[1024,512]{1,0:T(8,128)(2,1)}, u32[]{:S(2)}, u32[]{:S(2)}) collective-permute-start(bf16[1024,512]{1,0:T(8,128)(2,1)} %convolution_convert_fusion.6), channel_id=1, source_target_pairs={{0,4},{1,5},{2,6},{3,7},{4,0},{5,1},{6,2},{7,3},{8,12},{9,13},{10,... | collective-permute-start | bytes 3145736 | tf_op jit(solution)/shard_map/ppermute | solution.py:404
  595.7 21.4 %collective-permute-start.40 = (f32[34,128]{1,0:T(8,128)S(1)}, f32[34,128]{1,0:T(8,128)S(1)}, u32[]{:S(2)}, u32[]{:S(2)}) collective-permute-start(f32[34,128]{1,0:T(8,128)S(1)} %fusion.45), channel_id=1, source_target_pairs={{0,2},{1,3},{2,0},{3,1},{4,6},{5,7},{6,4},{7,5},{8,10},{9,11},{10,... | collective-permute-start | bytes 52232 | tf_op jit(solution)/shard_map/ppermute | solution.py:404
  617.2 4.6 collective-permute-start.41
  620.2 21.7 %collective-permute-start.25 = (bf16[1024,256]{1,0:T(8,128)(2,1)S(1)}, bf16[1024,256]{1,0:T(8,128)(2,1)S(1)}, u32[]{:S(2)}, u32[]{:S(2)}) collective-permute-start(bf16[1024,256]{1,0:T(8,128)(2,1)S(1)} %convolution_convert_fusion.8), channel_id=1, source_target_pairs={{0,4},{1,5},{2,6},{3,7},{4,0},{5,1},{6,2},{7,3},{8,12},{9,13},{10,... | collective-permute-start | bytes 1572872 | tf_op jit(solution)/shard_map/ppermute | solution.py:404
  621.8 3.8 collective-permute-start.42
  625.6 16.2 %collective-permute-start.43 = (f32[34,128]{1,0:T(8,128)S(1)}, f32[34,128]{1,0:T(8,128)S(1)}, u32[]{:S(2)}, u32[]{:S(2)}) collective-permute-start(f32[34,128]{1,0:T(8,128)S(1)} %add.276), channel_id=1, source_target_pairs={{0,16},{1,17},{2,18},{3,19},{4,20},{5,21},{6,22},{7,23},{8,24},{9,... | collective-permute-start | bytes 52232 | tf_op jit(solution)/shard_map/ppermute | solution.py:404
  644.3 13.0 %collective-permute-start.26 = (bf16[2,256,256]{2,1,0:T(8,128)(2,1)S(1)}, bf16[2,256,256]{2,1,0:T(8,128)(2,1)S(1)}, u32[]{:S(2)}, u32[]{:S(2)}) collective-permute-start(bf16[2,256,256]{2,1,0:T(8,128)(2,1)S(1)} %fusion.29), channel_id=1, source_target_pairs={{0,16},{1,17},{2,18},{3,19},{4,20},{5,21},{6,22},{7,23},{8,24},{9,... | collective-permute-start | bytes 786440 | tf_op jit(solution)/shard_map/ppermute | solution.py:404
  657.5 4.4 collective-permute-start.27
  657.9 5.3 collective-permute-start.29
  661.9 4.3 collective-permute-start.28
  663.2 66.4 %collective-permute-start.36 = (bf16[1024,768]{1,0:T(8,128)(2,1)}, bf16[1024,768]{1,0:T(8,128)(2,1)S(1)}, u32[]{:S(2)}, u32[]{:S(2)}) collective-permute-start(bf16[1024,768]{1,0:T(8,128)(2,1)} %convolution_convert_fusion.3), channel_id=1, source_target_pairs={{0,4},{1,5},{2,6},{3,7},{4,0},{5,1},{6,2},{7,3},{8,12},{9,13},{10,... | collective-permute-start | bytes 4718600 | tf_op jit(solution)/shard_map/ppermute | solution.py:404
  669.8 57.1 %collective-permute-start.21 = (bf16[2,256,512]{2,1,0:T(8,128)(2,1)S(1)}, bf16[2,256,512]{2,1,0:T(8,128)(2,1)S(1)}, u32[]{:S(2)}, u32[]{:S(2)}) collective-permute-start(bf16[2,256,512]{2,1,0:T(8,128)(2,1)S(1)} %fusion.14), channel_id=1, source_target_pairs={{0,16},{1,17},{2,18},{3,19},{4,20},{5,21},{6,22},{7,23},{8,24},{9,... | collective-permute-start | bytes 1572872 | tf_op jit(solution)/shard_map/ppermute | solution.py:404
  674.3 97.1 %collective-permute-start.31 = (bf16[2,256,768]{2,1,0:T(8,128)(2,1)}, bf16[2,256,768]{2,1,0:T(8,128)(2,1)}, u32[]{:S(2)}, u32[]{:S(2)}) collective-permute-start(bf16[2,256,768]{2,1,0:T(8,128)(2,1)} %fusion.11), channel_id=1, source_target_pairs={{0,16},{1,17},{2,18},{3,19},{4,20},{5,21},{6,22},{7,23},{8,24},{9,... | collective-permute-start | bytes 2359304 | tf_op jit(solution)/shard_map/ppermute | solution.py:404
  680.5 46.6 %copy-start.50 = (f32[1024,768]{1,0:T(8,128)}, f32[1024,768]{1,0:T(8,128)S(1)}, u32[]{:S(2)}) copy-start(f32[1024,768]{1,0:T(8,128)S(1)} %convert_add_fusion.1) | copy-start | bytes 9437188
  680.5 50.2 %copy-start.62 = (bf16[1024,768]{1,0:T(8,128)(2,1)S(1)}, bf16[1024,768]{1,0:T(8,128)(2,1)}, u32[]{:S(2)}) copy-start(bf16[1024,768]{1,0:T(8,128)(2,1)} %copy-done.60) | copy-start | bytes 4718596
  681.5 49.2 %copy-start.46 = (bf16[1024,4,1,256]{0,3,2,1:T(8,128)(2,1)S(1)}, bf16[1024,4,1,256]{0,3,2,1:T(8,128)(2,1)}, u32[]{:S(2)}) copy-start(bf16[1024,4,1,256]{0,3,2,1:T(8,128)(2,1)} %get-tuple-element.61) | copy-start | bytes 6291460
  681.5 92.1 %collective-permute-start.34 = (bf16[2,256,768]{2,1,0:T(8,128)(2,1)}, bf16[2,256,768]{2,1,0:T(8,128)(2,1)}, u32[]{:S(2)}, u32[]{:S(2)}) collective-permute-start(bf16[2,256,768]{2,1,0:T(8,128)(2,1)} %fusion.12), channel_id=1, source_target_pairs={{0,16},{1,17},{2,18},{3,19},{4,20},{5,21},{6,22},{7,23},{8,24},{9,... | collective-permute-start | bytes 2359304 | tf_op jit(solution)/shard_map/ppermute | solution.py:404
  727.1 36.3 %collective-permute-start.22 = (bf16[128,512]{1,0:T(8,128)(2,1)S(1)}, bf16[128,512]{1,0:T(8,128)(2,1)S(1)}, u32[]{:S(2)}, u32[]{:S(2)}) collective-permute-start(bf16[128,512]{1,0:T(8,128)(2,1)S(1)} %get-tuple-element.94), channel_id=1, source_target_pairs={{0,8},{1,9},{2,10},{3,11},{4,12},{5,13},{6,14},{7,15},{8,0},{9,1},... | collective-permute-start | bytes 393224 | tf_op jit(solution)/shard_map/ppermute | solution.py:404
  727.2 39.2 %collective-permute-start.24 = (bf16[128,512]{1,0:T(8,128)(2,1)S(1)}, bf16[128,512]{1,0:T(8,128)(2,1)S(1)}, u32[]{:S(2)}, u32[]{:S(2)}) collective-permute-start(bf16[128,512]{1,0:T(8,128)(2,1)S(1)} %get-tuple-element.95), channel_id=1, source_target_pairs={{0,10},{1,11},{2,8},{3,9},{4,14},{5,15},{6,12},{7,13},{8,2},{9,3},... | collective-permute-start | bytes 393224 | tf_op jit(solution)/shard_map/ppermute | solution.py:404
  729.6 36.9 %collective-permute-start.23 = (bf16[128,512]{1,0:T(8,128)(2,1)S(1)}, bf16[128,512]{1,0:T(8,128)(2,1)S(1)}, u32[]{:S(2)}, u32[]{:S(2)}) collective-permute-start(bf16[128,512]{1,0:T(8,128)(2,1)S(1)} %get-tuple-element.96), channel_id=1, source_target_pairs={{0,2},{1,3},{2,0},{3,1},{4,6},{5,7},{6,4},{7,5},{8,10},{9,11},{10,... | collective-permute-start | bytes 393224 | tf_op jit(solution)/shard_map/ppermute | solution.py:404
  732.5 34.0 %copy-start.52 = (f32[1024,768]{1,0:T(8,128)}, f32[1024,768]{1,0:T(8,128)S(1)}, u32[]{:S(2)}) copy-start(f32[1024,768]{1,0:T(8,128)S(1)} %convert_add_fusion) | copy-start | bytes 9437188
  763.4 36.5 %collective-permute-start.37 = (bf16[2,256,768]{2,1,0:T(8,128)(2,1)}, bf16[2,256,768]{2,1,0:T(8,128)(2,1)}, u32[]{:S(2)}, u32[]{:S(2)}) collective-permute-start(bf16[2,256,768]{2,1,0:T(8,128)(2,1)} %fusion.13), channel_id=1, source_target_pairs={{0,16},{1,17},{2,18},{3,19},{4,20},{5,21},{6,22},{7,23},{8,24},{9,... | collective-permute-start | bytes 2359304 | tf_op jit(solution)/shard_map/ppermute | solution.py:404
  773.5 26.4 %copy-start.53 = (f32[1024,768]{1,0:T(8,128)S(1)}, f32[1024,768]{1,0:T(8,128)}, u32[]{:S(2)}) copy-start(f32[1024,768]{1,0:T(8,128)} %copy-done.52) | copy-start | bytes 9437188
  773.5 29.3 %collective-permute-start.32 = (bf16[256,768]{1,0:T(8,128)(2,1)S(1)}, bf16[256,768]{1,0:T(8,128)(2,1)S(1)}, u32[]{:S(2)}, u32[]{:S(2)}) collective-permute-start(bf16[256,768]{1,0:T(8,128)(2,1)S(1)} %fusion.16), channel_id=1, source_target_pairs={{0,8},{1,9},{2,10},{3,11},{4,12},{5,13},{6,14},{7,15},{8,0},{9,1},... | collective-permute-start | bytes 1179656 | tf_op jit(solution)/shard_map/ppermute | solution.py:404
  775.7 35.0 %collective-permute-start.35 = (bf16[256,768]{1,0:T(8,128)(2,1)S(1)}, bf16[256,768]{1,0:T(8,128)(2,1)S(1)}, u32[]{:S(2)}, u32[]{:S(2)}) collective-permute-start(bf16[256,768]{1,0:T(8,128)(2,1)S(1)} %fusion.17), channel_id=1, source_target_pairs={{0,8},{1,9},{2,10},{3,11},{4,12},{5,13},{6,14},{7,15},{8,0},{9,1},... | collective-permute-start | bytes 1179656 | tf_op jit(solution)/shard_map/ppermute | solution.py:404
  802.7 16.6 %collective-permute-start.38 = (bf16[256,768]{1,0:T(8,128)(2,1)S(1)}, bf16[256,768]{1,0:T(8,128)(2,1)S(1)}, u32[]{:S(2)}, u32[]{:S(2)}) collective-permute-start(bf16[256,768]{1,0:T(8,128)(2,1)S(1)} %fusion.18), channel_id=1, source_target_pairs={{0,8},{1,9},{2,10},{3,11},{4,12},{5,13},{6,14},{7,15},{8,0},{9,1},... | collective-permute-start | bytes 1179656 | tf_op jit(solution)/shard_map/ppermute | solution.py:404
  (49 other events, 183.7 us)
Sparse Core Ops, SparseCore 0:
  21.2 50.6 all-gather.1
  433.8 83.5 reduce-scatter.1

commit v2 on v1

v2 whole, which is shorter than its diff:
```python
import functools

import jax
import jax.numpy as jnp
from jax import lax
from jax.experimental import pallas as pl
from jax.experimental.pallas import tpu as pltpu
from jax.sharding import PartitionSpec as P

EPS = 1e-06
THETA = 1000000.0
AXES = ("fsdp", "ctx", "tp")
MESH = pl.DeviceIdType.MESH
BF16 = jnp.bfloat16
F32 = jnp.float32
TP_BIT, CTX_BIT = 1, 2
PAIR = 2
PAIR_BIT = PAIR * 4


def dot_rows(left, right):
    return lax.dot_general(left, right, (((0,), (0,)), ((), ())), preferred_element_type=F32)


def dot_cols(left, right):
    return lax.dot_general(left, right, (((1,), (1,)), ((), ())), preferred_element_type=F32)


def dot(left, right):
    return lax.dot_general(left, right, (((1,), (0,)), ((), ())), preferred_element_type=F32)


def remote(src, dst, send, recv, device):
    return pltpu.make_async_remote_copy(
        src_ref=src, dst_ref=dst, send_sem=send, recv_sem=recv, device_id=device, device_id_type=MESH
    )


class Moves:
    def __init__(self, send, recv, local):
        self.send, self.recv, self.local = send, recv, local
        self.sent, self.loads = 0, 0
        self.open = []

    def swap(self, src, there, here, device):
        k = self.sent
        self.sent += 1
        copy = remote(src, there, self.send.at[k], self.recv.at[k], device)
        copy.start()
        self.open.append(copy.wait_send)
        return remote(src, here, self.send.at[k], self.recv.at[k], device).wait_recv

    def load(self, src, dst):
        k = self.loads
        self.loads += 1
        copy = pltpu.make_async_copy(src, dst, self.local.at[k])
        copy.start()
        return copy.wait

    def store(self, src, dst):
        self.open.append(self.load(src, dst))

    def close(self):
        for wait in self.open:
            wait()


class Place:
    def __init__(self, bits):
        self.bits = bits
        f, c, t = lax.axis_index("fsdp"), lax.axis_index("ctx"), lax.axis_index("tp")
        self.f, self.c, self.t = f, c, t
        self.pair = (f // PAIR) % 2
        far_f = self.block(PAIR)
        fs, cs = [f, f, far_f, far_f], [c, 1 - c, c, 1 - c]
        pairs = [self.pair, self.pair, 1 - self.pair, 1 - self.pair]
        self.at = [(fs[j], cs[j], pairs[j]) for j in range(4)]
        self.rows_of = [pairs[j] * 4 + cs[j] * 2 for j in range(4)]
        self.chunk_of = [cs[j] * 2 + pairs[j] for j in range(4)]
        self.chips = [None, {"ctx": 1 - c}, {"fsdp": far_f}, {"fsdp": far_f, "ctx": 1 - c}]
        self.sibling = {"tp": 1 - t}

    def block(self, mask):
        out = self.f
        for i in range(mask.bit_length()):
            b = 1 << i
            if mask & b:
                out = out + b - 2 * b * ((self.f // b) % 2)
        return out

    def along(self, bit):
        return {"fsdp": self.block(bit)}

    def greet(self):
        barrier = pltpu.get_barrier_semaphore()
        devices = [*self.chips[1:], self.sibling, *[self.along(b) for b in self.bits]]
        for device in devices:
            pl.semaphore_signal(barrier, inc=1, device_id=device, device_id_type=MESH)
        pl.semaphore_wait(barrier, len(devices))


class Spread:
    def __init__(self, moves, place, own, out):
        self.moves, self.place, self.out = moves, place, out
        self.rows = own.shape[0]
        mine = self.at(0, place.t)
        self.here = moves.load(own, mine)
        self.pair = moves.swap(own, mine, self.at(2, place.t), place.chips[2])
        self.ctx = moves.swap(own, mine, self.at(1, place.t), place.chips[1])
        self.beside = [moves.swap(own, mine, self.at(0, 1 - place.t), place.sibling)]

    def at(self, j, t):
        start = (self.place.rows_of[j] + t) * self.rows
        return self.out.at[pl.ds(pl.multiple_of(start, self.rows), self.rows)]

    def hand(self, j):
        block = self.at(j, self.place.t)
        self.beside.append(
            self.moves.swap(block, block, self.at(j, 1 - self.place.t), self.place.sibling)
        )

    def from_pair(self):
        self.pair()
        block = self.at(2, self.place.t)
        self.both = self.moves.swap(block, block, self.at(3, self.place.t), self.place.chips[1])
        self.hand(2)

    def from_ctx(self):
        self.ctx()
        self.hand(1)

    def from_both(self):
        self.both()
        self.hand(3)

    def finish(self):
        self.here()
        for wait in self.beside:
            wait()


class Collect:
    def __init__(self, moves, place, part, held, first, ctx_in, pair_in, sending, load):
        self.moves, self.place = moves, place
        self.first, self.ctx_in, self.pair_in, self.sending = first, ctx_in, pair_in, sending
        t = place.t
        self.hands, self.loads = {}, {}
        for j in (3, 1, 2, 0):
            self.hands[j] = moves.swap(part(j, 1 - t), first.at[j], first.at[j], place.sibling)
            if load:
                self.loads[j] = moves.load(part(j, t), held.at[j])
        self.held = (lambda j: held.at[j]) if load else (lambda j: part(j, t))

    def two(self, j, at):
        return self.held(j)[at].astype(F32) + self.first[j, at].astype(F32)

    def ready(self, j):
        self.hands[j]()
        if j in self.loads:
            self.loads[j]()

    def to_ctx(self):
        self.waits = {}
        for j, slot in ((3, 0), (1, 1)):
            self.ready(j)

            def body(at):
                self.sending[slot, at] = self.two(j, at).astype(BF16)

            row_loop(self.sending.shape[1], body)
            self.waits[j] = self.moves.swap(
                self.sending.at[slot], self.ctx_in.at[slot], self.ctx_in.at[slot], self.place.chips[1]
            )

    def to_pair(self):
        self.ready(2)
        self.waits[3]()

        def body(at):
            self.sending[2, at] = (self.two(2, at) + self.ctx_in[0, at].astype(F32)).astype(BF16)

        row_loop(self.sending.shape[1], body)
        self.waits[2] = self.moves.swap(self.sending.at[2], self.pair_in, self.pair_in, self.place.chips[2])

    def finish(self):
        self.ready(0)
        self.waits[1]()
        self.waits[2]()

    def total(self, at):
        return self.two(0, at) + (self.ctx_in[1, at].astype(F32) + self.pair_in[at].astype(F32))


def collect_buffers(rows, width):
    return [
        pltpu.VMEM((4, rows, width), BF16),
        pltpu.VMEM((2, rows, width), BF16),
        pltpu.VMEM((rows, width), BF16),
        pltpu.VMEM((3, rows, width), BF16),
    ]


def row_loop(rows, body):
    step = 16

    @pl.loop(0, rows // step)
    def _(i):
        body(pl.ds(pl.multiple_of(i * step, step), step))


def unit_and_scale(x):
    scale = lax.rsqrt(jnp.mean(x * x, axis=-1, keepdims=True) + EPS)
    return x * scale, scale


class Gather:
    def __init__(self, moves, place, block):
        self.moves, self.place, self.block = moves, place, block
        self.waits = {}

    def forward(self, mask, src=None):
        done = [i for i, b in enumerate(self.place.bits) if mask & b]
        here = self.block(self.place.block(mask))
        for b in self.place.bits[max(done, default=-1) + 1 :]:
            self.waits[mask | b] = self.moves.swap(
                here if src is None else src, here, self.block(self.place.block(mask | b)), self.place.along(b)
            )

    def masks(self, stage):
        out = [0, PAIR]
        for b in self.place.bits[:stage]:
            out += [m | b for m in out]
        return [m | self.place.bits[stage] for m in out]

    def middle(self):
        for stage in range(len(self.place.bits) - 1):
            for m in self.masks(stage):
                self.waits.pop(m)()
                self.forward(m)

    def finish(self):
        for wait in self.waits.values():
            wait()


def head_unit(x):
    scale = lax.rsqrt(jnp.mean(x * x, axis=-1, keepdims=True) + EPS)
    return x * scale, scale


def rot(a, cos, sin):
    return a * cos + pltpu.roll(a, a.shape[-1] // 2, 1) * sin


def rot_back(b, cos, sin):
    return b * cos - pltpu.roll(b, b.shape[-1] // 2, 1) * sin


def allowed_keys(seg_col, seg_row):
    length = seg_col.shape[0]
    row = lax.broadcasted_iota(jnp.int32, (length, length), 0)
    col = lax.broadcasted_iota(jnp.int32, (length, length), 1)
    return (seg_col == seg_row) & (row >= col)


def soft_of(scores):
    peak = jnp.max(scores, axis=-1, keepdims=True)
    lse = peak + jnp.log(jnp.sum(jnp.exp(scores - peak), axis=-1, keepdims=True))
    return jnp.exp(scores - lse)


def attend_one(groups, s, qkv, seg_col, seg_row, cos_ref, sin_ref, gain_q, gain_k, out):
    d = gain_q.shape[-1]
    length = cos_ref.shape[1]
    rows = pl.ds(pl.multiple_of(s * length, length), length)
    cos, sin = cos_ref[s], sin_ref[s]
    allowed = allowed_keys(seg_col[s], seg_row[s])
    unit_k, _ = head_unit(qkv[rows, groups * d : (groups + 1) * d].astype(F32))
    key = rot(unit_k * gain_k[...], cos, sin).astype(BF16)
    value = qkv[rows, (groups + 1) * d : (groups + 2) * d]
    for g in range(groups):
        unit_q, _ = head_unit(qkv[rows, g * d : (g + 1) * d].astype(F32))
        query = rot(unit_q * gain_q[...], cos, sin).astype(BF16)
        scores = jnp.where(allowed, dot_cols(query, key) * d**-0.5, -jnp.inf)
        soft = soft_of(scores).astype(BF16)
        out[rows, g * d : (g + 1) * d] = dot(soft, value).astype(BF16)


def attend_back_kernel(
    groups, qkv, att, datt, seg_col, seg_row, cos_ref, sin_ref, gain_q, gain_k, grad, gains
):
    d = gain_q.shape[-1]
    cos, sin = cos_ref[0], sin_ref[0]
    scale = d**-0.5
    allowed = allowed_keys(seg_col[0], seg_row[0])
    unit_k, scale_k = head_unit(qkv[0, :, groups * d : (groups + 1) * d].astype(F32))
    key = rot(unit_k * gain_k[...], cos, sin).astype(BF16)
    value = qkv[0, :, (groups + 1) * d : (groups + 2) * d]
    key_grad = jnp.zeros(unit_k.shape, F32)
    value_grad = jnp.zeros(unit_k.shape, F32)
    gq = jnp.zeros((8, d), F32)

    def through_norm(b, unit, scale_, gain):
        e = b * gain
        return scale_ * (e - unit * jnp.mean(e * unit, axis=-1, keepdims=True))

    for g in range(groups):
        at = slice(g * d, (g + 1) * d)
        unit_q, scale_q = head_unit(qkv[0, :, at].astype(F32))
        query = rot(unit_q * gain_q[...], cos, sin).astype(BF16)
        scores = jnp.where(allowed, dot_cols(query, key) * scale, -jnp.inf)
        soft = soft_of(scores)
        up = datt[0, :, at]
        delta = jnp.sum(up.astype(F32) * att[0, :, at].astype(F32), axis=-1, keepdims=True)
        ds = (soft * (dot_cols(up, value) - delta) * scale).astype(BF16)
        value_grad += dot_rows(soft.astype(BF16), up)
        key_grad += dot_rows(ds, query)
        b = rot_back(dot(ds, key), cos, sin)
        gq += jnp.sum((b * unit_q).reshape(-1, 8, d), axis=0)
        grad[0, :, at] = through_norm(b, unit_q, scale_q, gain_q[...]).astype(BF16)
    b = rot_back(key_grad, cos, sin)
    gk = jnp.sum((b * unit_k).reshape(-1, 8, d), axis=0)
    grad[0, :, groups * d : (groups + 1) * d] = through_norm(b, unit_k, scale_k, gain_k[...]).astype(BF16)
    grad[0, :, (groups + 1) * d : (groups + 2) * d] = value_grad.astype(BF16)
    gains[0, 0] = gq
    gains[0, 1] = gk


def per_sequence(*shape):
    return pl.BlockSpec((1, *shape), lambda s: (s,) + (0,) * len(shape))


def attention_specs(length, d):
    return [
        per_sequence(length, 1),
        per_sequence(1, length),
        per_sequence(length, d),
        per_sequence(length, d),
        pl.BlockSpec((1, d), lambda s: (0, 0)),
        pl.BlockSpec((1, d), lambda s: (0, 0)),
    ]


def attend_back(groups, qkv, att, datt, common):
    n, length, width = qkv.shape
    d = width // (groups + 2)
    return pl.pallas_call(
        functools.partial(attend_back_kernel, groups),
        grid=(n,),
        out_shape=(
            jax.ShapeDtypeStruct((n, length, width), BF16),
            jax.ShapeDtypeStruct((n, 2, 8, d), F32),
        ),
        in_specs=[
            per_sequence(length, width),
            per_sequence(length, groups * d),
            per_sequence(length, groups * d),
            *attention_specs(length, d),
        ],
        out_specs=(per_sequence(length, width), per_sequence(2, 8, d)),
        compiler_params=pltpu.CompilerParams(vmem_limit_bytes=40 << 20),
        cost_estimate=pl.CostEstimate(
            flops=n * groups * length * length * (10 * d + 30),
            bytes_accessed=n * length * width * 8,
            transcendentals=n * groups * length * length * 2,
        ),
        name="attend_back",
    )(qkv, att, datt, *common)


def forward_kernel(
    bits, groups, natural,
    hidden, cot, gain_attn, gain_mlp, seg_col, seg_row, cos, sin, gain_q, gain_k, wq, wk, wv, wo, wg, wu, wd,
    mid, normed_one, normed_two, cot_rows, qkv_out, att_out, qkv_weight, out_weight, gate_weight, up_weight, down_weight,
    own_one, own_two, rows_one, w_qkv, w_out, qkv, att, part, first, ctx_in, pair_in, sending, send, recv, local,
):
    place = Place(bits)
    moves = Moves(send, recv, local)
    rows, width = hidden.shape
    at_rows, ff_rows, ff_cols = wq.shape[0], wg.shape[0], wg.shape[1] // 2
    q_cols, kv_cols = wq.shape[1] // 4, wk.shape[1] // 4

    def lanes(start, size):
        return pl.ds(pl.multiple_of(start, size), size)

    def qkv_rows(f, c=None):
        if c is None:
            return lanes(f * 2 * at_rows, 2 * at_rows)
        return lanes((f * 2 + c) * at_rows, at_rows)

    place.greet()

    def out_block(f, c=None):
        return w_out.at[:, qkv_rows(f, c)] if natural else w_out.at[qkv_rows(f, c)]

    def out_chunk(j):
        at = lanes(place.chunk_of[j] * q_cols, q_cols)
        return wo.at[at] if natural else wo.at[:, at]

    pieces = (
        (wq, q_cols, pl.ds(0, q_cols)),
        (wk, kv_cols, pl.ds(q_cols, kv_cols)),
        (wv, kv_cols, pl.ds(q_cols + kv_cols, kv_cols)),
    )
    f0, c0, _ = place.at[0]
    qkv_in, out_in = {}, {}
    for j in (3, 2, 1):
        fj, cj, _ = place.at[j]
        qkv_in[j] = [
            moves.swap(
                w.at[:, lanes(place.chunk_of[j] * size, size)],
                w_qkv.at[qkv_rows(f0, c0), to],
                w_qkv.at[qkv_rows(fj, cj), to],
                place.chips[j],
            )
            for w, size, to in pieces
        ]
    qkv_in[0] = [
        moves.load(w.at[:, lanes(place.chunk_of[0] * size, size)], w_qkv.at[qkv_rows(f0, c0), to])
        for w, size, to in pieces
    ]
    for j in (3, 2, 1):
        fj, cj, _ = place.at[j]
        out_in[j] = moves.swap(out_chunk(j), out_block(f0, c0), out_block(fj, cj), place.chips[j])
    out_in[0] = moves.load(out_chunk(0), out_block(f0, c0))

    def rows_block(w):
        return lambda f: w.at[lanes(f * ff_rows, ff_rows)]

    def cols_block(w):
        return lambda f: w.at[:, lanes(f * ff_rows, ff_rows)]

    mine, theirs = lanes(place.pair * ff_cols, ff_cols), lanes((1 - place.pair) * ff_cols, ff_cols)
    feed = [
        (Gather(moves, place, rows_block(gate_weight)), wg.at[:, mine], wg.at[:, theirs]),
        (Gather(moves, place, rows_block(up_weight)), wu.at[:, mine], wu.at[:, theirs]),
        (Gather(moves, place, cols_block(down_weight)), wd.at[mine], wd.at[theirs])
        if natural
        else (Gather(moves, place, rows_block(down_weight)), wd.at[:, mine], wd.at[:, theirs]),
    ]

    def swap_pair(i):
        gather, own, other = feed[i]
        gather.waits[PAIR] = moves.swap(
            other, gather.block(place.f), gather.block(place.block(PAIR)), place.along(PAIR)
        )
        moves.store(own, gather.block(place.f))

    def norm_one(at):
        unit, _ = unit_and_scale(hidden[at].astype(F32))
        own_one[at] = (unit * gain_attn[...]).astype(BF16)

    row_loop(rows, norm_one)
    spread_one = Spread(moves, place, own_one, rows_one)

    qkv_gather = Gather(moves, place, lambda f: w_qkv.at[qkv_rows(f)])
    out_gather = Gather(moves, place, out_block)
    for gather, arrivals in ((qkv_gather, qkv_in), (out_gather, {j: [w] for j, w in out_in.items()})):
        for wait in (*arrivals[0], *arrivals[1]):
            wait()
        gather.forward(0)
        for wait in (*arrivals[2], *arrivals[3]):
            wait()
        gather.forward(PAIR)
    swap_pair(0)
    spread_one.from_pair()
    spread_one.from_ctx()
    qkv_gather.middle()
    out_gather.middle()
    feed[0][0].forward(0, feed[0][1])
    feed[0][0].waits.pop(PAIR)()
    feed[0][0].forward(PAIR)
    swap_pair(1)
    spread_one.from_both()
    spread_one.finish()
    qkv_gather.finish()

    moves.store(rows_one, normed_one)
    moves.store(w_qkv, qkv_weight)
    step = 2 * rows

    @pl.loop(0, 8 * rows // step)
    def _(i):
        at = lanes(i * step, step)
        qkv[at] = dot(rows_one[at], w_qkv[...]).astype(BF16)

    moves.store(qkv, qkv_out)
    spread_cot = Spread(moves, place, cot, cot_rows)
    swap_pair(2)

    def pump(i):
        feed[i][0].middle()
        if i + 1 < len(feed):
            gather, own, _ = feed[i + 1]
            gather.forward(0, own)
            gather.waits.pop(PAIR)()
            gather.forward(PAIR)

    @pl.loop(0, cos.shape[0])
    def _(s):
        attend_one(groups, s, qkv, seg_col, seg_row, cos, sin, gain_q, gain_k, att)

    moves.store(att, att_out)
    spread_cot.from_pair()
    out_gather.finish()
    moves.store(w_out, out_weight)

    @pl.loop(0, 8)
    def _(i):
        part[i] = (dot if natural else dot_cols)(att[lanes(i * rows, rows)], w_out[...]).astype(BF16)

    collect = Collect(
        moves, place, lambda j, t: part.at[place.rows_of[j] + t], None, first, ctx_in, pair_in, sending, False
    )
    collect.to_ctx()
    spread_cot.from_ctx()
    pump(0)
    collect.to_pair()
    spread_cot.from_both()
    collect.finish()

    def norm_two(at):
        x = hidden[at].astype(F32) + collect.total(at)
        mid[at] = x
        unit, _ = unit_and_scale(x)
        own_two[at] = (unit * gain_mlp[...]).astype(BF16)

    row_loop(rows, norm_two)
    spread_two = Spread(moves, place, own_two, normed_two)
    spread_two.from_pair()
    pump(1)
    spread_two.from_ctx()
    spread_two.from_both()
    spread_two.finish()
    spread_cot.finish()
    pump(2)
    for gather, _, _ in feed:
        gather.finish()
    moves.close()


def norm_back(grad, x, gain, gain_grad):
    unit, scale = unit_and_scale(x)
    gain_grad[...] += jnp.sum((grad * unit).reshape(-1, 8, grad.shape[-1]), axis=0)
    e = grad * gain
    return scale * (e - unit * jnp.mean(e * unit, axis=-1, keepdims=True))


def turn_kernel(
    bits, partial, mid, cot, gain, grad_mid, gain_grad, out,
    own, held, first, ctx_in, pair_in, sending, send, recv, local,
):
    place = Place(bits)
    moves = Moves(send, recv, local)
    place.greet()
    collect = Collect(
        moves, place, lambda j, t: partial.at[place.rows_of[j] + t], held, first, ctx_in, pair_in, sending, True
    )
    collect.to_ctx()
    collect.to_pair()
    collect.finish()
    gain_grad[...] = jnp.zeros_like(gain_grad)

    def back(at):
        g = cot[at].astype(F32) + norm_back(collect.total(at), mid[at], gain[...], gain_grad)
        grad_mid[at] = g
        own[at] = g.astype(BF16)

    row_loop(mid.shape[0], back)
    spread = Spread(moves, place, own, out)
    spread.from_pair()
    spread.from_ctx()
    spread.from_both()
    spread.finish()
    moves.close()


def last_kernel(
    bits, partial, hidden, grad_mid, gain, grad_in, gain_grad,
    held, first, ctx_in, pair_in, sending, send, recv, local,
):
    place = Place(bits)
    moves = Moves(send, recv, local)
    place.greet()
    collect = Collect(
        moves, place, lambda j, t: partial.at[place.rows_of[j] + t], held, first, ctx_in, pair_in, sending, True
    )
    collect.to_ctx()
    collect.to_pair()
    collect.finish()
    gain_grad[...] = jnp.zeros_like(gain_grad)

    def back(at):
        grad_in[at] = grad_mid[at] + norm_back(
            collect.total(at), hidden[at].astype(F32), gain[...], gain_grad
        )

    row_loop(hidden.shape[0], back)
    moves.close()


VMEM_SPEC = pl.BlockSpec(memory_space=pltpu.VMEM)
ANY_SPEC = pl.BlockSpec(memory_space=pl.ANY)


def comm_call(kernel, bits, collective_id, operands, in_specs, outs, out_specs, scratch, nbytes, copies, *more):
    return pl.pallas_call(
        functools.partial(kernel, bits, *more),
        out_shape=outs,
        in_specs=in_specs,
        out_specs=out_specs,
        scratch_shapes=[
            *scratch,
            pltpu.SemaphoreType.DMA((copies,)),
            pltpu.SemaphoreType.DMA((copies,)),
            pltpu.SemaphoreType.DMA((40,)),
        ],
        compiler_params=pltpu.CompilerParams(
            collective_id=collective_id, has_side_effects=True, vmem_limit_bytes=56 << 20
        ),
        cost_estimate=pl.CostEstimate(flops=nbytes * 20, bytes_accessed=nbytes, transcendentals=0),
        name=kernel.__name__,
    )(*operands)


def build(mesh):
    n = mesh.size
    n_f = mesh.shape["fsdp"]
    spread_bits = [b for b in (1 << i for i in range(n_f.bit_length() - 2, -1, -1)) if b != PAIR]
    all_bits = sorted([*spread_bits, PAIR], reverse=True)

    def swap(v, bit):
        return lax.ppermute(v, AXES, [(i, i ^ bit) for i in range(n)])

    def bit_of(f, b):
        return (f // b) % 2

    def in_order(bit, own, other, axis):
        low = jnp.where(bit == 0, own, other)
        high = jnp.where(bit == 0, other, own)
        return jnp.stack([low, high], axis=axis)

    def pick(v, index, axis):
        return lax.dynamic_index_in_dim(v, index, axis, keepdims=False)

    def scatter(keep, got, f, width):
        v = keep + got.astype(F32)
        have = [b for b in all_bits if b != 1]
        v = v.reshape(*([2] * len(have)), width, v.shape[-1])
        for b in [b for b in reversed(spread_bits) if b != 1]:
            axis = have.index(b)
            bit = bit_of(f, b)
            v = pick(v, bit, axis) + swap(pick(v, 1 - bit, axis).astype(BF16), b * 4).astype(F32)
            have.remove(b)
        return v

    def body(
        hidden_in,
        cotangent,
        segments,
        w_query,
        key_projection_weight,
        value_projection_weight,
        w_out,
        w_gate,
        w_up,
        w_down,
        gain_attn,
        gain_mlp,
        gain_query,
        key_norm_gain,
    ):
        rows, width = hidden_in.shape
        d = gain_query.shape[0]
        length = segments.shape[0]
        f, c = lax.axis_index("fsdp"), lax.axis_index("ctx")
        pair = bit_of(f, PAIR)
        at_rows = w_query.shape[0]
        ff_rows = w_gate.shape[0]
        ff_cols = w_gate.shape[1] // 2
        q_cols, kv_cols = w_query.shape[1] // 4, key_projection_weight.shape[1] // 4
        groups = q_cols // kv_cols

        seg = in_order(pair, segments, swap(segments, PAIR_BIT), 0)
        before = jnp.sum((seg[:, None, :] < seg[:, :, None]).astype(jnp.int32), axis=-1)
        positions = jnp.arange(length, dtype=jnp.int32)[None] - before
        freqs = THETA ** (-2.0 * jnp.arange(d // 2, dtype=F32) / d)
        angles = positions.astype(F32)[..., None] * freqs
        cos, sin = jnp.cos(angles), jnp.sin(angles)
        common = (
            seg[:, :, None],
            seg[:, None, :],
            jnp.concatenate([cos, cos], axis=-1),
            jnp.concatenate([-sin, sin], axis=-1),
            gain_query[None],
            key_norm_gain[None],
        )

        n_rows = 8 * rows
        all_rows = jax.ShapeDtypeStruct((n_rows, width), BF16)
        own_rows = jax.ShapeDtypeStruct((rows, width), F32)
        gain_rows = jax.ShapeDtypeStruct((8, width), F32)
        block = pltpu.VMEM((rows, width), BF16)
        nbytes = rows * width * 16
        qkv_cols = q_cols + 2 * kv_cols

        def shape(*dims):
            return jax.ShapeDtypeStruct(dims, BF16)

        copies = 120 + 10 * n_f
        natural = at_rows % 128 == 0 and ff_rows % 128 == 0
        out_dims = (q_cols, width) if natural else (width, q_cols)
        down_dims = (ff_cols, width) if natural else (width, ff_cols)
        times, times_t = (dot, dot_cols) if natural else (dot_cols, dot)
        (
            residual_mid, normed_one, normed_two, grad_rows, qkv, attended, full_qkv, full_out,
            full_gate, full_up, full_down,
        ) = comm_call(
            forward_kernel, spread_bits, 0,
            (hidden_in, cotangent, gain_attn[None], gain_mlp[None], *common, w_query, key_projection_weight,
             value_projection_weight, w_out if natural else w_out.T, w_gate, w_up, w_down if natural else w_down.T),
            [VMEM_SPEC] * 10 + [ANY_SPEC] * 7,
            (own_rows, all_rows, all_rows, all_rows, shape(n_rows, qkv_cols), shape(n_rows, q_cols),
             shape(width, qkv_cols), shape(*out_dims), shape(width, ff_cols), shape(width, ff_cols),
             shape(*down_dims)),
            (VMEM_SPEC, *[ANY_SPEC] * 10),
            [block, block, pltpu.VMEM((n_rows, width), BF16), pltpu.VMEM((width, qkv_cols), BF16),
             pltpu.VMEM(out_dims, BF16), pltpu.VMEM((n_rows, qkv_cols), BF16),
             pltpu.VMEM((n_rows, q_cols), BF16), pltpu.VMEM((8, rows, width), BF16),
             *collect_buffers(rows, width)],
            16 * nbytes, copies, groups, natural,
        )
        qkv3 = qkv.reshape(2, length, qkv_cols)
        attended3 = attended.reshape(2, length, q_cols)
        teams = sorted(
            sorted(i ^ b ^ p for b in range(4) for p in (0, PAIR_BIT))
            for i in range(0, n, 4)
            if not i & PAIR_BIT
        )

        gate_pre = dot(normed_two, full_gate)
        up_pre = dot(normed_two, full_up)
        gate_sig = jax.nn.sigmoid(gate_pre)
        gate_act = gate_pre * gate_sig
        mixed = (gate_act * up_pre).astype(BF16)
        grad_mixed = times_t(grad_rows, full_down)
        grad_gate = (grad_mixed * up_pre * gate_sig * (1.0 + gate_pre * (1.0 - gate_sig))).astype(BF16)
        grad_up = (grad_mixed * gate_act).astype(BF16)
        norm_two_part = (dot_cols(grad_gate, full_gate) + dot_cols(grad_up, full_up)).astype(BF16)
        grad_mid, gain_mlp_part, grad_mid_rows = comm_call(
            turn_kernel, spread_bits, 2, (norm_two_part.reshape(8, rows, width), residual_mid, cotangent, gain_mlp[None]),
            [ANY_SPEC, VMEM_SPEC, VMEM_SPEC, VMEM_SPEC], (own_rows, gain_rows, all_rows),
            (VMEM_SPEC, VMEM_SPEC, ANY_SPEC),
            [block, pltpu.VMEM((4, rows, width), BF16), *collect_buffers(rows, width)], 2 * nbytes, 40,
        )

        down_part = times(mixed, full_down).astype(BF16)
        hidden_out = residual_mid + lax.psum_scatter(
            down_part, AXES, scatter_dimension=0, axis_index_groups=teams, tiled=True
        ).astype(F32)

        low = bit_of(f, 1)

        def weight_grad(acts, grads):
            split = acts.reshape(acts.shape[0], n_f // 2, 2, width // n_f)
            mine = pick(split, low, 2).reshape(acts.shape[0], -1)
            theirs = pick(split, 1 - low, 2).reshape(acts.shape[0], -1)
            got = swap(dot_rows(theirs, grads).astype(BF16), 4)
            return scatter(dot_rows(mine, grads), got, f, width // n_f)

        def ff_grad(acts, grads):
            v = weight_grad(acts, grads)
            other = swap(pick(v, 1 - pair, 0).astype(BF16), PAIR_BIT).astype(F32)
            return in_order(pair, pick(v, pair, 0), other, 1).reshape(ff_rows, 2 * ff_cols)

        grad_w_gate = ff_grad(normed_two, grad_gate)
        grad_w_up = ff_grad(normed_two, grad_up)
        grad_w_down = ff_grad(grad_rows, mixed).T

        def attn_grad(acts, grads):
            v = weight_grad(acts, grads)
            v = v.reshape(2, 2, at_rows, v.shape[-1])
            mine = pick(pick(v, pair, 0), c, 0)
            by_ctx = swap(pick(pick(v, pair, 0), 1 - c, 0).astype(BF16), CTX_BIT).astype(F32)
            by_pair = swap(pick(pick(v, 1 - pair, 0), c, 0).astype(BF16), PAIR_BIT).astype(F32)
            by_both = swap(pick(pick(v, 1 - pair, 0), 1 - c, 0).astype(BF16), CTX_BIT | PAIR_BIT).astype(F32)
            near = in_order(pair, mine, by_pair, 1)
            far = in_order(pair, by_ctx, by_both, 1)
            return in_order(c, near, far, 1)

        grad_w_out = attn_grad(grad_mid_rows, attended).reshape(at_rows, 4 * q_cols).T

        datt = times_t(grad_mid_rows, full_out).astype(BF16).reshape(attended3.shape)
        grad_qkv, head_gains = attend_back(groups, qkv3, attended3, datt, common)
        grad_qkv = grad_qkv.reshape(8 * rows, -1)
        norm_one_part = dot_cols(grad_qkv, full_qkv).astype(BF16)
        grad_input, gain_attn_part = comm_call(
            last_kernel, spread_bits, 3, (norm_one_part.reshape(8, rows, width), hidden_in, grad_mid, gain_attn[None]),
            [ANY_SPEC, VMEM_SPEC, VMEM_SPEC, VMEM_SPEC], (own_rows, gain_rows), (VMEM_SPEC, VMEM_SPEC),
            [pltpu.VMEM((4, rows, width), BF16), *collect_buffers(rows, width)], nbytes, 40,
        )
        grad_qkv_w = attn_grad(normed_one, grad_qkv)
        grad_w_query = grad_qkv_w[..., :q_cols].reshape(at_rows, -1)
        grad_w_key = grad_qkv_w[..., q_cols : q_cols + kv_cols].reshape(at_rows, -1)
        grad_w_value = grad_qkv_w[..., q_cols + kv_cols :].reshape(at_rows, -1)

        head_gains = jnp.sum(head_gains, axis=(0, 2))
        gains = jnp.concatenate(
            [jnp.sum(gain_attn_part, axis=0), jnp.sum(gain_mlp_part, axis=0), head_gains[0], head_gains[1]]
        ).reshape(-1, d)
        for i in range(n.bit_length() - 1):
            gains = gains + swap(gains, 1 << i)
        gains = gains.reshape(-1)
        return (
            hidden_out,
            grad_input,
            grad_w_query,
            grad_w_key,
            grad_w_value,
            grad_w_out,
            grad_w_gate,
            grad_w_up,
            grad_w_down,
            gains[:width],
            gains[width : 2 * width],
            gains[2 * width : 2 * width + d],
            gains[2 * width + d :],
        )

    return body


def solution(mesh):
    everyone = P(("fsdp", "ctx", "tp"), None)
    attn = P(("fsdp", "ctx"), "tp")
    attn_out = P("tp", ("fsdp", "ctx"))
    ff_in = P("fsdp", ("ctx", "tp"))
    ff_out = P(("ctx", "tp"), "fsdp")
    same = P()
    return jax.shard_map(
        build(mesh),
        mesh=mesh,
        in_specs=(
            everyone, everyone, P("fsdp"), attn, attn, attn, attn_out, ff_in, ff_in, ff_out,
            same, same, same, same,
        ),
        out_specs=(
            everyone, everyone, attn, attn, attn, attn_out, ff_in, ff_in, ff_out,
            same, same, same, same,
        ),
        check_vma=False,
    )
```

time: 847 us -> 773 us (0.913)
  waiting for transfers between devices: 243 us -> 129 us
  Pallas kernels: 222 us -> 322 us
  starting transfers between devices: 55 us -> 29 us
  other arithmetic: 34.7 us -> 16.4 us
  local copies, waits for them, and re-layouts: 187 us -> 177 us
    ppermute x44 -> x25, waiting for transfers between devices: 243 us -> 129 us  [swap(): return lax.ppermute(v, AXES, [(i, i ^ bit) for i in range(n)])]
    pallas_call x5 -> x3, Pallas kernels: 213 us -> 314 us  [comm_call(): pl.pallas_call(functools.partial(kernel, bits, *more), out_shape=outs, in...]
    reshape x1 -> x6, local copies, waits for them, and re-layouts: 0.97 us -> 34.6 us  [the longest x4 31.9 us: weight_grad(): split = acts.reshape(acts.shape[0], n_f // 2, 2, width // n_f)]
    ppermute x44 -> x25, starting transfers between devices: 55 us -> 29 us  [swap(): return lax.ppermute(v, AXES, [(i, i ^ bit) for i in range(n)])]
    another operation x3 -> x0, local copies, waits for them, and re-layouts: 23.5 us -> none  [weight_grad(): split = acts.reshape(acts.shape[0], n_f // 2, 2, width // n_f)]
    another operation x45 -> x12, other arithmetic: 23.2 us -> 2.72 us  [in_order(): return jnp.stack([low, high], axis=axis)]
    dot_general x5 -> x3, matrix products: 28 us -> 17.5 us  [dot(): lax.dot_general(left, right, (((1,), (0,)), ((), ())), preferred_element_...]
    dot_general x5, matrix products: 20.3 us -> 30.8 us  [dot_cols(): lax.dot_general(left, right, (((1,), (1,)), ((), ())), preferred_element_...]
  transfers between devices with their start and end apart: 46 -> 26, of which waited for: 17 -> 10; matrix products, arithmetic and copies ran while one was open for 31% -> 28% of each run, Pallas kernels for 27% -> 15%
where the time goes in v2:
time: 773 us; the launch traced here: 767 us
  Pallas kernels  322 us (42%)
  local copies, waits for them, and re-layouts  177 us (23%)
  waiting for transfers between devices  129 us (17%)
  matrix products  78.9 us (10%)
  starting transfers between devices  29 us (4%)
  other arithmetic  16.4 us (2%)
  between operations  15.1 us (2%)
    pallas_call x3, Pallas kernels, comm_call(): pl.pallas_call(functools.partial(kernel, bits, *more), out_shape=outs, in...  314 us
    ppermute x25, waiting for transfers between devices, swap(): return lax.ppermute(v, AXES, [(i, i ^ bit) for i in range(n)])  129 us
    unnamed x80, local copies, waits for them, and re-layouts  88.6 us
    dynamic_slice x7, local copies, waits for them, and re-layouts, pick(): return lax.dynamic_index_in_dim(v, index, axis, keepdims=False)  43.6 us
    reshape x4, local copies, waits for them, and re-layouts, weight_grad(): split = acts.reshape(acts.shape[0], n_f // 2, 2, width // n_f)  31.9 us
    dot_general x5, matrix products, dot_cols(): lax.dot_general(left, right, (((1,), (1,)), ((), ())), preferred_element_...  30.8 us
    dot_general x10, matrix products, dot_rows(): lax.dot_general(left, right, (((0,), (0,)), ((), ())), preferred_element_...  30.7 us
    ppermute x25, starting transfers between devices, swap(): return lax.ppermute(v, AXES, [(i, i ^ bit) for i in range(n)])  29 us
  transfers between devices with their start and end apart: 26, of which 10 were waited for; matrix products, arithmetic and copies ran while one was open for 28% of the time, Pallas kernels for 15%

profile of v2, /device:TPU:0, one launch (start us, length us, event | category | flops | bytes accessed | tf_op | source)
XLA Modules:
  0.0 767.1 jit_solution(10995968153838600100)
XLA Ops:
  7.2 3.1 collective-permute-start
  10.3 1.8 collective-permute-done
  14.8 1.9 fusion.22
  18.0 206.9 %forward_kernel.1 = (f32[128,2048]{1,0:T(8,128)}, bf16[1024,2048]{1,0:T(8,128)(2,1)}, bf16[1024,2048]{1,0:T(8,128)(2,1)}, bf16[1024,2048]{1,0:T(8,128)(2,1)}, bf...) custom-call(bf16[128,2048]{1,0:T(8,128)(2,1)} %hidden.3, ...), custom_call_target="tpu_custom_call" | custom-call | flops 1342177280 | bytes 67108864 | tf_op jit(solution)/shard_map/forward_kernel/pallas_call | solution.py:607
  225.0 8.0 %reshape.443 = bf16[1024,4,2,256]{3,2,1,0:T(2,128)(2,1)} reshape(bf16[1024,2048]{1,0:T(8,128)(2,1)} %get-tuple-element.32) | data formatting | bytes 8388608 | tf_op jit(solution)/shard_map/reshape | solution.py:765
  233.0 7.4 fusion.32
  240.4 5.1 fusion.33
  245.4 8.2 %reshape.450 = bf16[1024,4,2,256]{3,2,1,0:T(2,128)(2,1)} reshape(bf16[1024,2048]{1,0:T(8,128)(2,1)} %get-tuple-element.38) | data formatting | bytes 8388608 | tf_op jit(solution)/shard_map/reshape | solution.py:765
  253.7 10.1 %multiply_convert_fusion = (bf16[1024,768]{1,0:T(8,128)(2,1)}, bf16[1024,768]{1,0:T(8,128)(2,1)}, bf16[1024,768]{1,0:T(8,128)(2,1)S(1)}) fusion(f32[1024,768]{1,0:T(8,128)} %fusion.32, f32[1024,768]{1,0:T(8,128)} %fusion.33, bf16[1024,2048]{1,0:T(8,128)(2,1)} %get-tuple-element.38, bf16[768,2048]{1,0:T(8,128)(2,1)S(1)} %copy-done.26), kind=kOutput, calls=%fused_computation.6 | convolution fusion | flops 3233021952 | bytes 18350080 | tf_op jit(solution)/shard_map/dot_general | solution.py:26
  264.9 5.0 convolution_convert_fusion.1
  269.9 7.8 %reshape.429 = bf16[1024,4,2,256]{3,2,1,0:T(2,128)(2,1)} reshape(bf16[1024,2048]{1,0:T(8,128)(2,1)} %get-tuple-element.45) | data formatting | bytes 8388608 | tf_op jit(solution)/shard_map/reshape | solution.py:765
  277.7 11.6 %constant_dynamic-slice_fusion.10 = (bf16[1024,4,1,256]{3,2,1,0:T(2,128)(2,1)}, bf16[1024,4,1,256]{3,2,1,0:T(2,128)(2,1)}) fusion(bf16[1024,4,2,256]{3,2,1,0:T(2,128)(2,1)} %reshape.429, s32[]{:T(128)S(6)} %select_n.251, s32[]{:T(128)S(6)} %select_n.250), kind=kLoop, calls=%fused_computation.115 | loop fusion | bytes 8388616 | tf_op jit(solution)/shard_map/jit(dynamic_index_in_dim)/dynamic_slice | solution.py:644
  289.3 10.6 %copy.80 = bf16[1024,4,1,256]{0,3,1,2:T(8,128)(2,1)} copy(bf16[1024,4,1,256]{3,2,1,0:T(2,128)(2,1)} %get-tuple-element.58) | data formatting | bytes 4194304
  299.9 11.3 %constant_dynamic-slice_fusion.2 = (bf16[1024,4,1,256]{3,2,1,0:T(2,128)(2,1)}, bf16[1024,4,1,256]{3,2,1,0:T(2,128)(2,1)}) fusion(bf16[1024,4,2,256]{3,2,1,0:T(2,128)(2,1)} %reshape.443, s32[]{:T(128)S(6)} %select_n.251, s32[]{:T(128)S(6)} %select_n.250), kind=kLoop, calls=%fused_computation.107 | loop fusion | bytes 8388616 | tf_op jit(solution)/shard_map/jit(dynamic_index_in_dim)/dynamic_slice | solution.py:644
  311.2 9.4 %copy.87 = bf16[1024,4,1,256]{0,3,1,2:T(8,128)(2,1)S(1)} copy(bf16[1024,4,1,256]{3,2,1,0:T(2,128)(2,1)} %get-tuple-element.54) | data formatting | bytes 4194304
  320.6 6.0 fusion.34
  326.6 3.0 convolution_convert_fusion.4
  329.5 3.0 convolution_convert_fusion.3
  332.5 2.6 collective-permute-start.11
  335.2 5.1 add_convert_fusion
  340.2 70.0 %turn_kernel.1 = (f32[128,2048]{1,0:T(8,128)}, f32[8,2048]{1,0:T(8,128)}, bf16[1024,2048]{1,0:T(8,128)(2,1)}) custom-call(bf16[8,128,2048]{2,1,0:T(8,128)(2,1)} %bitcast.187, f32[128,2048]{1,0:T(8,128)} %get-tuple-element.31.mid, bf16[128,2048]{1,0:T(8,128)(2,1)} %cot.3, f32[1,2048]{1,0:T(1,128)} %bitcast.219), custom_call_target="tpu_custom_call" | custom-call | flops 167772160 | bytes 8388608 | tf_op jit(solution)/shard_map/turn_kernel/pallas_call | solution.py:607
  410.3 7.9 %reshape.437 = bf16[1024,4,2,256]{3,2,1,0:T(2,128)(2,1)} reshape(bf16[1024,2048]{1,0:T(8,128)(2,1)} %get-tuple-element.39) | data formatting | bytes 8388608 | tf_op jit(solution)/shard_map/reshape | solution.py:765
  418.3 3.6 convolution_convert_fusion.7
  422.0 8.6 %attend_back.1 = (bf16[2,512,512]{2,1,0:T(8,128)(2,1)S(1)}, f32[2,2,8,128]{3,2,1,0:T(8,128)S(1)}) custom-call(bf16[2,512,512]{2,1,0:T(8,128)(2,1)S(1)} %bitcast.181, bf16[2,512,256]{2,1,0:T(8,128)(2,1)S(1)} %bitcast.182, bf16[2,512,256]{2,1,0:T(8,128)(2,1)S(1)} %bitcast.186, s32[2,512,1]{2,1,0:T(8,128)S(1)} %copy-done.2, s32[2,1,512]{2,1,0:T(1,128)S(1)} %copy-done.3, ...), custom_call_target="tpu_custom_call" | custom-call | flops 1373634560 | bytes 4194304 | tf_op jit(solution)/shard_map/attend_back/pallas_call | solution.py:347
  430.6 6.0 convolution_convert_fusion
  436.6 36.8 %last_kernel.1 = (f32[128,2048]{1,0:T(8,128)}, f32[8,2048]{1,0:T(8,128)}) custom-call(bf16[8,128,2048]{2,1,0:T(8,128)(2,1)} %bitcast.188, bf16[128,2048]{1,0:T(8,128)(2,1)} %hidden.3, f32[128,2048]{1,0:T(8,128)} %get-tuple-element.43.grad_mid, f32[1,2048]{1,0:T(1,128)} %bitcast.221), custom_call_target="tpu_custom_call" | custom-call | flops 83886080 | bytes 4194304 | tf_op jit(solution)/shard_map/last_kernel/pallas_call | solution.py:607
  474.4 4.0 convolution_convert_fusion.5
  478.4 2.1 collective-permute-start.21
  480.4 9.8 %constant_dynamic-slice_fusion.8 = (bf16[1024,4,1,256]{3,2,1,0:T(2,128)(2,1)}, bf16[1024,4,1,256]{3,2,1,0:T(2,128)(2,1)}) fusion(bf16[1024,4,2,256]{3,2,1,0:T(2,128)(2,1)S(1)} %copy-done.9, s32[]{:T(128)S(6)} %select_n.251, s32[]{:T(128)S(6)} %select_n.250), kind=kLoop, calls=%fused_computation.113 | loop fusion | bytes 8388616 | tf_op jit(solution)/shard_map/jit(dynamic_index_in_dim)/dynamic_slice | solution.py:644
  490.3 10.5 %copy.82 = bf16[1024,4,1,256]{0,3,1,2:T(8,128)(2,1)} copy(bf16[1024,4,1,256]{3,2,1,0:T(2,128)(2,1)} %get-tuple-element.56) | data formatting | bytes 4194304
  501.2 2.4 convolution_convert_fusion.6
  503.6 1.8 collective-permute-start.6
  506.0 9.9 %constant_dynamic-slice_fusion = (bf16[1024,4,1,256]{3,2,1,0:T(2,128)(2,1)}, bf16[1024,4,1,256]{3,2,1,0:T(2,128)(2,1)}) fusion(bf16[1024,4,2,256]{3,2,1,0:T(2,128)(2,1)S(1)} %copy-done.8, s32[]{:T(128)S(6)} %select_n.251, s32[]{:T(128)S(6)} %select_n.250), kind=kLoop, calls=%fused_computation.105 | loop fusion | bytes 8388616 | tf_op jit(solution)/shard_map/jit(dynamic_index_in_dim)/dynamic_slice | solution.py:644
  515.9 10.5 %copy.89 = bf16[1024,4,1,256]{0,3,1,2:T(8,128)(2,1)} copy(bf16[1024,4,1,256]{3,2,1,0:T(2,128)(2,1)} %get-tuple-element.52) | data formatting | bytes 4194304
  526.4 1.5 collective-permute-start.24
  528.0 5.1 convolution_convert_fusion.2
  533.1 10.5 %copy.79 = bf16[1024,4,1,256]{0,3,1,2:T(8,128)(2,1)} copy(bf16[1024,4,1,256]{3,2,1,0:T(2,128)(2,1)} %get-tuple-element.59) | data formatting | bytes 4194304
  543.6 10.5 %copy.86 = bf16[1024,4,1,256]{0,3,1,2:T(8,128)(2,1)} copy(bf16[1024,4,1,256]{3,2,1,0:T(2,128)(2,1)} %get-tuple-element.55) | data formatting | bytes 4194304
  554.1 10.5 %copy.81 = bf16[1024,4,1,256]{0,3,1,2:T(8,128)(2,1)} copy(bf16[1024,4,1,256]{3,2,1,0:T(2,128)(2,1)} %get-tuple-element.57) | data formatting | bytes 4194304
  564.7 10.8 %copy.88 = bf16[1024,4,1,256]{0,3,1,2:T(8,128)(2,1)} copy(bf16[1024,4,1,256]{3,2,1,0:T(2,128)(2,1)} %get-tuple-element.53) | data formatting | bytes 4194304
  575.5 2.3 convert_add_fusion.4
  577.9 1.5 collective-permute-start.7
  580.5 11.0 %collective-permute-done.7 = bf16[2,256,256]{2,1,0:T(8,128)(2,1)S(1)} collective-permute-done((bf16[2,256,256]{2,1,0:T(8,128)(2,1)S(1)}, bf16[2,256,256]{2,1,0:T(8,128)(2,1)S(1)}, u32[]{:S(2)}, u32[]{:S(2)}) %collective-permute-start.7) | collective-permute-done | bytes 262176 | tf_op jit(solution)/shard_map/ppermute | solution.py:633
  595.0 3.0 collective-permute-start.10
  598.0 1.6 collective-permute-start.9
  603.4 2.6 convert_add_fusion.3
  606.1 1.4 collective-permute-start.2
  607.5 3.3 convert_add_fusion.2
  610.9 1.7 collective-permute-start.12
  612.6 3.2 convert_add_fusion.1
  616.0 1.4 collective-permute-start.15
  617.4 46.7 %collective-permute-done.2 = bf16[2,256,512]{2,1,0:T(8,128)(2,1)S(1)} collective-permute-done((bf16[2,256,512]{2,1,0:T(8,128)(2,1)S(1)}, bf16[2,256,512]{2,1,0:T(8,128)(2,1)S(1)}, u32[]{:S(2)}, u32[]{:S(2)}) %collective-permute-start.2) | collective-permute-done | bytes 524320 | tf_op jit(solution)/shard_map/ppermute | solution.py:633
  664.3 2.3 collective-permute-start.5
  667.8 1.8 convert_add_fusion
  670.7 29.8 %collective-permute-done.3 = bf16[128,512]{1,0:T(8,128)(2,1)S(1)} collective-permute-done((bf16[128,512]{1,0:T(8,128)(2,1)S(1)}, bf16[128,512]{1,0:T(8,128)(2,1)S(1)}, u32[]{:S(2)}, u32[]{:S(2)}) %collective-permute-start.3) | collective-permute-done | bytes 131104 | tf_op jit(solution)/shard_map/ppermute | solution.py:633
  701.1 2.1 collective-permute-done.5
  708.3 1.9 bitcast_add_fusion.2
  710.9 1.6 bitcast_add_fusion.1
  713.9 23.2 %collective-permute-done.18 = bf16[2,256,768]{2,1,0:T(8,128)(2,1)} collective-permute-done((bf16[2,256,768]{2,1,0:T(8,128)(2,1)}, bf16[2,256,768]{2,1,0:T(8,128)(2,1)}, u32[]{:S(2)}, u32[]{:S(2)}) %collective-permute-start.18) | collective-permute-done | bytes 786464 | tf_op jit(solution)/shard_map/ppermute | solution.py:633
  739.3 1.4 copy.90
  740.7 6.8 collective-permute-done.16
  749.1 5.9 collective-permute-done.19
  755.3 1.6 copy.78
  756.9 2.2 convert_add_fusion.5
  (163 shorter events, 31.2 us)
Async XLA Ops:
  7.2 749.7 %reduce-scatter.2.cloned.1.call-start = ((), (), s32[]{:S(2)}) async-start(), calls=%async_computation.1 | async-start | bytes 4718592 | tf_op jit(solution)/shard_map/reduce_scatter | solution.py:758
  7.2 4.9 collective-permute-start
  225.0 8.0 %copy-start.25 = (bf16[2048,768]{1,0:T(8,128)(2,1)S(1)}, bf16[2048,768]{1,0:T(8,128)(2,1)}, u32[]{:S(2)}) copy-start(bf16[2048,768]{1,0:T(8,128)(2,1)} %get-tuple-element.33) | copy-start | bytes 9437188
  233.0 7.4 copy-start.10
  233.0 7.4 copy-start.23
  245.4 8.2 %copy-start.26 = (bf16[768,2048]{1,0:T(8,128)(2,1)S(1)}, bf16[768,2048]{1,0:T(8,128)(2,1)}, u32[]{:S(2)}) copy-start(bf16[768,2048]{1,0:T(8,128)(2,1)} %get-tuple-element.35) | copy-start | bytes 9437188
  263.8 1.1 copy-start.28
  320.6 6.0 copy-start.32
  326.6 3.0 copy-start.30
  329.5 5.6 copy-start.24
  332.5 275.0 %collective-permute-start.11 = (bf16[1024,768]{1,0:T(8,128)(2,1)}, bf16[1024,768]{1,0:T(8,128)(2,1)}, u32[]{:S(2)}, u32[]{:S(2)}) collective-permute-start(bf16[1024,768]{1,0:T(8,128)(2,1)} %convolution_convert_fusion.4), channel_id=1, source_target_pairs={{0,4},{1,5},{2,6},{3,7},{4,0},{5,1},{6,2},{7,3},{8,12},{9,13},{10,... | collective-permute-start | bytes 4718600 | tf_op jit(solution)/shard_map/ppermute | solution.py:633
  335.1 277.5 %collective-permute-start.14 = (bf16[1024,768]{1,0:T(8,128)(2,1)}, bf16[1024,768]{1,0:T(8,128)(2,1)}, u32[]{:S(2)}, u32[]{:S(2)}) collective-permute-start(bf16[1024,768]{1,0:T(8,128)(2,1)} %convolution_convert_fusion.3), channel_id=1, source_target_pairs={{0,4},{1,5},{2,6},{3,7},{4,0},{5,1},{6,2},{7,3},{8,12},{9,13},{10,... | collective-permute-start | bytes 4718600 | tf_op jit(solution)/shard_map/ppermute | solution.py:633
  410.3 7.9 %copy-start.27 = (bf16[256,2048]{1,0:T(8,128)(2,1)S(1)}, bf16[256,2048]{1,0:T(8,128)(2,1)}, u32[]{:S(2)}) copy-start(bf16[256,2048]{1,0:T(8,128)(2,1)} %get-tuple-element.40) | copy-start | bytes 3145732
  418.2 3.7 copy-start
  418.2 3.7 copy-start.1
  418.2 3.7 copy-start.2
  418.2 3.7 copy-start.3
  418.2 3.7 copy-start.4
  418.2 3.7 copy-start.5
  418.2 3.7 copy-start.6
  418.2 3.7 copy-start.7
  422.0 8.6 %copy-start.22 = (f32[8,2048]{1,0:T(8,128)S(1)}, f32[8,2048]{1,0:T(8,128)}, u32[]{:S(2)}) copy-start(f32[8,2048]{1,0:T(8,128)} %get-tuple-element.47) | copy-start | bytes 196612
  474.3 4.1 collective-permute-start.20
  474.4 6.1 copy-start.9
  478.3 125.0 %collective-permute-start.1 = (bf16[1024,512]{1,0:T(8,128)(2,1)}, bf16[1024,512]{1,0:T(8,128)(2,1)}, u32[]{:S(2)}, u32[]{:S(2)}) collective-permute-start(bf16[1024,512]{1,0:T(8,128)(2,1)} %convolution_convert_fusion.5), channel_id=1, source_target_pairs={{0,4},{1,5},{2,6},{3,7},{4,0},{5,1},{6,2},{7,3},{8,12},{9,13},{10,... | collective-permute-start | bytes 3145736 | tf_op jit(solution)/shard_map/ppermute | solution.py:633
  478.4 22.4 %collective-permute-start.21 = (f32[34,128]{1,0:T(8,128)S(1)}, f32[34,128]{1,0:T(8,128)S(1)}, u32[]{:S(2)}, u32[]{:S(2)}) collective-permute-start(f32[34,128]{1,0:T(8,128)S(1)} %fusion.31), channel_id=1, source_target_pairs={{0,2},{1,3},{2,0},{3,1},{4,6},{5,7},{6,4},{7,5},{8,10},{9,11},{10,... | collective-permute-start | bytes 52232 | tf_op jit(solution)/shard_map/ppermute | solution.py:633
  500.8 4.6 collective-permute-start.22
  501.2 4.8 copy-start.8
  503.6 71.8 %collective-permute-start.6 = (bf16[1024,256]{1,0:T(8,128)(2,1)S(1)}, bf16[1024,256]{1,0:T(8,128)(2,1)S(1)}, u32[]{:S(2)}, u32[]{:S(2)}) collective-permute-start(bf16[1024,256]{1,0:T(8,128)(2,1)S(1)} %convolution_convert_fusion.6), channel_id=1, source_target_pairs={{0,4},{1,5},{2,6},{3,7},{4,0},{5,1},{6,2},{7,3},{8,12},{9,13},{10,... | collective-permute-start | bytes 1572872 | tf_op jit(solution)/shard_map/ppermute | solution.py:633
  505.4 21.0 %collective-permute-start.23 = (f32[34,128]{1,0:T(8,128)S(1)}, f32[34,128]{1,0:T(8,128)S(1)}, u32[]{:S(2)}, u32[]{:S(2)}) collective-permute-start(f32[34,128]{1,0:T(8,128)S(1)} %add.206), channel_id=1, source_target_pairs={{0,8},{1,9},{2,10},{3,11},{4,12},{5,13},{6,14},{7,15},{8,0},{9,1},... | collective-permute-start | bytes 52232 | tf_op jit(solution)/shard_map/ppermute | solution.py:633
  526.4 49.0 %collective-permute-start.24 = (f32[34,128]{1,0:T(8,128)S(1)}, f32[34,128]{1,0:T(8,128)S(1)}, u32[]{:S(2)}, u32[]{:S(2)}) collective-permute-start(f32[34,128]{1,0:T(8,128)S(1)} %add.207), channel_id=1, source_target_pairs={{0,16},{1,17},{2,18},{3,19},{4,20},{5,21},{6,22},{7,23},{8,24},{9,... | collective-permute-start | bytes 52232 | tf_op jit(solution)/shard_map/ppermute | solution.py:633
  577.9 13.6 %collective-permute-start.7 = (bf16[2,256,256]{2,1,0:T(8,128)(2,1)S(1)}, bf16[2,256,256]{2,1,0:T(8,128)(2,1)S(1)}, u32[]{:S(2)}, u32[]{:S(2)}) collective-permute-start(bf16[2,256,256]{2,1,0:T(8,128)(2,1)S(1)} %fusion.19), channel_id=1, source_target_pairs={{0,16},{1,17},{2,18},{3,19},{4,20},{5,21},{6,22},{7,23},{8,24},{9,... | collective-permute-start | bytes 786440 | tf_op jit(solution)/shard_map/ppermute | solution.py:633
  591.5 0.8 copy-start.20
  592.3 11.0 %copy-start.14 = (bf16[1024,4,1,256]{0,3,1,2:T(8,128)(2,1)S(1)}, bf16[1024,4,1,256]{0,3,1,2:T(8,128)(2,1)}, u32[]{:S(2)}) copy-start(bf16[1024,4,1,256]{0,3,1,2:T(8,128)(2,1)} %copy.79) | copy-start | bytes 6291460
  593.1 4.9 collective-permute-start.8
  595.0 5.5 collective-permute-start.10
  598.0 4.5 collective-permute-start.9
  600.4 66.2 %collective-permute-start.17 = (bf16[1024,768]{1,0:T(8,128)(2,1)}, bf16[1024,768]{1,0:T(8,128)(2,1)S(1)}, u32[]{:S(2)}, u32[]{:S(2)}) collective-permute-start(bf16[1024,768]{1,0:T(8,128)(2,1)} %convolution_convert_fusion.2), channel_id=1, source_target_pairs={{0,4},{1,5},{2,6},{3,7},{4,0},{5,1},{6,2},{7,3},{8,12},{9,13},{10,... | collective-permute-start | bytes 4718600 | tf_op jit(solution)/shard_map/ppermute | solution.py:633
  603.4 4.1 copy-start.13
  603.4 4.1 copy-start.33
  606.1 57.9 %collective-permute-start.2 = (bf16[2,256,512]{2,1,0:T(8,128)(2,1)S(1)}, bf16[2,256,512]{2,1,0:T(8,128)(2,1)S(1)}, u32[]{:S(2)}, u32[]{:S(2)}) collective-permute-start(bf16[2,256,512]{2,1,0:T(8,128)(2,1)S(1)} %fusion.10), channel_id=1, source_target_pairs={{0,16},{1,17},{2,18},{3,19},{4,20},{5,21},{6,22},{7,23},{8,24},{9,... | collective-permute-start | bytes 1572872 | tf_op jit(solution)/shard_map/ppermute | solution.py:633
  607.5 5.1 copy-start.31
  610.8 5.0 copy-start.15
  610.9 97.4 %collective-permute-start.12 = (bf16[2,256,768]{2,1,0:T(8,128)(2,1)S(1)}, bf16[2,256,768]{2,1,0:T(8,128)(2,1)}, u32[]{:S(2)}, u32[]{:S(2)}) collective-permute-start(bf16[2,256,768]{2,1,0:T(8,128)(2,1)S(1)} %fusion.7), channel_id=1, source_target_pairs={{0,16},{1,17},{2,18},{3,19},{4,20},{5,21},{6,22},{7,23},{8,24},{9,... | collective-permute-start | bytes 2359304 | tf_op jit(solution)/shard_map/ppermute | solution.py:633
  615.8 48.3 %copy-start.16 = (f32[1024,768]{1,0:T(8,128)}, f32[1024,768]{1,0:T(8,128)S(1)}, u32[]{:S(2)}) copy-start(f32[1024,768]{1,0:T(8,128)S(1)} %convert_add_fusion.1) | copy-start | bytes 9437188
  615.9 52.0 %copy-start.29 = (bf16[1024,768]{1,0:T(8,128)(2,1)S(1)}, bf16[1024,768]{1,0:T(8,128)(2,1)}, u32[]{:S(2)}) copy-start(bf16[1024,768]{1,0:T(8,128)(2,1)} %copy-done.28) | copy-start | bytes 4718596
  616.0 51.9 %copy-start.12 = (bf16[1024,4,1,256]{0,3,1,2:T(8,128)(2,1)S(1)}, bf16[1024,4,1,256]{0,3,1,2:T(8,128)(2,1)}, u32[]{:S(2)}) copy-start(bf16[1024,4,1,256]{0,3,1,2:T(8,128)(2,1)} %copy.88) | copy-start | bytes 6291460
  616.0 94.4 %collective-permute-start.15 = (bf16[2,256,768]{2,1,0:T(8,128)(2,1)S(1)}, bf16[2,256,768]{2,1,0:T(8,128)(2,1)}, u32[]{:S(2)}, u32[]{:S(2)}) collective-permute-start(bf16[2,256,768]{2,1,0:T(8,128)(2,1)S(1)} %fusion.8), channel_id=1, source_target_pairs={{0,16},{1,17},{2,18},{3,19},{4,20},{5,21},{6,22},{7,23},{8,24},{9,... | collective-permute-start | bytes 2359304 | tf_op jit(solution)/shard_map/ppermute | solution.py:633
  664.3 36.3 %collective-permute-start.3 = (bf16[128,512]{1,0:T(8,128)(2,1)S(1)}, bf16[128,512]{1,0:T(8,128)(2,1)S(1)}, u32[]{:S(2)}, u32[]{:S(2)}) collective-permute-start(bf16[128,512]{1,0:T(8,128)(2,1)S(1)} %get-tuple-element.72), channel_id=1, source_target_pairs={{0,8},{1,9},{2,10},{3,11},{4,12},{5,13},{6,14},{7,15},{8,0},{9,1},... | collective-permute-start | bytes 393224 | tf_op jit(solution)/shard_map/ppermute | solution.py:633
  664.3 38.9 %collective-permute-start.5 = (bf16[128,512]{1,0:T(8,128)(2,1)S(1)}, bf16[128,512]{1,0:T(8,128)(2,1)S(1)}, u32[]{:S(2)}, u32[]{:S(2)}) collective-permute-start(bf16[128,512]{1,0:T(8,128)(2,1)S(1)} %get-tuple-element.73), channel_id=1, source_target_pairs={{0,10},{1,11},{2,8},{3,9},{4,14},{5,15},{6,12},{7,13},{8,2},{9,3},... | collective-permute-start | bytes 393224 | tf_op jit(solution)/shard_map/ppermute | solution.py:633
  666.6 36.7 %collective-permute-start.4 = (bf16[128,512]{1,0:T(8,128)(2,1)S(1)}, bf16[128,512]{1,0:T(8,128)(2,1)S(1)}, u32[]{:S(2)}, u32[]{:S(2)}) collective-permute-start(bf16[128,512]{1,0:T(8,128)(2,1)S(1)} %get-tuple-element.74), channel_id=1, source_target_pairs={{0,2},{1,3},{2,0},{3,1},{4,6},{5,7},{6,4},{7,5},{8,10},{9,11},{10,... | collective-permute-start | bytes 393224 | tf_op jit(solution)/shard_map/ppermute | solution.py:633
  669.6 33.7 %copy-start.18 = (f32[1024,768]{1,0:T(8,128)}, f32[1024,768]{1,0:T(8,128)S(1)}, u32[]{:S(2)}) copy-start(f32[1024,768]{1,0:T(8,128)S(1)} %convert_add_fusion) | copy-start | bytes 9437188
  700.5 36.5 %collective-permute-start.18 = (bf16[2,256,768]{2,1,0:T(8,128)(2,1)}, bf16[2,256,768]{2,1,0:T(8,128)(2,1)}, u32[]{:S(2)}, u32[]{:S(2)}) collective-permute-start(bf16[2,256,768]{2,1,0:T(8,128)(2,1)} %fusion.9), channel_id=1, source_target_pairs={{0,16},{1,17},{2,18},{3,19},{4,20},{5,21},{6,22},{7,23},{8,24},{9,... | collective-permute-start | bytes 2359304 | tf_op jit(solution)/shard_map/ppermute | solution.py:633
  708.3 2.6 copy-start.17
  710.3 26.7 %copy-start.19 = (f32[1024,768]{1,0:T(8,128)S(1)}, f32[1024,768]{1,0:T(8,128)}, u32[]{:S(2)}) copy-start(f32[1024,768]{1,0:T(8,128)} %copy-done.18) | copy-start | bytes 9437188
  710.3 28.8 %collective-permute-start.13 = (bf16[256,768]{1,0:T(8,128)(2,1)S(1)}, bf16[256,768]{1,0:T(8,128)(2,1)S(1)}, u32[]{:S(2)}, u32[]{:S(2)}) collective-permute-start(bf16[256,768]{1,0:T(8,128)(2,1)S(1)} %fusion.12), channel_id=1, source_target_pairs={{0,8},{1,9},{2,10},{3,11},{4,12},{5,13},{6,14},{7,15},{8,0},{9,1},... | collective-permute-start | bytes 1179656 | tf_op jit(solution)/shard_map/ppermute | solution.py:633
  712.5 35.0 %collective-permute-start.16 = (bf16[256,768]{1,0:T(8,128)(2,1)S(1)}, bf16[256,768]{1,0:T(8,128)(2,1)S(1)}, u32[]{:S(2)}, u32[]{:S(2)}) collective-permute-start(bf16[256,768]{1,0:T(8,128)(2,1)S(1)} %fusion.13), channel_id=1, source_target_pairs={{0,8},{1,9},{2,10},{3,11},{4,12},{5,13},{6,14},{7,15},{8,0},{9,1},... | collective-permute-start | bytes 1179656 | tf_op jit(solution)/shard_map/ppermute | solution.py:633
  738.4 16.6 %collective-permute-start.19 = (bf16[256,768]{1,0:T(8,128)(2,1)S(1)}, bf16[256,768]{1,0:T(8,128)(2,1)S(1)}, u32[]{:S(2)}, u32[]{:S(2)}) collective-permute-start(bf16[256,768]{1,0:T(8,128)(2,1)S(1)} %fusion.14), channel_id=1, source_target_pairs={{0,8},{1,9},{2,10},{3,11},{4,12},{5,13},{6,14},{7,15},{8,0},{9,1},... | collective-permute-start | bytes 1179656 | tf_op jit(solution)/shard_map/ppermute | solution.py:633
  755.3 1.6 copy-start.11
  756.9 2.2 copy-start.21
Sparse Core Ops, SparseCore 0:
  270.1 53.7 reduce-scatter.1

commit v3 on v2

--- a/solution.py
+++ b/solution.py
@@ -42,12 +42,12 @@
         self.sent, self.loads = 0, 0
         self.open = []
 
-    def swap(self, src, there, here, device):
+    def swap(self, src, there, here, device, open_=None):
         k = self.sent
         self.sent += 1
         copy = remote(src, there, self.send.at[k], self.recv.at[k], device)
         copy.start()
-        self.open.append(copy.wait_send)
+        (self.open if open_ is None else open_).append(copy.wait_send)
         return remote(src, here, self.send.at[k], self.recv.at[k], device).wait_recv
 
     def load(self, src, dst):
@@ -144,9 +144,9 @@
         self.moves, self.place = moves, place
         self.first, self.ctx_in, self.pair_in, self.sending = first, ctx_in, pair_in, sending
         t = place.t
-        self.hands, self.loads = {}, {}
+        self.hands, self.loads, self.open = {}, {}, []
         for j in (3, 1, 2, 0):
-            self.hands[j] = moves.swap(part(j, 1 - t), first.at[j], first.at[j], place.sibling)
+            self.hands[j] = moves.swap(part(j, 1 - t), first.at[j], first.at[j], place.sibling, self.open)
             if load:
                 self.loads[j] = moves.load(part(j, t), held.at[j])
         self.held = (lambda j: held.at[j]) if load else (lambda j: part(j, t))
@@ -169,7 +169,7 @@
 
             row_loop(self.sending.shape[1], body)
             self.waits[j] = self.moves.swap(
-                self.sending.at[slot], self.ctx_in.at[slot], self.ctx_in.at[slot], self.place.chips[1]
+                self.sending.at[slot], self.ctx_in.at[slot], self.ctx_in.at[slot], self.place.chips[1], self.open
             )
 
     def to_pair(self):
@@ -180,12 +180,16 @@
             self.sending[2, at] = (self.two(2, at) + self.ctx_in[0, at].astype(F32)).astype(BF16)
 
         row_loop(self.sending.shape[1], body)
-        self.waits[2] = self.moves.swap(self.sending.at[2], self.pair_in, self.pair_in, self.place.chips[2])
+        self.waits[2] = self.moves.swap(
+            self.sending.at[2], self.pair_in, self.pair_in, self.place.chips[2], self.open
+        )
 
     def finish(self):
         self.ready(0)
         self.waits[1]()
         self.waits[2]()
+        for wait in self.open:
+            wait()
 
     def total(self, at):
         return self.two(0, at) + (self.ctx_in[1, at].astype(F32) + self.pair_in[at].astype(F32))
@@ -286,83 +290,70 @@
         out[rows, g * d : (g + 1) * d] = dot(soft, value).astype(BF16)
 
 
-def attend_back_kernel(
-    groups, qkv, att, datt, seg_col, seg_row, cos_ref, sin_ref, gain_q, gain_k, grad, gains
+def through_norm(b, unit, scale, gain):
+    e = b * gain
+    return scale * (e - unit * jnp.mean(e * unit, axis=-1, keepdims=True))
+
+
+def attend_back_one(
+    groups, s, qkv, att, datt, seg_col, seg_row, cos_ref, sin_ref, gain_q, gain_k, grad, gains
 ):
     d = gain_q.shape[-1]
-    cos, sin = cos_ref[0], sin_ref[0]
+    length = cos_ref.shape[1]
+    rows = pl.ds(pl.multiple_of(s * length, length), length)
+    cos, sin = cos_ref[s], sin_ref[s]
     scale = d**-0.5
-    allowed = allowed_keys(seg_col[0], seg_row[0])
-    unit_k, scale_k = head_unit(qkv[0, :, groups * d : (groups + 1) * d].astype(F32))
+    allowed = allowed_keys(seg_col[s], seg_row[s])
+    at_k, at_v = slice(groups * d, (groups + 1) * d), slice((groups + 1) * d, (groups + 2) * d)
+    unit_k, scale_k = head_unit(qkv[rows, at_k].astype(F32))
     key = rot(unit_k * gain_k[...], cos, sin).astype(BF16)
-    value = qkv[0, :, (groups + 1) * d : (groups + 2) * d]
+    value = qkv[rows, at_v]
     key_grad = jnp.zeros(unit_k.shape, F32)
     value_grad = jnp.zeros(unit_k.shape, F32)
-    gq = jnp.zeros((8, d), F32)
-
-    def through_norm(b, unit, scale_, gain):
-        e = b * gain
-        return scale_ * (e - unit * jnp.mean(e * unit, axis=-1, keepdims=True))
-
     for g in range(groups):
         at = slice(g * d, (g + 1) * d)
-        unit_q, scale_q = head_unit(qkv[0, :, at].astype(F32))
+        unit_q, scale_q = head_unit(qkv[rows, at].astype(F32))
         query = rot(unit_q * gain_q[...], cos, sin).astype(BF16)
         scores = jnp.where(allowed, dot_cols(query, key) * scale, -jnp.inf)
         soft = soft_of(scores)
-        up = datt[0, :, at]
-        delta = jnp.sum(up.astype(F32) * att[0, :, at].astype(F32), axis=-1, keepdims=True)
+        up = datt[rows, at]
+        delta = jnp.sum(up.astype(F32) * att[rows, at].astype(F32), axis=-1, keepdims=True)
         ds = (soft * (dot_cols(up, value) - delta) * scale).astype(BF16)
         value_grad += dot_rows(soft.astype(BF16), up)
         key_grad += dot_rows(ds, query)
         b = rot_back(dot(ds, key), cos, sin)
-        gq += jnp.sum((b * unit_q).reshape(-1, 8, d), axis=0)
-        grad[0, :, at] = through_norm(b, unit_q, scale_q, gain_q[...]).astype(BF16)
+        gains[0] += jnp.sum((b * unit_q).reshape(-1, 8, d), axis=0)
+        grad[rows, at] = through_norm(b, unit_q, scale_q, gain_q[...]).astype(BF16)
     b = rot_back(key_grad, cos, sin)
-    gk = jnp.sum((b * unit_k).reshape(-1, 8, d), axis=0)
-    grad[0, :, groups * d : (groups + 1) * d] = through_norm(b, unit_k, scale_k, gain_k[...]).astype(BF16)
-    grad[0, :, (groups + 1) * d : (groups + 2) * d] = value_grad.astype(BF16)
-    gains[0, 0] = gq
-    gains[0, 1] = gk
-
-
-def per_sequence(*shape):
-    return pl.BlockSpec((1, *shape), lambda s: (s,) + (0,) * len(shape))
-
-
-def attention_specs(length, d):
-    return [
-        per_sequence(length, 1),
-        per_sequence(1, length),
-        per_sequence(length, d),
-        per_sequence(length, d),
-        pl.BlockSpec((1, d), lambda s: (0, 0)),
-        pl.BlockSpec((1, d), lambda s: (0, 0)),
-    ]
+    gains[1] += jnp.sum((b * unit_k).reshape(-1, 8, d), axis=0)
+    grad[rows, at_k] = through_norm(b, unit_k, scale_k, gain_k[...]).astype(BF16)
+    grad[rows, at_v] = value_grad.astype(BF16)
+
+
+def attend_back_kernel(
+    groups, qkv, att, datt, seg_col, seg_row, cos, sin, gain_q, gain_k, grad, gains
+):
+    gains[...] = jnp.zeros_like(gains)
+
+    @pl.loop(0, cos.shape[0])
+    def _(s):
+        attend_back_one(
+            groups, s, qkv, att, datt, seg_col, seg_row, cos, sin, gain_q, gain_k, grad, gains
+        )
 
 
 def attend_back(groups, qkv, att, datt, common):
-    n, length, width = qkv.shape
+    n_rows, width = qkv.shape
     d = width // (groups + 2)
+    length = n_rows // 2
     return pl.pallas_call(
         functools.partial(attend_back_kernel, groups),
-        grid=(n,),
-        out_shape=(
-            jax.ShapeDtypeStruct((n, length, width), BF16),
-            jax.ShapeDtypeStruct((n, 2, 8, d), F32),
-        ),
-        in_specs=[
-            per_sequence(length, width),
-            per_sequence(length, groups * d),
-            per_sequence(length, groups * d),
-            *attention_specs(length, d),
-        ],
-        out_specs=(per_sequence(length, width), per_sequence(2, 8, d)),
+        out_shape=(jax.ShapeDtypeStruct(qkv.shape, BF16), jax.ShapeDtypeStruct((2, 8, d), F32)),
         compiler_params=pltpu.CompilerParams(vmem_limit_bytes=40 << 20),
         cost_estimate=pl.CostEstimate(
-            flops=n * groups * length * length * (10 * d + 30),
-            bytes_accessed=n * length * width * 8,
-            transcendentals=n * groups * length * length * 2,
+            flops=n_rows * groups * length * (10 * d + 30),
+            bytes_accessed=n_rows * width * 8,
+            transcendentals=n_rows * groups * length * 2,
         ),
         name="attend_back",
     )(qkv, att, datt, *common)
@@ -599,6 +590,276 @@
     moves.close()
 
 
+class Scatter:
+    def __init__(self, moves, place, product, out0, in0, out1, in1, acc):
+        self.moves, self.place, self.product = moves, place, product
+        self.out0, self.in0, self.out1, self.in1, self.acc = out0, in0, out1, in1, acc
+        self.low, self.high = place.bits[1], place.bits[0]
+        self.order = [self.high, self.high | PAIR, 0, PAIR]
+        self.first, self.second = {}, {}
+
+    def send(self, i):
+        def emit(at, value):
+            self.out0[(i, *at)] = value.astype(BF16)
+
+        self.product(self.order[i] | self.low, emit)
+        self.first[i] = self.moves.swap(
+            self.out0.at[i], self.in0.at[i], self.in0.at[i], self.place.along(self.low)
+        )
+
+    def take(self, i):
+        self.first[i]()
+
+        def emit(at, value):
+            value = value + self.in0[(i, *at)].astype(F32)
+            if i < 2:
+                self.out1[(i, *at)] = value.astype(BF16)
+            else:
+                self.acc[(i - 2, *at)] = value
+
+        self.product(self.order[i], emit)
+        if i < 2:
+            self.second[i] = self.moves.swap(
+                self.out1.at[i], self.in1.at[i], self.in1.at[i], self.place.along(self.high)
+            )
+
+    def take_high(self, i):
+        self.second[i]()
+        rows = self.acc.shape[1]
+        step = 64
+
+        @pl.loop(0, rows // step)
+        def _(k):
+            at = pl.ds(pl.multiple_of(k * step, step), step)
+            self.acc[i, at] += self.in1[i, at].astype(F32)
+
+
+class Blocks:
+    def __init__(self, moves, place, slots, order):
+        self.moves, self.place, self.slots, self.order = moves, place, slots, order
+        self.next, self.waits = 0, {}
+        self.start(0)
+
+    def start(self, k):
+        if k < len(self.order):
+            ref, mask = self.order[k]
+            size = self.slots.shape[2]
+            at = pl.ds(pl.multiple_of(self.place.block(mask) * size, size), size)
+            self.waits[k] = self.moves.load(ref.at[:, at], self.slots.at[k % 2])
+
+    def get(self, ref, mask):
+        k = self.next
+        assert self.order[k][0] is ref and self.order[k][1] == mask
+        self.next += 1
+        self.waits.pop(k)()
+        self.start(k + 1)
+        return self.slots[k % 2]
+
+
+def backward_kernel(
+    bits, groups,
+    mid, hidden, cot, gain_attn, gain_mlp, seg_col, seg_row, cos, sin, gain_q, gain_k,
+    part_two, normed_one, normed_two, cot_rows, qkv_in, att_in, qkv_weight, out_weight, grad_gate, grad_up, mixed_t,
+    grad_in, gains, feed_own, feed_other, down_own, down_other, qkv_own, qkv_other, out_own, out_other,
+    own, rows_mid, feed, mixed, lhs, lhs_t, part, w_qkv, w_out, qkv, att, datt, dqkv,
+    first, ctx_in, pair_in, sending, gain_a, gain_m, gain_h, tree, tree_in,
+    f_out0, f_in0, f_out1, f_in1, f_acc, d_out0, d_in0, d_out1, d_in1, d_acc,
+    q_out0, q_in0, q_out1, q_in1, q_acc, o_out0, o_in0, o_out1, o_in1, o_acc,
+    send, recv, local,
+):
+    place = Place(bits)
+    moves = Moves(send, recv, local)
+    rows, width = hidden.shape
+    cols = mixed.shape[0]
+    tile = lhs.shape[2]
+    half = tile // 2
+    high, low = bits
+    place.greet()
+
+    def lanes(start, size):
+        return pl.ds(pl.multiple_of(start, size), size)
+
+    ready_feed = [
+        moves.load(grad_gate, feed.at[:, pl.ds(0, cols)]),
+        moves.load(grad_up, feed.at[:, pl.ds(cols, cols)]),
+    ]
+    collect_two = Collect(
+        moves, place, lambda j, t: part_two.at[place.rows_of[j] + t], part, first, ctx_in, pair_in, sending, True
+    )
+    masks = [high, high | PAIR, 0, PAIR]
+    sends = [m | low for m in masks]
+    order = (
+        [(normed_two, m) for m in [*sends, masks[0], masks[1]]]
+        + [(cot_rows, m) for m in sends]
+        + [(normed_one, m) for m in sends]
+        + [(normed_two, m) for m in masks[2:]]
+        + [(cot_rows, m) for m in masks]
+        + [(normed_one, m) for m in masks]
+    )
+    blocks = Blocks(moves, place, lhs, order)
+    ready_mixed = moves.load(mixed_t, mixed)
+    ready_late = [
+        moves.load(out_weight, w_out),
+        moves.load(att_in, att),
+        moves.load(qkv_in, qkv),
+        moves.load(qkv_weight, w_qkv),
+    ]
+
+    def by_rows(source, right):
+        def product(mask, emit):
+            lhs_t[...] = blocks.get(source, mask).T
+            step = min(512, right.shape[1])
+
+            @pl.loop(0, right.shape[1] // step)
+            def _(i):
+                at = lanes(i * step, step)
+                emit((slice(None), at), dot(lhs_t[...], right[:, at]))
+
+        return product
+
+    def down_product(mask, emit):
+        block = blocks.get(cot_rows, mask)
+        step = min(256, cols)
+
+        @pl.loop(0, cols // step)
+        def _(i):
+            at = lanes(i * step, step)
+            emit((at, slice(None)), dot(mixed[at], block))
+
+    def out_product(mask, emit):
+        at = lanes(place.block(mask) * tile, tile)
+        emit((slice(None), slice(None)), dot_rows(att[...], rows_mid[:, at]))
+
+    feed_s = Scatter(moves, place, by_rows(normed_two, feed), f_out0, f_in0, f_out1, f_in1, f_acc)
+    down_s = Scatter(moves, place, down_product, d_out0, d_in0, d_out1, d_in1, d_acc)
+    qkv_s = Scatter(moves, place, by_rows(normed_one, dqkv), q_out0, q_in0, q_out1, q_in1, q_acc)
+    out_s = Scatter(moves, place, out_product, o_out0, o_in0, o_out1, o_in1, o_acc)
+
+    for wait in ready_feed:
+        wait()
+    feed_s.send(0)
+    collect_two.to_ctx()
+    feed_s.send(1)
+    feed_s.send(2)
+    collect_two.to_pair()
+    feed_s.send(3)
+    feed_s.take(0)
+    collect_two.finish()
+    gain_m[...] = jnp.zeros_like(gain_m)
+    gain_a[...] = jnp.zeros_like(gain_a)
+    gain_h[...] = jnp.zeros_like(gain_h)
+
+    def back_two(at):
+        g = cot[at].astype(F32) + norm_back(collect_two.total(at), mid[at], gain_mlp[...], gain_m)
+        grad_in[at] = g
+        own[at] = g.astype(BF16)
+
+    row_loop(rows, back_two)
+    spread = Spread(moves, place, own, rows_mid)
+    feed_s.take(1)
+    spread.from_pair()
+    ready_mixed()
+    down_s.send(0)
+    down_s.send(1)
+    spread.from_ctx()
+    spread.from_both()
+    down_s.send(2)
+    down_s.send(3)
+    for wait in ready_late:
+        wait()
+    spread.finish()
+
+    @pl.loop(0, 8 // 2)
+    def _(i):
+        at = lanes(i * 2 * rows, 2 * rows)
+        datt[at] = dot_cols(rows_mid[at], w_out[...]).astype(BF16)
+
+    @pl.loop(0, cos.shape[0])
+    def _(s):
+        attend_back_one(
+            groups, s, qkv, att, datt, seg_col, seg_row, cos, sin, gain_q, gain_k, dqkv, gain_h
+        )
+
+    @pl.loop(0, 8)
+    def _(i):
+        part[i] = dot_cols(dqkv[lanes(i * rows, rows)], w_qkv[...]).astype(BF16)
+
+    collect_one = Collect(
+        moves, place, lambda j, t: part.at[place.rows_of[j] + t], None, first, ctx_in, pair_in, sending, False
+    )
+    for i in range(4):
+        out_s.send(i)
+    collect_one.to_ctx()
+    for i in range(4):
+        qkv_s.send(i)
+    collect_one.to_pair()
+    feed_s.take(2)
+    feed_s.take(3)
+    down_s.take(0)
+    down_s.take(1)
+    collect_one.finish()
+
+    def back_one(at):
+        grad_in[at] += norm_back(collect_one.total(at), hidden[at].astype(F32), gain_attn[...], gain_a)
+
+    row_loop(rows, back_one)
+
+    d = gain_q.shape[1]
+    tree[0, :, 0:width] = jnp.sum(gain_a[...], axis=0, keepdims=True)
+    tree[0, :, width : 2 * width] = jnp.sum(gain_m[...], axis=0, keepdims=True)
+    tree[0, :, 2 * width : 2 * width + d] = jnp.sum(gain_h[0], axis=0, keepdims=True)
+    tree[0, :, 2 * width + d : 2 * width + 2 * d] = jnp.sum(gain_h[1], axis=0, keepdims=True)
+    for k, device in enumerate([place.sibling, place.chips[1], place.chips[2], *[place.along(b) for b in bits]]):
+        moves.swap(tree.at[k], tree_in.at[k], tree_in.at[k], device)()
+        tree[k + 1] = tree[k] + tree_in[k]
+    gains[...] = tree[3 + len(bits)]
+
+    finals = []
+
+    def feed_final(scatter, mine, other):
+        scatter.take_high(1)
+        pair_out = scatter.in0.at[0]
+        n, step = pair_out.shape[0], 64
+
+        @pl.loop(0, n // step)
+        def _(k):
+            at = lanes(k * step, step)
+            pair_out[at] = scatter.acc[1, at].astype(BF16)
+
+        finals.append(moves.swap(pair_out, other, other, place.chips[2]))
+        scatter.take_high(0)
+        moves.store(scatter.acc.at[0], mine)
+
+    def mates_final(scatter, piece, spare, mine, other):
+        scatter.take_high(1)
+        scatter.take_high(0)
+        for j in (3, 2, 1):
+            out = spare(j)
+            out[...] = piece(j // 2, place.at[j][1]).astype(BF16)
+            finals.append(moves.swap(out, other.at[j - 1], other.at[j - 1], place.chips[j]))
+        mine[...] = piece(0, place.c)
+
+    feed_final(feed_s, feed_own, feed_other)
+    down_s.take(2)
+    down_s.take(3)
+    for i in range(4):
+        out_s.take(i)
+    for i in range(4):
+        qkv_s.take(i)
+    feed_final(down_s, down_own, down_other)
+    mates_final(
+        out_s, lambda slot, c: o_acc[slot, :, lanes(c * half, half)],
+        lambda j: o_in0.at[j, :, pl.ds(0, half)], out_own, out_other,
+    )
+    mates_final(
+        qkv_s, lambda slot, c: q_acc[slot, lanes(c * half, half)],
+        lambda j: q_in0.at[j, pl.ds(0, half)], qkv_own, qkv_other,
+    )
+    for wait in finals:
+        wait()
+    moves.close()
+
+
 VMEM_SPEC = pl.BlockSpec(memory_space=pltpu.VMEM)
 ANY_SPEC = pl.BlockSpec(memory_space=pl.ANY)
 
@@ -613,10 +874,10 @@
             *scratch,
             pltpu.SemaphoreType.DMA((copies,)),
             pltpu.SemaphoreType.DMA((copies,)),
-            pltpu.SemaphoreType.DMA((40,)),
+            pltpu.SemaphoreType.DMA((80,)),
         ],
         compiler_params=pltpu.CompilerParams(
-            collective_id=collective_id, has_side_effects=True, vmem_limit_bytes=56 << 20
+            collective_id=collective_id, has_side_effects=True, vmem_limit_bytes=61 << 20
         ),
         cost_estimate=pl.CostEstimate(flops=nbytes * 20, bytes_accessed=nbytes, transcendentals=0),
         name=kernel.__name__,
@@ -730,8 +991,6 @@
              *collect_buffers(rows, width)],
             16 * nbytes, copies, groups, natural,
         )
-        qkv3 = qkv.reshape(2, length, qkv_cols)
-        attended3 = attended.reshape(2, length, q_cols)
         teams = sorted(
             sorted(i ^ b ^ p for b in range(4) for p in (0, PAIR_BIT))
             for i in range(0, n, 4)
@@ -747,17 +1006,120 @@
         grad_gate = (grad_mixed * up_pre * gate_sig * (1.0 + gate_pre * (1.0 - gate_sig))).astype(BF16)
         grad_up = (grad_mixed * gate_act).astype(BF16)
         norm_two_part = (dot_cols(grad_gate, full_gate) + dot_cols(grad_up, full_up)).astype(BF16)
+        down_part = times(mixed, full_down).astype(BF16)
+        hidden_out = residual_mid + lax.psum_scatter(
+            down_part, AXES, scatter_dimension=0, axis_index_groups=teams, tiled=True
+        ).astype(F32)
+        backward = one_kernel if natural and len(spread_bits) == 2 else by_steps
+        return hidden_out, *backward(
+            hidden_in, cotangent, residual_mid, gain_attn, gain_mlp, common, norm_two_part, normed_one, normed_two,
+            grad_rows, qkv, attended, full_qkv, full_out, grad_gate, grad_up, mixed, (at_rows, ff_rows),
+        )
+
+    def one_kernel(
+        hidden_in, cotangent, residual_mid, gain_attn, gain_mlp, common, norm_two_part, normed_one, normed_two,
+        grad_rows, qkv, attended, full_qkv, full_out, grad_gate, grad_up, mixed, sizes,
+    ):
+        rows, width = hidden_in.shape
+        n_rows, cols = mixed.shape
+        (at_rows, ff_rows), q_cols, qkv_cols = sizes, attended.shape[1], qkv.shape[1]
+        d = common[-1].shape[1]
+        kv_cols = (qkv_cols - q_cols) // 2
+        groups = q_cols // kv_cols
+
+        def out(dtype, *dims):
+            return jax.ShapeDtypeStruct(dims, dtype)
+
+        def v(*dims, dtype=BF16):
+            return pltpu.VMEM(dims, dtype)
+
+        def scatter(*block):
+            return [v(4, *block), v(4, *block), v(2, *block), v(2, *block), v(2, *block, dtype=F32)]
+
+        n_gain = 2 * width + 2 * d
+        nbytes = n_rows * width * 20
+        (
+            grad_input, gains, feed_own, feed_other, down_own, down_other, qkv_own, qkv_other, out_own, out_other,
+        ) = comm_call(
+            backward_kernel, spread_bits, 2,
+            (residual_mid, hidden_in, cotangent, gain_attn[None], gain_mlp[None], *common,
+             norm_two_part.reshape(8, rows, width), normed_one, normed_two, grad_rows, qkv, attended, full_qkv,
+             full_out, grad_gate, grad_up, mixed.T),
+            [VMEM_SPEC] * 11 + [ANY_SPEC] * 11,
+            (out(F32, rows, width), out(F32, 1, n_gain), out(F32, ff_rows, 2 * cols), out(BF16, ff_rows, 2 * cols),
+             out(F32, cols, ff_rows), out(BF16, cols, ff_rows), out(F32, at_rows, qkv_cols),
+             out(BF16, 3, at_rows, qkv_cols), out(F32, q_cols, at_rows), out(BF16, 3, q_cols, at_rows)),
+            (VMEM_SPEC, VMEM_SPEC, ANY_SPEC, ANY_SPEC, ANY_SPEC, ANY_SPEC, VMEM_SPEC, ANY_SPEC, VMEM_SPEC, ANY_SPEC),
+            [v(rows, width), v(n_rows, width), v(n_rows, 2 * cols), v(cols, n_rows), v(2, n_rows, ff_rows),
+             v(ff_rows, n_rows), v(8, rows, width), v(width, qkv_cols), v(q_cols, width), v(n_rows, qkv_cols),
+             v(n_rows, q_cols), v(n_rows, q_cols), v(n_rows, qkv_cols),
+             *collect_buffers(rows, width), v(8, width, dtype=F32), v(8, width, dtype=F32), v(2, 8, d, dtype=F32),
+             v(4 + len(spread_bits), 1, n_gain, dtype=F32), v(3 + len(spread_bits), 1, n_gain, dtype=F32),
+             *scatter(ff_rows, 2 * cols), *scatter(cols, ff_rows), *scatter(ff_rows, qkv_cols),
+             *scatter(q_cols, ff_rows)],
+            nbytes, 80, groups,
+        )
+        pair = bit_of(lax.axis_index("fsdp"), PAIR)
+        c = lax.axis_index("ctx")
+
+        def feed(mine, other, axis):
+            return in_order(pair, mine, other.astype(F32), axis)
+
+        def heads(mine, other, axis):
+            other = other.astype(F32)
+            near = in_order(pair, mine, other[1], axis)
+            far = in_order(pair, other[0], other[2], axis)
+            return in_order(c, near, far, axis)
+
+        grad_w_gate = feed(feed_own[:, :cols], feed_other[:, :cols], 1).reshape(ff_rows, 2 * cols)
+        grad_w_up = feed(feed_own[:, cols:], feed_other[:, cols:], 1).reshape(ff_rows, 2 * cols)
+        grad_w_down = feed(down_own, down_other, 0).reshape(2 * cols, ff_rows)
+        grad_w_out = heads(out_own, out_other, 0).reshape(4 * q_cols, at_rows)
+
+        def columns(start, size):
+            at = slice(start, start + size)
+            return heads(qkv_own[:, at], qkv_other[:, :, at], 1).reshape(at_rows, 4 * size)
+
+        gains = gains[0]
+        return (
+            grad_input,
+            columns(0, q_cols),
+            columns(q_cols, kv_cols),
+            columns(q_cols + kv_cols, kv_cols),
+            grad_w_out,
+            grad_w_gate,
+            grad_w_up,
+            grad_w_down,
+            gains[:width],
+            gains[width : 2 * width],
+            gains[2 * width : 2 * width + d],
+            gains[2 * width + d :],
+        )
+
+    def by_steps(
+        hidden_in, cotangent, residual_mid, gain_attn, gain_mlp, common, norm_two_part, normed_one, normed_two,
+        grad_rows, qkv, attended, full_qkv, full_out, grad_gate, grad_up, mixed, sizes,
+    ):
+        rows, width = hidden_in.shape
+        (at_rows, ff_rows), ff_cols, q_cols = sizes, mixed.shape[1], attended.shape[1]
+        d = common[-1].shape[1]
+        kv_cols = (qkv.shape[1] - q_cols) // 2
+        groups = q_cols // kv_cols
+        natural = full_out.shape[0] != width
+        times_t = dot_cols if natural else dot
+        f, c = lax.axis_index("fsdp"), lax.axis_index("ctx")
+        pair = bit_of(f, PAIR)
+        all_rows = jax.ShapeDtypeStruct((8 * rows, width), BF16)
+        own_rows = jax.ShapeDtypeStruct((rows, width), F32)
+        gain_rows = jax.ShapeDtypeStruct((8, width), F32)
+        block = pltpu.VMEM((rows, width), BF16)
+        nbytes = rows * width * 16
         grad_mid, gain_mlp_part, grad_mid_rows = comm_call(
             turn_kernel, spread_bits, 2, (norm_two_part.reshape(8, rows, width), residual_mid, cotangent, gain_mlp[None]),
             [ANY_SPEC, VMEM_SPEC, VMEM_SPEC, VMEM_SPEC], (own_rows, gain_rows, all_rows),
             (VMEM_SPEC, VMEM_SPEC, ANY_SPEC),
             [block, pltpu.VMEM((4, rows, width), BF16), *collect_buffers(rows, width)], 2 * nbytes, 40,
         )
-
-        down_part = times(mixed, full_down).astype(BF16)
-        hidden_out = residual_mid + lax.psum_scatter(
-            down_part, AXES, scatter_dimension=0, axis_index_groups=teams, tiled=True
-        ).astype(F32)
 
         low = bit_of(f, 1)
 
@@ -790,9 +1152,8 @@
 
         grad_w_out = attn_grad(grad_mid_rows, attended).reshape(at_rows, 4 * q_cols).T
 
-        datt = times_t(grad_mid_rows, full_out).astype(BF16).reshape(attended3.shape)
-        grad_qkv, head_gains = attend_back(groups, qkv3, attended3, datt, common)
-        grad_qkv = grad_qkv.reshape(8 * rows, -1)
+        datt = times_t(grad_mid_rows, full_out).astype(BF16)
+        grad_qkv, head_gains = attend_back(groups, qkv, attended, datt, common)
         norm_one_part = dot_cols(grad_qkv, full_qkv).astype(BF16)
         grad_input, gain_attn_part = comm_call(
             last_kernel, spread_bits, 3, (norm_one_part.reshape(8, rows, width), hidden_in, grad_mid, gain_attn[None]),
@@ -804,7 +1165,7 @@
         grad_w_key = grad_qkv_w[..., q_cols : q_cols + kv_cols].reshape(at_rows, -1)
         grad_w_value = grad_qkv_w[..., q_cols + kv_cols :].reshape(at_rows, -1)
 
-        head_gains = jnp.sum(head_gains, axis=(0, 2))
+        head_gains = jnp.sum(head_gains, axis=1)
         gains = jnp.concatenate(
             [jnp.sum(gain_attn_part, axis=0), jnp.sum(gain_mlp_part, axis=0), head_gains[0], head_gains[1]]
         ).reshape(-1, d)
@@ -812,7 +1173,6 @@
             gains = gains + swap(gains, 1 << i)
         gains = gains.reshape(-1)
         return (
-            hidden_out,
             grad_input,
             grad_w_query,
             grad_w_key,

time: 773 us -> 524 us (0.68)
  local copies, waits for them, and re-layouts: 177 us -> 20.6 us
  waiting for transfers between devices: 129 us -> 1.78 us
  Pallas kernels: 322 us -> 426 us
  matrix products: 78.9 us -> 30.7 us
  starting transfers between devices: 29 us -> 3.13 us
    ppermute x25 -> x1, waiting for transfers between devices: 129 us -> 1.77 us  [swap(): return lax.ppermute(v, AXES, [(i, i ^ bit) for i in range(n)])]
    pallas_call x3 -> x2, Pallas kernels: 314 us -> 426 us  [comm_call(): pl.pallas_call(functools.partial(kernel, bits, *more), out_shape=outs, in...]
    unnamed x80 -> x44, local copies, waits for them, and re-layouts: 88.6 us -> 9.2 us
    dynamic_slice x7 -> x0, local copies, waits for them, and re-layouts: 43.6 us -> none  [pick(): return lax.dynamic_index_in_dim(v, index, axis, keepdims=False)]
    reshape x9 -> x0, local copies, waits for them, and re-layouts: 37.6 us -> none  [the longest x4 31.9 us: weight_grad(): split = acts.reshape(acts.shape[0], n_f // 2, 2, width // n_f)]
    dot_general x10 -> x0, matrix products: 30.7 us -> none  [dot_rows(): lax.dot_general(left, right, (((0,), (0,)), ((), ())), preferred_element_...]
    ppermute x25 -> x1, starting transfers between devices: 29 us -> 3.09 us  [swap(): return lax.ppermute(v, AXES, [(i, i ^ bit) for i in range(n)])]
    dot_general x5 -> x3, matrix products: 30.8 us -> 16 us  [dot_cols(): lax.dot_general(left, right, (((1,), (1,)), ((), ())), preferred_element_...]
  transfers between devices with their start and end apart: 26 -> 2, of which waited for: 10 -> 1; matrix products, arithmetic and copies ran while one was open for 28% -> 9% of each run, Pallas kernels for 15% -> 43%
where the time goes in v3:
time: 524 us; the launch traced here: 517 us
  Pallas kernels  426 us (81%)
  matrix products  30.7 us (6%)
  local copies, waits for them, and re-layouts  20.6 us (4%)
  other arithmetic  20.4 us (4%)
  between operations  14.7 us (3%)
    pallas_call x2, Pallas kernels, comm_call(): pl.pallas_call(functools.partial(kernel, bits, *more), out_shape=outs, in...  426 us
    dot_general x3, matrix products, dot_cols(): lax.dot_general(left, right, (((1,), (1,)), ((), ())), preferred_element_...  16 us
    dot_general x3, matrix products, dot(): lax.dot_general(left, right, (((1,), (0,)), ((), ())), preferred_element_...  14.7 us
  transfers between devices with their start and end apart: 2, of which 1 were waited for; matrix products, arithmetic and copies ran while one was open for 9% of the time, Pallas kernels for 43%

profile of v3, /device:TPU:0, one launch (start us, length us, event | category | flops | bytes accessed | tf_op | source)
XLA Modules:
  0.0 517.1 jit_solution(7758430664313168629)
XLA Ops:
  7.2 0.0 reduce-scatter.2.cloned.1.call-start
  7.2 3.1 collective-permute-start
  10.3 1.8 collective-permute-done
  12.1 0.7 broadcast_select_fusion.1
  12.8 0.6 broadcast_in_dim.28.seg_row
  13.4 0.4 convert_reduce_fusion
  13.8 1.0 copy.45.seg_col
  14.8 1.9 fusion.16
  16.7 1.0 pad_maximum_fusion.3.cos
  17.7 1.0 pad_maximum_fusion.4.sin
  18.7 205.2 %forward_kernel.1 = (f32[128,2048]{1,0:T(8,128)}, bf16[1024,2048]{1,0:T(8,128)(2,1)}, bf16[1024,2048]{1,0:T(8,128)(2,1)}, bf16[1024,2048]{1,0:T(8,128)(2,1)}, bf...) custom-call(bf16[128,2048]{1,0:T(8,128)(2,1)} %hidden.3, ...), custom_call_target="tpu_custom_call" | custom-call | flops 1342177280 | bytes 67108864 | tf_op jit(solution)/shard_map/forward_kernel/pallas_call | solution.py:868
  223.9 0.0 copy-start.1
  223.9 0.0 copy-start.15
  224.0 6.3 %fusion.24 = f32[1024,768]{1,0:T(8,128)S(1)} fusion(bf16[1024,2048]{1,0:T(8,128)(2,1)} %get-tuple-element.35.normed_two, bf16[2048,768]{1,0:T(8,128)(2,1)} %get-tuple-element.36), kind=kOutput, calls=%fused_computation.89 | convolution fusion | flops 3221225472 | bytes 10485760 | tf_op jit(solution)/shard_map/dot_general | solution.py:30
  230.2 0.0 copy-start.3
  230.3 0.0 copy-done.1
  230.3 0.0 copy-done.15
  230.3 0.0 copy-start.18
  230.3 3.4 fusion.25
  233.7 0.0 copy-start.5
  233.7 0.0 copy-done.3
  233.7 1.7 copy-done.5
  235.4 0.0 copy-done.18
  235.4 5.0 convolution_convert_fusion
  240.4 0.0 reduce-scatter.2.cloned.1.call-update
  240.5 2.4 copy.47
  242.8 3.5 copy.46
  246.4 4.2 fusion.mixed_t
  250.5 0.0 copy-done.2
  250.5 0.1 copy-done.4
  250.7 7.3 %multiply_convert_fusion = (bf16[1024,768]{1,0:T(8,128)(2,1)S(1)}, bf16[1024,768]{1,0:T(8,128)(2,1)S(1)}) fusion(f32[1024,768]{1,0:T(8,128)S(1)} %copy-done.4, f32[1024,768]{1,0:T(8,128)} %copy-done.5, bf16[1024,2048]{1,0:T(8,128)(2,1)S(1)} %copy-done.2, bf16[768,2048]{1,0:T(8,128)(2,1)} %get-tuple-element.38), kind=kOutput, calls=%fused_computation.9 | convolution fusion | flops 3231449088 | bytes 16777216 | tf_op jit(solution)/shard_map/dot_general | solution.py:26
  258.0 0.0 copy-start.7
  258.0 0.0 copy-start.6
  258.0 0.0 copy-done.17
  258.0 0.0 copy-start.16
  258.1 3.4 fusion.26
  261.5 5.2 add_convert_fusion
  266.7 220.6 %backward_kernel.1 = (f32[128,2048]{1,0:T(8,128)}, f32[1,4352]{1,0:T(1,128)}, f32[256,1536]{1,0:T(8,128)}, bf16[256,1536]{1,0:T(8,128)(2,1)}, f32[768,256]{1,0:T...) custom-call(f32[128,2048]{1,0:T(8,128)} %get-tuple-element.34.mid, ...), custom_call_target="tpu_custom_call" | custom-call | flops 838860800 | bytes 41943040 | tf_op jit(solution)/shard_map/backward_kernel/pallas_call | solution.py:868
  487.3 1.0 convert_element_type.64
  488.3 1.0 slice_convert_fusion.1
  489.3 0.9 select_bitcast_fusion.11
  490.3 0.1 copy.51
  490.4 0.8 copy.56
  491.3 0.1 copy.50
  491.4 0.8 copy.55
  492.3 0.9 select_bitcast_fusion.7
  493.3 0.2 copy.49
  493.5 1.0 copy.54
  494.6 1.4 fusion.7
  495.9 1.4 pad_maximum_fusion
  497.4 1.9 copy.52
  499.2 1.6 copy.57
  500.9 0.5 copy.53
  501.3 1.6 copy.58
  503.1 0.8 pad_maximum_fusion.6
  503.9 0.4 copy-done.10
  504.3 0.1 copy-done.12
  504.4 0.1 fusion.9
  504.5 0.0 copy-start.9
  504.5 1.2 pad_maximum_fusion.2
  505.8 0.5 slice_bitcast_fusion.4
  506.3 0.6 fusion.23
  506.9 2.1 convert_add_fusion
  509.0 1.0 copy.60
  (35 shorter events, 0.4 us)
Async XLA Ops:
  7.2 499.7 %reduce-scatter.2.cloned.1.call-start = ((), (), s32[]{:S(2)}) async-start(), calls=%async_computation.1 | async-start | bytes 4718592 | tf_op jit(solution)/shard_map/reduce_scatter | solution.py:1010
  7.2 4.9 collective-permute-start
  223.9 6.3 %copy-start.1 = (bf16[1024,2048]{1,0:T(8,128)(2,1)S(1)}, bf16[1024,2048]{1,0:T(8,128)(2,1)}, u32[]{:S(2)}) copy-start(bf16[1024,2048]{1,0:T(8,128)(2,1)} %get-tuple-element.35.normed_two) | copy-start | bytes 12582916
  223.9 6.3 %copy-start.15 = (bf16[2048,768]{1,0:T(8,128)(2,1)S(1)}, bf16[2048,768]{1,0:T(8,128)(2,1)}, u32[]{:S(2)}) copy-start(bf16[2048,768]{1,0:T(8,128)(2,1)} %get-tuple-element.37) | copy-start | bytes 9437188
  230.2 3.5 copy-start.3
  230.3 5.1 copy-start.18
  233.7 1.7 copy-start.5
  246.4 4.2 copy-start.2
  246.4 4.3 copy-start.4
  250.7 7.4 %copy-start.17 = (bf16[2048,768]{1,0:T(8,128)(2,1)S(1)}, bf16[2048,768]{1,0:T(8,128)(2,1)}, u32[]{:S(2)}) copy-start(bf16[2048,768]{1,0:T(8,128)(2,1)} %get-tuple-element.36) | copy-start | bytes 9437188
  258.0 3.5 copy-start.7
  258.0 3.5 copy-start.6
  258.0 3.5 copy-start.16
  487.3 5.0 copy-start.11
  491.4 3.1 copy-start.8
  501.3 1.7 copy-start.13
  503.0 1.3 copy-start.10
  503.0 1.4 copy-start.12
  503.9 1.9 copy-start.14
  503.9 3.0 copy-start
  504.5 4.5 copy-start.9
Sparse Core Ops, SparseCore 0:
  240.6 70.9 reduce-scatter.1

commit v4 on v3

--- a/solution.py
+++ b/solution.py
@@ -77,6 +77,9 @@
         self.at = [(fs[j], cs[j], pairs[j]) for j in range(4)]
         self.rows_of = [pairs[j] * 4 + cs[j] * 2 for j in range(4)]
         self.chunk_of = [cs[j] * 2 + pairs[j] for j in range(4)]
+        self.relay = len(bits) == 2
+        self.across_mask = bits[0] | PAIR
+        self.inner = (f // bits[0]) % 2 != self.pair
         self.chips = [None, {"ctx": 1 - c}, {"fsdp": far_f}, {"fsdp": far_f, "ctx": 1 - c}]
         self.sibling = {"tp": 1 - t}
 
@@ -94,20 +97,79 @@
     def greet(self):
         barrier = pltpu.get_barrier_semaphore()
         devices = [*self.chips[1:], self.sibling, *[self.along(b) for b in self.bits]]
+        if self.relay:
+            devices.append(self.along(self.across_mask))
         for device in devices:
             pl.semaphore_signal(barrier, inc=1, device_id=device, device_id_type=MESH)
         pl.semaphore_wait(barrier, len(devices))
+
+
+class Cross:
+    def __init__(self, moves, place, src, here, came_in, across_to, came_out, pair_to):
+        self.place, self.here = place, here
+        self.came_in, self.came_out = came_in, came_out
+        k = moves.sent
+        moves.sent += 4
+        pair, across = place.chips[2], place.along(place.across_mask)
+
+        def copy(i, source, to, device):
+            return remote(source, to, moves.send.at[k + i], moves.recv.at[k + i], device)
+
+        self.hand = copy(0, src, came_in, pair)
+        self.own = copy(1, src, came_out, across)
+        self.on = copy(2, came_in, across_to, across)
+        self.back = copy(3, came_out, pair_to, pair)
+        self.came = [copy(0, came_in, came_in, pair), copy(1, came_out, came_out, across)]
+        self.landed = [copy(2, here, here, across), copy(3, here, here, pair)]
+        moves.open.append(self.left)
+
+        @pl.when(place.inner)
+        def _():
+            self.own.start()
+
+        @pl.when(jnp.logical_not(place.inner))
+        def _():
+            self.hand.start()
+
+    def relay(self):
+        @pl.when(self.place.inner)
+        def _():
+            self.came[0].wait_recv()
+            self.on.start()
+            self.came[1].wait_recv()
+            self.back.start()
+
+    def arrive(self):
+        @pl.when(self.place.inner)
+        def _():
+            self.landed[0].wait_recv()
+
+        @pl.when(jnp.logical_not(self.place.inner))
+        def _():
+            self.landed[1].wait_recv()
+
+    def left(self):
+        @pl.when(self.place.inner)
+        def _():
+            self.own.wait_send()
+            self.on.wait_send()
+            self.back.wait_send()
+
+        @pl.when(jnp.logical_not(self.place.inner))
+        def _():
+            self.hand.wait_send()
 
 
 class Spread:
     def __init__(self, moves, place, own, out):
         self.moves, self.place, self.out = moves, place, out
         self.rows = own.shape[0]
+        self.open = []
         mine = self.at(0, place.t)
         self.here = moves.load(own, mine)
-        self.pair = moves.swap(own, mine, self.at(2, place.t), place.chips[2])
-        self.ctx = moves.swap(own, mine, self.at(1, place.t), place.chips[1])
-        self.beside = [moves.swap(own, mine, self.at(0, 1 - place.t), place.sibling)]
+        self.pair = moves.swap(own, mine, self.at(2, place.t), place.chips[2], self.open)
+        self.ctx = moves.swap(own, mine, self.at(1, place.t), place.chips[1], self.open)
+        self.beside = [moves.swap(own, mine, self.at(0, 1 - place.t), place.sibling, self.open)]
 
     def at(self, j, t):
         start = (self.place.rows_of[j] + t) * self.rows
@@ -116,13 +178,13 @@
     def hand(self, j):
         block = self.at(j, self.place.t)
         self.beside.append(
-            self.moves.swap(block, block, self.at(j, 1 - self.place.t), self.place.sibling)
+            self.moves.swap(block, block, self.at(j, 1 - self.place.t), self.place.sibling, self.open)
         )
 
     def from_pair(self):
         self.pair()
         block = self.at(2, self.place.t)
-        self.both = self.moves.swap(block, block, self.at(3, self.place.t), self.place.chips[1])
+        self.both = self.moves.swap(block, block, self.at(3, self.place.t), self.place.chips[1], self.open)
         self.hand(2)
 
     def from_ctx(self):
@@ -135,7 +197,7 @@
 
     def finish(self):
         self.here()
-        for wait in self.beside:
+        for wait in (*self.beside, *self.open):
             wait()
 
 
@@ -218,14 +280,24 @@
 
 
 class Gather:
-    def __init__(self, moves, place, block):
-        self.moves, self.place, self.block = moves, place, block
-        self.waits = {}
+    def __init__(self, moves, place, block, spare):
+        self.moves, self.place, self.block, self.spare = moves, place, block, spare
+        self.waits, self.crosses = {}, {}
 
     def forward(self, mask, src=None):
         done = [i for i, b in enumerate(self.place.bits) if mask & b]
         here = self.block(self.place.block(mask))
         for b in self.place.bits[max(done, default=-1) + 1 :]:
+            if self.place.relay and b == self.place.bits[0]:
+                far = self.place.across_mask
+                slot = 0 if mask == 0 else 2
+                self.crosses[mask] = Cross(
+                    self.moves, self.place, here if src is None else src, self.block(self.place.block(mask | b)),
+                    self.spare.at[slot], self.block(self.place.block(mask ^ PAIR)),
+                    self.spare.at[slot + 1], self.block(self.place.block(mask ^ far)),
+                )
+                self.waits[mask | b] = self.crosses[mask].arrive
+                continue
             self.waits[mask | b] = self.moves.swap(
                 here if src is None else src, here, self.block(self.place.block(mask | b)), self.place.along(b)
             )
@@ -236,11 +308,20 @@
             out += [m | b for m in out]
         return [m | self.place.bits[stage] for m in out]
 
+    def relay(self):
+        for m in list(self.crosses):
+            self.crosses.pop(m).relay()
+
+    def pass_on(self, m):
+        self.waits.pop(m)()
+        self.forward(m)
+
     def middle(self):
+        self.relay()
         for stage in range(len(self.place.bits) - 1):
             for m in self.masks(stage):
-                self.waits.pop(m)()
-                self.forward(m)
+                if m in self.waits:
+                    self.pass_on(m)
 
     def finish(self):
         for wait in self.waits.values():
@@ -260,11 +341,11 @@
     return b * cos - pltpu.roll(b, b.shape[-1] // 2, 1) * sin
 
 
-def allowed_keys(seg_col, seg_row):
-    length = seg_col.shape[0]
+def allowed_keys(start):
+    length = start.shape[0]
     row = lax.broadcasted_iota(jnp.int32, (length, length), 0)
     col = lax.broadcasted_iota(jnp.int32, (length, length), 1)
-    return (seg_col == seg_row) & (row >= col)
+    return (col.astype(F32) >= start) & (row >= col)
 
 
 def soft_of(scores):
@@ -273,12 +354,12 @@
     return jnp.exp(scores - lse)
 
 
-def attend_one(groups, s, qkv, seg_col, seg_row, cos_ref, sin_ref, gain_q, gain_k, out):
+def attend_one(groups, s, qkv, starts, cos_ref, sin_ref, gain_q, gain_k, out):
     d = gain_q.shape[-1]
-    length = cos_ref.shape[1]
+    length = cos_ref.shape[0] // 2
     rows = pl.ds(pl.multiple_of(s * length, length), length)
-    cos, sin = cos_ref[s], sin_ref[s]
-    allowed = allowed_keys(seg_col[s], seg_row[s])
+    cos, sin = cos_ref[rows], sin_ref[rows]
+    allowed = allowed_keys(starts[rows, 0:1])
     unit_k, _ = head_unit(qkv[rows, groups * d : (groups + 1) * d].astype(F32))
     key = rot(unit_k * gain_k[...], cos, sin).astype(BF16)
     value = qkv[rows, (groups + 1) * d : (groups + 2) * d]
@@ -296,14 +377,14 @@
 
 
 def attend_back_one(
-    groups, s, qkv, att, datt, seg_col, seg_row, cos_ref, sin_ref, gain_q, gain_k, grad, gains
+    groups, s, qkv, att, datt, starts, cos_ref, sin_ref, gain_q, gain_k, grad, gains
 ):
     d = gain_q.shape[-1]
-    length = cos_ref.shape[1]
+    length = cos_ref.shape[0] // 2
     rows = pl.ds(pl.multiple_of(s * length, length), length)
-    cos, sin = cos_ref[s], sin_ref[s]
+    cos, sin = cos_ref[rows], sin_ref[rows]
     scale = d**-0.5
-    allowed = allowed_keys(seg_col[s], seg_row[s])
+    allowed = allowed_keys(starts[rows, 0:1])
     at_k, at_v = slice(groups * d, (groups + 1) * d), slice((groups + 1) * d, (groups + 2) * d)
     unit_k, scale_k = head_unit(qkv[rows, at_k].astype(F32))
     key = rot(unit_k * gain_k[...], cos, sin).astype(BF16)
@@ -331,15 +412,13 @@
 
 
 def attend_back_kernel(
-    groups, qkv, att, datt, seg_col, seg_row, cos, sin, gain_q, gain_k, grad, gains
+    groups, qkv, att, datt, starts, cos, sin, gain_q, gain_k, grad, gains
 ):
     gains[...] = jnp.zeros_like(gains)
 
-    @pl.loop(0, cos.shape[0])
+    @pl.loop(0, 2)
     def _(s):
-        attend_back_one(
-            groups, s, qkv, att, datt, seg_col, seg_row, cos, sin, gain_q, gain_k, grad, gains
-        )
+        attend_back_one(groups, s, qkv, att, datt, starts, cos, sin, gain_q, gain_k, grad, gains)
 
 
 def attend_back(groups, qkv, att, datt, common):
@@ -361,15 +440,19 @@
 
 def forward_kernel(
     bits, groups, natural,
-    hidden, cot, gain_attn, gain_mlp, seg_col, seg_row, cos, sin, gain_q, gain_k, wq, wk, wv, wo, wg, wu, wd,
-    mid, normed_one, normed_two, cot_rows, qkv_out, att_out, qkv_weight, out_weight, gate_weight, up_weight, down_weight,
-    own_one, own_two, rows_one, w_qkv, w_out, qkv, att, part, first, ctx_in, pair_in, sending, send, recv, local,
+    hidden, cot, gain_attn, gain_mlp, seg, table, gain_q, gain_k, wq, wk, wv, wo, wg, wu, wd,
+    mid, normed_one, normed_two, cot_out, qkv_out, att_out, qkv_weight, out_weight, starts_out, cos_out, sin_out,
+    grad_gate_out, grad_up_out, mixed_out, part_out, down_out, spare_qkv, spare_out, spare_gate, spare_up, spare_down,
+    own_one, own_two, rows_one, rows_two, rows_cot, w_qkv, w_out, w_gate, w_up, w_down, qkv, att, part,
+    gate, up, grad_gate, grad_up, mixed, mixed_t, starts, cos, sin, seg_in, first, ctx_in, pair_in, sending,
+    send, recv, local,
 ):
     place = Place(bits)
     moves = Moves(send, recv, local)
     rows, width = hidden.shape
     at_rows, ff_rows, ff_cols = wq.shape[0], wg.shape[0], wg.shape[1] // 2
     q_cols, kv_cols = wq.shape[1] // 4, wk.shape[1] // 4
+    n_rows, length = rows_one.shape[0], seg.shape[1]
 
     def lanes(start, size):
         return pl.ds(pl.multiple_of(start, size), size)
@@ -395,7 +478,7 @@
     )
     f0, c0, _ = place.at[0]
     qkv_in, out_in = {}, {}
-    for j in (3, 2, 1):
+    for j in (1, 3, 2):
         fj, cj, _ = place.at[j]
         qkv_in[j] = [
             moves.swap(
@@ -410,11 +493,13 @@
         moves.load(w.at[:, lanes(place.chunk_of[0] * size, size)], w_qkv.at[qkv_rows(f0, c0), to])
         for w, size, to in pieces
     ]
-    for j in (3, 2, 1):
-        fj, cj, _ = place.at[j]
-        out_in[j] = moves.swap(out_chunk(j), out_block(f0, c0), out_block(fj, cj), place.chips[j])
-    out_in[0] = moves.load(out_chunk(0), out_block(f0, c0))
-
+    seg_wait = moves.swap(seg, seg_in, seg_in, place.chips[2])
+
+    def norm_one(at):
+        unit, _ = unit_and_scale(hidden[at].astype(F32))
+        own_one[at] = (unit * gain_attn[...]).astype(BF16)
+
+    row_loop(rows, norm_one)
     def rows_block(w):
         return lambda f: w.at[lanes(f * ff_rows, ff_rows)]
 
@@ -423,91 +508,115 @@
 
     mine, theirs = lanes(place.pair * ff_cols, ff_cols), lanes((1 - place.pair) * ff_cols, ff_cols)
     feed = [
-        (Gather(moves, place, rows_block(gate_weight)), wg.at[:, mine], wg.at[:, theirs]),
-        (Gather(moves, place, rows_block(up_weight)), wu.at[:, mine], wu.at[:, theirs]),
-        (Gather(moves, place, cols_block(down_weight)), wd.at[mine], wd.at[theirs])
+        (Gather(moves, place, rows_block(w_gate), spare_gate), wg.at[:, mine], wg.at[:, theirs]),
+        (Gather(moves, place, rows_block(w_up), spare_up), wu.at[:, mine], wu.at[:, theirs]),
+        (Gather(moves, place, cols_block(w_down), spare_down), wd.at[mine], wd.at[theirs])
         if natural
-        else (Gather(moves, place, rows_block(down_weight)), wd.at[:, mine], wd.at[:, theirs]),
+        else (Gather(moves, place, rows_block(w_down), spare_down), wd.at[:, mine], wd.at[:, theirs]),
     ]
+    own_feed = [moves.load(own, gather.block(place.f)) for gather, own, _ in feed]
 
     def swap_pair(i):
-        gather, own, other = feed[i]
+        gather, _, other = feed[i]
         gather.waits[PAIR] = moves.swap(
             other, gather.block(place.f), gather.block(place.block(PAIR)), place.along(PAIR)
         )
-        moves.store(own, gather.block(place.f))
-
-    def norm_one(at):
-        unit, _ = unit_and_scale(hidden[at].astype(F32))
-        own_one[at] = (unit * gain_attn[...]).astype(BF16)
-
-    row_loop(rows, norm_one)
-    spread_one = Spread(moves, place, own_one, rows_one)
-
-    qkv_gather = Gather(moves, place, lambda f: w_qkv.at[qkv_rows(f)])
-    out_gather = Gather(moves, place, out_block)
-    for gather, arrivals in ((qkv_gather, qkv_in), (out_gather, {j: [w] for j, w in out_in.items()})):
+
+    def send_feed(i):
+        gather, own, _ = feed[i]
+        gather.forward(0, own)
+        gather.pass_on(PAIR)
+
+    qkv_gather = Gather(moves, place, lambda f: w_qkv.at[qkv_rows(f)], spare_qkv)
+    out_gather = Gather(moves, place, out_block, spare_out)
+
+    def send_attn(gather, arrivals):
         for wait in (*arrivals[0], *arrivals[1]):
             wait()
         gather.forward(0)
         for wait in (*arrivals[2], *arrivals[3]):
             wait()
         gather.forward(PAIR)
+
+    send_attn(qkv_gather, qkv_in)
+    for j in (3, 2, 1):
+        fj, cj, _ = place.at[j]
+        out_in[j] = moves.swap(out_chunk(j), out_block(f0, c0), out_block(fj, cj), place.chips[j])
+    out_in[0] = moves.load(out_chunk(0), out_block(f0, c0))
+    spread_one = Spread(moves, place, own_one, rows_one)
     swap_pair(0)
+    seg_wait()
+    pair_first = place.pair == 0
+    own_seg, far_seg = seg[...].astype(F32), seg_in[...].astype(F32)
+    for i in range(2):
+        here = pair_first if i == 0 else jnp.logical_not(pair_first)
+        flags = jnp.where(here, own_seg, far_seg)
+        both = jnp.broadcast_to(flags, (128, length)).T[:, 0:1]
+        start = jnp.sum((flags < both).astype(F32), axis=1, keepdims=True)
+        row = lax.broadcasted_iota(jnp.int32, (length, length), 0).astype(F32)
+        col = lax.broadcasted_iota(jnp.int32, (length, length), 1).astype(F32)
+        chosen = (row - start == col).astype(F32)
+        at = pl.ds(i * length, length)
+        both_tables = lax.dot_general(
+            chosen, table[...], (((1,), (0,)), ((), ())),
+            precision=lax.Precision.HIGHEST, preferred_element_type=F32,
+        )
+        d = gain_q.shape[1]
+        starts[at] = jnp.broadcast_to(start, (length, 128))
+        cos[at] = both_tables[:, :d]
+        sin[at] = both_tables[:, d:]
+    moves.store(starts, starts_out)
+    moves.store(cos, cos_out)
+    moves.store(sin, sin_out)
+    qkv_gather.relay()
     spread_one.from_pair()
+    send_attn(out_gather, {j: [w] for j, w in out_in.items()})
+    qkv_gather.middle()
     spread_one.from_ctx()
-    qkv_gather.middle()
-    out_gather.middle()
-    feed[0][0].forward(0, feed[0][1])
-    feed[0][0].waits.pop(PAIR)()
-    feed[0][0].forward(PAIR)
+    send_feed(0)
     swap_pair(1)
+    out_gather.relay()
     spread_one.from_both()
     spread_one.finish()
     qkv_gather.finish()
-
-    moves.store(rows_one, normed_one)
-    moves.store(w_qkv, qkv_weight)
     step = 2 * rows
 
-    @pl.loop(0, 8 * rows // step)
+    @pl.loop(0, n_rows // step)
     def _(i):
         at = lanes(i * step, step)
         qkv[at] = dot(rows_one[at], w_qkv[...]).astype(BF16)
 
     moves.store(qkv, qkv_out)
-    spread_cot = Spread(moves, place, cot, cot_rows)
+    normed_stored = moves.load(rows_one, normed_one)
+    moves.store(w_qkv, qkv_weight)
+    spread_cot = Spread(moves, place, cot, rows_cot)
+    out_gather.middle()
+    feed[0][0].relay()
+    send_feed(1)
+
+    @pl.loop(0, 2)
+    def _(s):
+        attend_one(groups, s, qkv, starts, cos, sin, gain_q, gain_k, att)
+
+    moves.store(att, att_out)
+    out_gather.finish()
     swap_pair(2)
-
-    def pump(i):
-        feed[i][0].middle()
-        if i + 1 < len(feed):
-            gather, own, _ = feed[i + 1]
-            gather.forward(0, own)
-            gather.waits.pop(PAIR)()
-            gather.forward(PAIR)
-
-    @pl.loop(0, cos.shape[0])
-    def _(s):
-        attend_one(groups, s, qkv, seg_col, seg_row, cos, sin, gain_q, gain_k, att)
-
-    moves.store(att, att_out)
-    spread_cot.from_pair()
-    out_gather.finish()
-    moves.store(w_out, out_weight)
 
     @pl.loop(0, 8)
     def _(i):
         part[i] = (dot if natural else dot_cols)(att[lanes(i * rows, rows)], w_out[...]).astype(BF16)
 
+    moves.store(w_out, out_weight)
     collect = Collect(
         moves, place, lambda j, t: part.at[place.rows_of[j] + t], None, first, ctx_in, pair_in, sending, False
     )
     collect.to_ctx()
+    feed[0][0].middle()
+    feed[1][0].relay()
+    spread_cot.from_pair()
+    collect.to_pair()
+    send_feed(2)
     spread_cot.from_ctx()
-    pump(0)
-    collect.to_pair()
-    spread_cot.from_both()
     collect.finish()
 
     def norm_two(at):
@@ -517,16 +626,68 @@
         own_two[at] = (unit * gain_mlp[...]).astype(BF16)
 
     row_loop(rows, norm_two)
-    spread_two = Spread(moves, place, own_two, normed_two)
+    spread_two = Spread(moves, place, own_two, rows_two)
+    feed[1][0].middle()
+    feed[2][0].relay()
+    spread_cot.from_both()
     spread_two.from_pair()
-    pump(1)
     spread_two.from_ctx()
     spread_two.from_both()
     spread_two.finish()
+    moves.store(rows_two, normed_two)
+    for wait in own_feed:
+        wait()
+    feed[0][0].finish()
+
+    @pl.loop(0, n_rows // step)
+    def _(i):
+        at = lanes(i * step, step)
+        gate[at] = dot(rows_two[at], w_gate[...])
+
     spread_cot.finish()
-    pump(2)
-    for gather, _, _ in feed:
-        gather.finish()
+    moves.store(rows_cot, cot_out)
+    feed[2][0].middle()
+    feed[1][0].finish()
+
+    @pl.loop(0, n_rows // step)
+    def _(i):
+        at = lanes(i * step, step)
+        u = dot(rows_two[at], w_up[...])
+        up[at] = u
+        g = gate[at]
+        mix = g * jax.nn.sigmoid(g) * u
+        mixed[at] = mix.astype(BF16)
+        mixed_t[:, at] = mix.T.astype(BF16)
+
+    moves.store(mixed_t, mixed_out)
+    normed_stored()
+    feed[2][0].finish()
+
+    @pl.loop(0, n_rows // step)
+    def _(i):
+        at = lanes(i * step, step)
+        m = (dot_cols if natural else dot)(rows_cot[at], w_down[...])
+        g = gate[at]
+        s = jax.nn.sigmoid(g)
+        grad_gate[at] = (m * up[at] * s * (1.0 + g * (1.0 - s))).astype(BF16)
+        grad_up[at] = (m * (g * s)).astype(BF16)
+
+    moves.store(grad_gate, grad_gate_out)
+    moves.store(grad_up, grad_up_out)
+
+    @pl.loop(0, 8)
+    def _(i):
+        at = lanes(i * rows, rows)
+        part[i] = (dot_cols(grad_gate[at], w_gate[...]) + dot_cols(grad_up[at], w_up[...])).astype(BF16)
+
+    moves.store(part, part_out)
+
+    @pl.loop(0, 8)
+    def _(i):
+        at = lanes(i * rows, rows)
+        rows_one[at] = (dot if natural else dot_cols)(mixed[at], w_down[...]).astype(BF16)
+
+    moves.store(rows_one, down_out)
     moves.close()
 
 
@@ -591,20 +752,25 @@
 
 
 class Scatter:
-    def __init__(self, moves, place, product, out0, in0, out1, in1, acc):
-        self.moves, self.place, self.product = moves, place, product
+    def __init__(self, moves, place, product, out0, in0, out1, in1, acc, spare):
+        self.moves, self.place, self.product, self.spare = moves, place, product, spare
         self.out0, self.in0, self.out1, self.in1, self.acc = out0, in0, out1, in1, acc
         self.low, self.high = place.bits[1], place.bits[0]
         self.order = [self.high, self.high | PAIR, 0, PAIR]
-        self.first, self.second = {}, {}
+        self.first, self.second, self.leaving = {}, {}, {}
 
     def send(self, i):
+        slot = i % 2
+        for wait in self.leaving.pop(slot, []):
+            wait()
+
         def emit(at, value):
-            self.out0[(i, *at)] = value.astype(BF16)
+            self.out0[(slot, *at)] = value.astype(BF16)
 
         self.product(self.order[i] | self.low, emit)
+        self.leaving[slot] = []
         self.first[i] = self.moves.swap(
-            self.out0.at[i], self.in0.at[i], self.in0.at[i], self.place.along(self.low)
+            self.out0.at[slot], self.in0.at[i], self.in0.at[i], self.place.along(self.low), self.leaving[slot]
         )
 
     def take(self, i):
@@ -619,12 +785,16 @@
 
         self.product(self.order[i], emit)
         if i < 2:
-            self.second[i] = self.moves.swap(
-                self.out1.at[i], self.in1.at[i], self.in1.at[i], self.place.along(self.high)
+            to = self.in1.at[i]
+            self.second[i] = Cross(
+                self.moves, self.place, self.out1.at[i], to, self.spare.at[2 * i], to, self.spare.at[2 * i + 1], to
             )
 
+    def relay(self, i):
+        self.second[i].relay()
+
     def take_high(self, i):
-        self.second[i]()
+        self.second[i].arrive()
         rows = self.acc.shape[1]
         step = 64
 
@@ -632,6 +802,11 @@
         def _(k):
             at = pl.ds(pl.multiple_of(k * step, step), step)
             self.acc[i, at] += self.in1[i, at].astype(F32)
+
+    def close(self):
+        for waits in self.leaving.values():
+            for wait in waits:
+                wait()
 
 
 class Blocks:
@@ -658,9 +833,11 @@
 
 def backward_kernel(
     bits, groups,
-    mid, hidden, cot, gain_attn, gain_mlp, seg_col, seg_row, cos, sin, gain_q, gain_k,
-    part_two, normed_one, normed_two, cot_rows, qkv_in, att_in, qkv_weight, out_weight, grad_gate, grad_up, mixed_t,
-    grad_in, gains, feed_own, feed_other, down_own, down_other, qkv_own, qkv_other, out_own, out_other,
+    mid, hidden, cot, gain_attn, gain_mlp, starts, cos, sin, gain_q, gain_k,
+    part_two, part_hidden, normed_one, normed_two, cot_rows, qkv_in, att_in, qkv_weight, out_weight, grad_gate, grad_up,
+    mixed_t,
+    grad_in, hidden_out, gains, feed_own, feed_other, down_own, down_other, qkv_own, qkv_other, out_own, out_other,
+    spare_feed, spare_down, spare_qkv, spare_out,
     own, rows_mid, feed, mixed, lhs, lhs_t, part, w_qkv, w_out, qkv, att, datt, dqkv,
     first, ctx_in, pair_in, sending, gain_a, gain_m, gain_h, tree, tree_in,
     f_out0, f_in0, f_out1, f_in1, f_acc, d_out0, d_in0, d_out1, d_in1, d_acc,
@@ -688,14 +865,15 @@
     )
     masks = [high, high | PAIR, 0, PAIR]
     sends = [m | low for m in masks]
-    order = (
-        [(normed_two, m) for m in [*sends, masks[0], masks[1]]]
-        + [(cot_rows, m) for m in sends]
-        + [(normed_one, m) for m in sends]
-        + [(normed_two, m) for m in masks[2:]]
-        + [(cot_rows, m) for m in masks]
-        + [(normed_one, m) for m in masks]
-    )
+    order = [
+        (cot_rows, sends[0]), (cot_rows, sends[1]), (normed_two, sends[0]), (cot_rows, masks[0]),
+        (normed_two, sends[1]), (cot_rows, masks[1]), (normed_two, masks[0]),
+        (cot_rows, sends[2]), (cot_rows, sends[3]), (normed_two, sends[2]), (normed_two, sends[3]),
+        (normed_two, masks[1]),
+        (normed_one, sends[0]), (normed_one, sends[1]), (cot_rows, masks[2]), (cot_rows, masks[3]),
+        (normed_one, sends[2]), (normed_one, sends[3]), (normed_two, masks[2]), (normed_two, masks[3]),
+        *[(normed_one, m) for m in masks],
+    ]
     blocks = Blocks(moves, place, lhs, order)
     ready_mixed = moves.load(mixed_t, mixed)
     ready_late = [
@@ -730,20 +908,23 @@
         at = lanes(place.block(mask) * tile, tile)
         emit((slice(None), slice(None)), dot_rows(att[...], rows_mid[:, at]))
 
-    feed_s = Scatter(moves, place, by_rows(normed_two, feed), f_out0, f_in0, f_out1, f_in1, f_acc)
-    down_s = Scatter(moves, place, down_product, d_out0, d_in0, d_out1, d_in1, d_acc)
-    qkv_s = Scatter(moves, place, by_rows(normed_one, dqkv), q_out0, q_in0, q_out1, q_in1, q_acc)
-    out_s = Scatter(moves, place, out_product, o_out0, o_in0, o_out1, o_in1, o_acc)
-
+    feed_s = Scatter(moves, place, by_rows(normed_two, feed), f_out0, f_in0, f_out1, f_in1, f_acc, spare_feed)
+    down_s = Scatter(moves, place, down_product, d_out0, d_in0, d_out1, d_in1, d_acc, spare_down)
+    qkv_s = Scatter(moves, place, by_rows(normed_one, dqkv), q_out0, q_in0, q_out1, q_in1, q_acc, spare_qkv)
+    out_s = Scatter(moves, place, out_product, o_out0, o_in0, o_out1, o_in1, o_acc, spare_out)
+
+    ready_mixed()
+    down_s.send(0)
+    down_s.send(1)
+    collect_two.to_ctx()
     for wait in ready_feed:
         wait()
     feed_s.send(0)
-    collect_two.to_ctx()
+    down_s.take(0)
+    collect_two.to_pair()
     feed_s.send(1)
-    feed_s.send(2)
-    collect_two.to_pair()
-    feed_s.send(3)
-    feed_s.take(0)
+    down_s.relay(0)
+    down_s.take(1)
     collect_two.finish()
     gain_m[...] = jnp.zeros_like(gain_m)
     gain_a[...] = jnp.zeros_like(gain_a)
@@ -756,15 +937,16 @@
 
     row_loop(rows, back_two)
     spread = Spread(moves, place, own, rows_mid)
-    feed_s.take(1)
+    feed_s.take(0)
+    down_s.relay(1)
     spread.from_pair()
-    ready_mixed()
-    down_s.send(0)
-    down_s.send(1)
-    spread.from_ctx()
-    spread.from_both()
     down_s.send(2)
     down_s.send(3)
+    spread.from_ctx()
+    feed_s.send(2)
+    feed_s.send(3)
+    spread.from_both()
+    feed_s.relay(0)
     for wait in ready_late:
         wait()
     spread.finish()
@@ -774,11 +956,11 @@
         at = lanes(i * 2 * rows, 2 * rows)
         datt[at] = dot_cols(rows_mid[at], w_out[...]).astype(BF16)
 
-    @pl.loop(0, cos.shape[0])
+    feed_s.take(1)
+
+    @pl.loop(0, 2)
     def _(s):
-        attend_back_one(
-            groups, s, qkv, att, datt, seg_col, seg_row, cos, sin, gain_q, gain_k, dqkv, gain_h
-        )
+        attend_back_one(groups, s, qkv, att, datt, starts, cos, sin, gain_q, gain_k, dqkv, gain_h)
 
     @pl.loop(0, 8)
     def _(i):
@@ -787,22 +969,35 @@
     collect_one = Collect(
         moves, place, lambda j, t: part.at[place.rows_of[j] + t], None, first, ctx_in, pair_in, sending, False
     )
-    for i in range(4):
-        out_s.send(i)
+    qkv_s.send(0)
+    qkv_s.send(1)
+    out_s.send(0)
+    out_s.send(1)
     collect_one.to_ctx()
-    for i in range(4):
-        qkv_s.send(i)
+    feed_s.relay(1)
+    down_s.take(2)
+    down_s.take(3)
     collect_one.to_pair()
+    qkv_s.send(2)
+    qkv_s.send(3)
+    out_s.send(2)
+    out_s.send(3)
+    collect_one.finish()
+
+    def back_one(at):
+        grad_in[at] += norm_back(collect_one.total(at), hidden[at].astype(F32), gain_attn[...], gain_a)
+
+    row_loop(rows, back_one)
     feed_s.take(2)
     feed_s.take(3)
-    down_s.take(0)
-    down_s.take(1)
-    collect_one.finish()
-
-    def back_one(at):
-        grad_in[at] += norm_back(collect_one.total(at), hidden[at].astype(F32), gain_attn[...], gain_a)
-
-    row_loop(rows, back_one)
+    qkv_s.take(0)
+    qkv_s.take(1)
+    out_s.take(0)
+    out_s.take(1)
+    qkv_s.relay(0)
+    qkv_s.relay(1)
+    out_s.relay(0)
+    out_s.relay(1)
 
     d = gain_q.shape[1]
     tree[0, :, 0:width] = jnp.sum(gain_a[...], axis=0, keepdims=True)
@@ -813,7 +1008,10 @@
         moves.swap(tree.at[k], tree_in.at[k], tree_in.at[k], device)()
         tree[k + 1] = tree[k] + tree_in[k]
     gains[...] = tree[3 + len(bits)]
-
+    collect_hidden = Collect(
+        moves, place, lambda j, t: part_hidden.at[place.rows_of[j] + t], part, first, ctx_in, pair_in, sending, True
+    )
+    collect_hidden.to_ctx()
     finals = []
 
     def feed_final(scatter, mine, other):
@@ -839,25 +1037,67 @@
             finals.append(moves.swap(out, other.at[j - 1], other.at[j - 1], place.chips[j]))
         mine[...] = piece(0, place.c)
 
+    feed_final(down_s, down_own, down_other)
+    collect_hidden.to_pair()
+    qkv_s.take(2)
+    qkv_s.take(3)
+    out_s.take(2)
+    out_s.take(3)
+    collect_hidden.finish()
+
+    def add_hidden(at):
+        hidden_out[at] = mid[at] + collect_hidden.total(at)
+
+    row_loop(rows, add_hidden)
     feed_final(feed_s, feed_own, feed_other)
-    down_s.take(2)
-    down_s.take(3)
-    for i in range(4):
-        out_s.take(i)
-    for i in range(4):
-        qkv_s.take(i)
-    feed_final(down_s, down_own, down_other)
+    mates_final(
+        qkv_s, lambda slot, c: q_acc[slot, lanes(c * half, half)],
+        lambda j: q_in0.at[j, pl.ds(0, half)], qkv_own, qkv_other,
+    )
     mates_final(
         out_s, lambda slot, c: o_acc[slot, :, lanes(c * half, half)],
         lambda j: o_in0.at[j, :, pl.ds(0, half)], out_own, out_other,
     )
-    mates_final(
-        qkv_s, lambda slot, c: q_acc[slot, lanes(c * half, half)],
-        lambda j: q_in0.at[j, pl.ds(0, half)], qkv_own, qkv_other,
-    )
+    for scatter in (feed_s, down_s, qkv_s, out_s):
+        scatter.close()
     for wait in finals:
         wait()
     moves.close()
+
+
+def join_kernel(
+    feed_own, feed_other, down_own, down_other, qkv_own, qkv_other, out_own, out_other, grad_in, hidden, gains,
+    g_query, g_key, g_value, g_out, g_gate, g_up, g_down, g_in, h_out, gain_a, gain_m, gain_q, gain_k,
+):
+    c = lax.axis_index("ctx")
+    pair = (lax.axis_index("fsdp") // PAIR) % 2
+    cols, n_q = down_own.shape[0], out_own.shape[0]
+    n_kv = (qkv_own.shape[1] - n_q) // 2
+
+    def lanes(start, size):
+        return pl.ds(pl.multiple_of(start, size), size)
+
+    mine, theirs = lanes(pair * cols, cols), lanes((1 - pair) * cols, cols)
+    g_gate[:, mine] = feed_own[:, :cols]
+    g_up[:, mine] = feed_own[:, cols:]
+    g_down[mine] = down_own[...]
+    g_gate[:, theirs] = feed_other[:, :cols].astype(F32)
+    g_up[:, theirs] = feed_other[:, cols:].astype(F32)
+    g_down[theirs] = down_other[...].astype(F32)
+    chunks = [c * 2 + pair, (1 - c) * 2 + pair, c * 2 + 1 - pair, (1 - c) * 2 + 1 - pair]
+    for j, chunk in enumerate(chunks):
+        qkv = qkv_own[...] if j == 0 else qkv_other[j - 1].astype(F32)
+        g_query[:, lanes(chunk * n_q, n_q)] = qkv[:, :n_q]
+        g_key[:, lanes(chunk * n_kv, n_kv)] = qkv[:, n_q : n_q + n_kv]
+        g_value[:, lanes(chunk * n_kv, n_kv)] = qkv[:, n_q + n_kv :]
+        g_out[lanes(chunk * n_q, n_q)] = out_own[...] if j == 0 else out_other[j - 1].astype(F32)
+    g_in[...] = grad_in[...]
+    h_out[...] = hidden[...]
+    width, d = gain_a.shape[1], gain_q.shape[1]
+    gain_a[...] = gains[:, :width]
+    gain_m[...] = gains[:, width : 2 * width]
+    gain_q[...] = gains[:, 2 * width : 2 * width + d]
+    gain_k[...] = gains[:, 2 * width + d :]
 
 
 VMEM_SPEC = pl.BlockSpec(memory_space=pltpu.VMEM)
@@ -874,7 +1114,7 @@
             *scratch,
             pltpu.SemaphoreType.DMA((copies,)),
             pltpu.SemaphoreType.DMA((copies,)),
-            pltpu.SemaphoreType.DMA((80,)),
+            pltpu.SemaphoreType.DMA((96,)),
         ],
         compiler_params=pltpu.CompilerParams(
             collective_id=collective_id, has_side_effects=True, vmem_limit_bytes=61 << 20
@@ -942,20 +1182,10 @@
         q_cols, kv_cols = w_query.shape[1] // 4, key_projection_weight.shape[1] // 4
         groups = q_cols // kv_cols
 
-        seg = in_order(pair, segments, swap(segments, PAIR_BIT), 0)
-        before = jnp.sum((seg[:, None, :] < seg[:, :, None]).astype(jnp.int32), axis=-1)
-        positions = jnp.arange(length, dtype=jnp.int32)[None] - before
         freqs = THETA ** (-2.0 * jnp.arange(d // 2, dtype=F32) / d)
-        angles = positions.astype(F32)[..., None] * freqs
-        cos, sin = jnp.cos(angles), jnp.sin(angles)
-        common = (
-            seg[:, :, None],
-            seg[:, None, :],
-            jnp.concatenate([cos, cos], axis=-1),
-            jnp.concatenate([-sin, sin], axis=-1),
-            gain_query[None],
-            key_norm_gain[None],
-        )
+        angles = jnp.arange(length, dtype=jnp.int32).astype(F32)[:, None] * freqs
+        table_cos, table_sin = jnp.cos(angles), jnp.sin(angles)
+        table = jnp.concatenate([table_cos, table_cos, -table_sin, table_sin], axis=-1)
 
         n_rows = 8 * rows
         all_rows = jax.ShapeDtypeStruct((n_rows, width), BF16)
@@ -968,60 +1198,54 @@
         def shape(*dims):
             return jax.ShapeDtypeStruct(dims, BF16)
 
-        copies = 120 + 10 * n_f
+        copies = 160 + 10 * n_f
         natural = at_rows % 128 == 0 and ff_rows % 128 == 0
         out_dims = (q_cols, width) if natural else (width, q_cols)
         down_dims = (ff_cols, width) if natural else (width, ff_cols)
-        times, times_t = (dot, dot_cols) if natural else (dot_cols, dot)
+        out_part = (q_cols, 2 * at_rows) if natural else (2 * at_rows, q_cols)
+        down_part_dims = (ff_cols, ff_rows) if natural else (ff_rows, ff_cols)
+        n_seq = 2 * length
+        all_tables = jax.ShapeDtypeStruct((n_seq, d), F32)
+
+        def v(*dims, dtype=BF16):
+            return pltpu.VMEM(dims, dtype)
+
         (
-            residual_mid, normed_one, normed_two, grad_rows, qkv, attended, full_qkv, full_out,
-            full_gate, full_up, full_down,
+            residual_mid, normed_one, normed_two, grad_rows, qkv, attended, full_qkv, full_out, starts, cos, sin,
+            grad_gate, grad_up, mixed_t, norm_two_part, down_part, *_,
         ) = comm_call(
             forward_kernel, spread_bits, 0,
-            (hidden_in, cotangent, gain_attn[None], gain_mlp[None], *common, w_query, key_projection_weight,
-             value_projection_weight, w_out if natural else w_out.T, w_gate, w_up, w_down if natural else w_down.T),
-            [VMEM_SPEC] * 10 + [ANY_SPEC] * 7,
+            (hidden_in, cotangent, gain_attn[None], gain_mlp[None], segments[None], table, gain_query[None],
+             key_norm_gain[None], w_query, key_projection_weight, value_projection_weight,
+             w_out if natural else w_out.T, w_gate, w_up, w_down if natural else w_down.T),
+            [VMEM_SPEC] * 8 + [ANY_SPEC] * 7,
             (own_rows, all_rows, all_rows, all_rows, shape(n_rows, qkv_cols), shape(n_rows, q_cols),
-             shape(width, qkv_cols), shape(*out_dims), shape(width, ff_cols), shape(width, ff_cols),
-             shape(*down_dims)),
-            (VMEM_SPEC, *[ANY_SPEC] * 10),
-            [block, block, pltpu.VMEM((n_rows, width), BF16), pltpu.VMEM((width, qkv_cols), BF16),
-             pltpu.VMEM(out_dims, BF16), pltpu.VMEM((n_rows, qkv_cols), BF16),
-             pltpu.VMEM((n_rows, q_cols), BF16), pltpu.VMEM((8, rows, width), BF16),
+             shape(width, qkv_cols), shape(*out_dims), jax.ShapeDtypeStruct((n_seq, 128), F32), all_tables, all_tables,
+             shape(n_rows, ff_cols), shape(n_rows, ff_cols), shape(ff_cols, n_rows), shape(8, rows, width), all_rows,
+             shape(4, 2 * at_rows, qkv_cols), shape(4, *out_part), shape(4, ff_rows, ff_cols),
+             shape(4, ff_rows, ff_cols), shape(4, *down_part_dims)),
+            (VMEM_SPEC, *[ANY_SPEC] * 20),
+            [block, block, v(n_rows, width), v(n_rows, width), v(n_rows, width), v(width, qkv_cols), v(*out_dims),
+             v(width, ff_cols), v(width, ff_cols), v(*down_dims), v(n_rows, qkv_cols), v(n_rows, q_cols),
+             v(8, rows, width), v(n_rows, ff_cols, dtype=F32), v(n_rows, ff_cols, dtype=F32), v(n_rows, ff_cols),
+             v(n_rows, ff_cols), v(n_rows, ff_cols), v(ff_cols, n_rows), v(n_seq, 128, dtype=F32),
+             v(n_seq, d, dtype=F32), v(n_seq, d, dtype=F32), v(1, length, dtype=jnp.int32),
              *collect_buffers(rows, width)],
             16 * nbytes, copies, groups, natural,
         )
-        teams = sorted(
-            sorted(i ^ b ^ p for b in range(4) for p in (0, PAIR_BIT))
-            for i in range(0, n, 4)
-            if not i & PAIR_BIT
+        common = (starts, cos, sin, gain_query[None], key_norm_gain[None])
+        backward = one_kernel if natural and len(spread_bits) == 2 else by_steps
+        return backward(
+            hidden_in, cotangent, residual_mid, gain_attn, gain_mlp, common, norm_two_part, down_part, normed_one,
+            normed_two, grad_rows, qkv, attended, full_qkv, full_out, grad_gate, grad_up, mixed_t, (at_rows, ff_rows),
         )
 
-        gate_pre = dot(normed_two, full_gate)
-        up_pre = dot(normed_two, full_up)
-        gate_sig = jax.nn.sigmoid(gate_pre)
-        gate_act = gate_pre * gate_sig
-        mixed = (gate_act * up_pre).astype(BF16)
-        grad_mixed = times_t(grad_rows, full_down)
-        grad_gate = (grad_mixed * up_pre * gate_sig * (1.0 + gate_pre * (1.0 - gate_sig))).astype(BF16)
-        grad_up = (grad_mixed * gate_act).astype(BF16)
-        norm_two_part = (dot_cols(grad_gate, full_gate) + dot_cols(grad_up, full_up)).astype(BF16)
-        down_part = times(mixed, full_down).astype(BF16)
-        hidden_out = residual_mid + lax.psum_scatter(
-            down_part, AXES, scatter_dimension=0, axis_index_groups=teams, tiled=True
-        ).astype(F32)
-        backward = one_kernel if natural and len(spread_bits) == 2 else by_steps
-        return hidden_out, *backward(
-            hidden_in, cotangent, residual_mid, gain_attn, gain_mlp, common, norm_two_part, normed_one, normed_two,
-            grad_rows, qkv, attended, full_qkv, full_out, grad_gate, grad_up, mixed, (at_rows, ff_rows),
-        )
-
     def one_kernel(
-        hidden_in, cotangent, residual_mid, gain_attn, gain_mlp, common, norm_two_part, normed_one, normed_two,
-        grad_rows, qkv, attended, full_qkv, full_out, grad_gate, grad_up, mixed, sizes,
+        hidden_in, cotangent, residual_mid, gain_attn, gain_mlp, common, norm_two_part, down_part, normed_one,
+        normed_two, grad_rows, qkv, attended, full_qkv, full_out, grad_gate, grad_up, mixed_t, sizes,
     ):
         rows, width = hidden_in.shape
-        n_rows, cols = mixed.shape
+        cols, n_rows = mixed_t.shape
         (at_rows, ff_rows), q_cols, qkv_cols = sizes, attended.shape[1], qkv.shape[1]
         d = common[-1].shape[1]
         kv_cols = (qkv_cols - q_cols) // 2
@@ -1034,22 +1258,26 @@
             return pltpu.VMEM(dims, dtype)
 
         def scatter(*block):
-            return [v(4, *block), v(4, *block), v(2, *block), v(2, *block), v(2, *block, dtype=F32)]
+            return [v(2, *block), v(4, *block), v(2, *block), v(2, *block), v(2, *block, dtype=F32)]
 
         n_gain = 2 * width + 2 * d
         nbytes = n_rows * width * 20
         (
-            grad_input, gains, feed_own, feed_other, down_own, down_other, qkv_own, qkv_other, out_own, out_other,
+            grad_input, hidden_out, gains, feed_own, feed_other, down_own, down_other, qkv_own, qkv_other, out_own,
+            out_other, *_,
         ) = comm_call(
             backward_kernel, spread_bits, 2,
-            (residual_mid, hidden_in, cotangent, gain_attn[None], gain_mlp[None], *common,
-             norm_two_part.reshape(8, rows, width), normed_one, normed_two, grad_rows, qkv, attended, full_qkv,
-             full_out, grad_gate, grad_up, mixed.T),
-            [VMEM_SPEC] * 11 + [ANY_SPEC] * 11,
-            (out(F32, rows, width), out(F32, 1, n_gain), out(F32, ff_rows, 2 * cols), out(BF16, ff_rows, 2 * cols),
-             out(F32, cols, ff_rows), out(BF16, cols, ff_rows), out(F32, at_rows, qkv_cols),
-             out(BF16, 3, at_rows, qkv_cols), out(F32, q_cols, at_rows), out(BF16, 3, q_cols, at_rows)),
-            (VMEM_SPEC, VMEM_SPEC, ANY_SPEC, ANY_SPEC, ANY_SPEC, ANY_SPEC, VMEM_SPEC, ANY_SPEC, VMEM_SPEC, ANY_SPEC),
+            (residual_mid, hidden_in, cotangent, gain_attn[None], gain_mlp[None], *common, norm_two_part,
+             down_part.reshape(8, rows, width), normed_one, normed_two, grad_rows, qkv, attended, full_qkv, full_out,
+             grad_gate, grad_up, mixed_t),
+            [VMEM_SPEC] * 10 + [ANY_SPEC] * 12,
+            (out(F32, rows, width), out(F32, rows, width), out(F32, 1, n_gain), out(F32, ff_rows, 2 * cols),
+             out(BF16, ff_rows, 2 * cols), out(F32, cols, ff_rows), out(BF16, cols, ff_rows),
+             out(F32, at_rows, qkv_cols), out(BF16, 3, at_rows, qkv_cols), out(F32, q_cols, at_rows),
+             out(BF16, 3, q_cols, at_rows), out(BF16, 4, ff_rows, 2 * cols), out(BF16, 4, cols, ff_rows),
+             out(BF16, 4, ff_rows, qkv_cols), out(BF16, 4, q_cols, ff_rows)),
+            (VMEM_SPEC, VMEM_SPEC, VMEM_SPEC, ANY_SPEC, ANY_SPEC, ANY_SPEC, ANY_SPEC, VMEM_SPEC, ANY_SPEC, VMEM_SPEC,
+             *[ANY_SPEC] * 5),
             [v(rows, width), v(n_rows, width), v(n_rows, 2 * cols), v(cols, n_rows), v(2, n_rows, ff_rows),
              v(ff_rows, n_rows), v(8, rows, width), v(width, qkv_cols), v(q_cols, width), v(n_rows, qkv_cols),
              v(n_rows, q_cols), v(n_rows, q_cols), v(n_rows, qkv_cols),
@@ -1057,51 +1285,30 @@
              v(4 + len(spread_bits), 1, n_gain, dtype=F32), v(3 + len(spread_bits), 1, n_gain, dtype=F32),
              *scatter(ff_rows, 2 * cols), *scatter(cols, ff_rows), *scatter(ff_rows, qkv_cols),
              *scatter(q_cols, ff_rows)],
-            nbytes, 80, groups,
+            nbytes, 110, groups,
         )
-        pair = bit_of(lax.axis_index("fsdp"), PAIR)
-        c = lax.axis_index("ctx")
-
-        def feed(mine, other, axis):
-            return in_order(pair, mine, other.astype(F32), axis)
-
-        def heads(mine, other, axis):
-            other = other.astype(F32)
-            near = in_order(pair, mine, other[1], axis)
-            far = in_order(pair, other[0], other[2], axis)
-            return in_order(c, near, far, axis)
-
-        grad_w_gate = feed(feed_own[:, :cols], feed_other[:, :cols], 1).reshape(ff_rows, 2 * cols)
-        grad_w_up = feed(feed_own[:, cols:], feed_other[:, cols:], 1).reshape(ff_rows, 2 * cols)
-        grad_w_down = feed(down_own, down_other, 0).reshape(2 * cols, ff_rows)
-        grad_w_out = heads(out_own, out_other, 0).reshape(4 * q_cols, at_rows)
-
-        def columns(start, size):
-            at = slice(start, start + size)
-            return heads(qkv_own[:, at], qkv_other[:, :, at], 1).reshape(at_rows, 4 * size)
-
-        gains = gains[0]
-        return (
-            grad_input,
-            columns(0, q_cols),
-            columns(q_cols, kv_cols),
-            columns(q_cols + kv_cols, kv_cols),
-            grad_w_out,
-            grad_w_gate,
-            grad_w_up,
-            grad_w_down,
-            gains[:width],
-            gains[width : 2 * width],
-            gains[2 * width : 2 * width + d],
-            gains[2 * width + d :],
+        own_rows = out(F32, rows, width)
+        made = (
+            out(F32, at_rows, 4 * q_cols), out(F32, at_rows, 4 * kv_cols), out(F32, at_rows, 4 * kv_cols),
+            out(F32, 4 * q_cols, at_rows), out(F32, ff_rows, 2 * cols), out(F32, ff_rows, 2 * cols),
+            out(F32, 2 * cols, ff_rows), own_rows, own_rows, out(F32, 1, width), out(F32, 1, width), out(F32, 1, d),
+            out(F32, 1, d),
         )
+        pieces = pl.pallas_call(
+            join_kernel,
+            out_shape=made,
+            compiler_params=pltpu.CompilerParams(vmem_limit_bytes=40 << 20),
+            name="join_kernel",
+        )(feed_own, feed_other, down_own, down_other, qkv_own, qkv_other, out_own, out_other, grad_input, hidden_out, gains)
+        grads, (grad_input, hidden_out), gains = pieces[:7], pieces[7:9], pieces[9:]
+        return hidden_out, grad_input, *grads, *(g[0] for g in gains)
 
     def by_steps(
-        hidden_in, cotangent, residual_mid, gain_attn, gain_mlp, common, norm_two_part, normed_one, normed_two,
-        grad_rows, qkv, attended, full_qkv, full_out, grad_gate, grad_up, mixed, sizes,
+        hidden_in, cotangent, residual_mid, gain_attn, gain_mlp, common, norm_two_part, down_part, normed_one,
+        normed_two, grad_rows, qkv, attended, full_qkv, full_out, grad_gate, grad_up, mixed_t, sizes,
     ):
         rows, width = hidden_in.shape
-        (at_rows, ff_rows), ff_cols, q_cols = sizes, mixed.shape[1], attended.shape[1]
+        (at_rows, ff_rows), ff_cols, q_cols = sizes, mixed_t.shape[0], attended.shape[1]
         d = common[-1].shape[1]
         kv_cols = (qkv.shape[1] - q_cols) // 2
         groups = q_cols // kv_cols
@@ -1137,7 +1344,7 @@
 
         grad_w_gate = ff_grad(normed_two, grad_gate)
         grad_w_up = ff_grad(normed_two, grad_up)
-        grad_w_down = ff_grad(grad_rows, mixed).T
+        grad_w_down = ff_grad(grad_rows, mixed_t.T).T
 
         def attn_grad(acts, grads):
             v = weight_grad(acts, grads)
@@ -1172,7 +1379,16 @@
         for i in range(n.bit_length() - 1):
             gains = gains + swap(gains, 1 << i)
         gains = gains.reshape(-1)
+        teams = sorted(
+            sorted(i ^ b ^ p for b in range(4) for p in (0, PAIR_BIT))
+            for i in range(0, n, 4)
+            if not i & PAIR_BIT
+        )
+        hidden_out = residual_mid + lax.psum_scatter(
+            down_part, AXES, scatter_dimension=0, axis_index_groups=teams, tiled=True
+        ).astype(F32)
         return (
+            hidden_out,
             grad_input,
             grad_w_query,
             grad_w_key,

time: 524 us -> 475 us (0.906); the launches traced: 517 us -> 474 us
  Pallas kernels: 426 us -> 460 us
  matrix products: 30.7 us -> 0 us
  other arithmetic: 20.4 us -> 2.08 us
  between operations: 14.7 us -> 0.7 us
  local copies, waits for them, and re-layouts: 20.6 us -> 11.6 us
    dot_general x6 -> x0, matrix products: 30.7 us -> none  [the longest x3 16 us: dot_cols(): lax.dot_general(left, right, (((1,), (1,)), ((), ())), preferred_element_...]
    pallas_call x2, Pallas kernels: 426 us -> 456 us  [comm_call(): pl.pallas_call(functools.partial(kernel, bits, *more), out_shape=outs, in...]
    another operation x15 -> x0, other arithmetic: 7 us -> none  [in_order(): return jnp.stack([low, high], axis=axis)]
    convert_element_type x5 -> x1, other arithmetic: 6.17 us -> 0.01 us  [body(): angles = jnp.arange(length, dtype=jnp.int32).astype(F32)[:, None] * freqs]
    dot_general x2 -> x0, local copies, waits for them, and re-layouts: 5.91 us -> none  [dot(): lax.dot_general(left, right, (((1,), (0,)), ((), ())), preferred_element_...]
    unnamed x44 -> x22, local copies, waits for them, and re-layouts: 9.2 us -> 11.6 us
  transfers between devices with their start and end apart: 2 -> 0, of which waited for: 1 -> 0; matrix products, arithmetic and copies ran while one was open for 9% -> 0% of each run, Pallas kernels for 43% -> 0%
where the time goes in v4:
time: 475 us; the launch traced here: 474 us
  Pallas kernels  460 us (97%)
  local copies, waits for them, and re-layouts  11.6 us (2%)
    pallas_call x2, Pallas kernels, comm_call(): pl.pallas_call(functools.partial(kernel, bits, *more), out_shape=outs, in...  456 us
    unnamed x22, local copies, waits for them, and re-layouts  11.6 us

profile of v4, /device:TPU:0, one launch (start us, length us, event | category | flops | bytes accessed | tf_op | source)
XLA Modules:
  0.0 474.3 jit_solution(8726111696041981406)
XLA Ops:
  0.7 1.0 multiply_cosine_fusion
  1.7 1.1 pad_maximum_fusion.table
  2.7 212.8 %forward_kernel.1 = (f32[128,2048]{1,0:T(8,128)}, bf16[1024,2048]{1,0:T(8,128)(2,1)}, bf16[1024,2048]{1,0:T(8,128)(2,1)}, bf16[1024,2048]{1,0:T(8,128)(2,1)}, bf...) custom-call(bf16[128,2048]{1,0:T(8,128)(2,1)} %hidden.3, ...), custom_call_target="tpu_custom_call" | custom-call | flops 1342177280 | bytes 67108864 | tf_op jit(solution)/shard_map/forward_kernel/pallas_call | solution.py:1108
  215.5 243.3 %backward_kernel.1 = (f32[128,2048]{1,0:T(8,128)}, f32[128,2048]{1,0:T(8,128)}, f32[1,4352]{1,0:T(1,128)}, f32[256,1536]{1,0:T(8,128)}, bf16[256,1536]{1,0:T(8,1...) custom-call(f32[128,2048]{1,0:T(8,128)} %get-tuple-element.53.mid, ...), custom_call_target="tpu_custom_call" | custom-call | flops 838860800 | bytes 41943040 | tf_op jit(solution)/shard_map/backward_kernel/pallas_call | solution.py:1108
  458.8 0.0 copy-start
  458.8 1.4 copy-done
  460.2 0.0 copy-start.1
  460.2 1.2 copy-done.1
  461.4 0.0 copy-start.2
  461.4 1.2 copy-done.2
  462.6 0.0 copy-start.3
  462.6 1.1 copy-done.3
  463.8 0.0 copy-start.4
  463.8 1.1 copy-done.4
  464.9 0.0 copy-start.5
  464.9 1.0 copy-done.5
  465.9 0.0 copy-start.6
  465.9 1.0 copy-done.6
  466.9 0.0 copy-start.7
  466.9 0.9 copy-done.7
  467.9 0.0 copy-start.8
  467.9 0.9 copy-done.8
  468.8 0.0 copy-start.9
  468.8 0.9 copy-done.9
  469.7 0.0 copy-start.10
  469.7 0.7 copy-done.10
  470.4 3.9 join_kernel.1
  (2 shorter events, 0.0 us)
Async XLA Ops:
  458.8 1.4 copy-start
  460.2 1.2 copy-start.1
  461.4 1.2 copy-start.2
  462.6 1.1 copy-start.3
  463.8 1.1 copy-start.4
  464.9 1.0 copy-start.5
  465.9 1.0 copy-start.6
  466.9 0.9 copy-start.7
  467.9 0.9 copy-start.8
  468.8 0.9 copy-start.9
  469.7 0.7 copy-start.10

commit v5 on v4

--- a/solution.py
+++ b/solution.py
@@ -245,6 +245,38 @@
         self.waits[2] = self.moves.swap(
             self.sending.at[2], self.pair_in, self.pair_in, self.place.chips[2], self.open
         )
+
+    def fold(self):
+        for j, slot in ((3, 0), (1, 1), (2, 2)):
+            self.ready(j)
+
+            def body(at):
+                self.sending[slot, at] = self.two(j, at).astype(BF16)
+
+            row_loop(self.sending.shape[1], body)
+        self.ready(0)
+
+    def post_ctx(self):
+        self.waits = {}
+        for j, slot in ((3, 0), (1, 1)):
+            self.waits[j] = self.moves.swap(
+                self.sending.at[slot], self.ctx_in.at[slot], self.ctx_in.at[slot], self.place.chips[1], self.open
+            )
+
+    def post_pair(self):
+        self.waits[3]()
+
+        def body(at):
+            self.sending[2, at] = (self.sending[2, at].astype(F32) + self.ctx_in[0, at].astype(F32)).astype(BF16)
+
+        row_loop(self.sending.shape[1], body)
+        self.waits[2] = self.moves.swap(
+            self.sending.at[2], self.pair_in, self.pair_in, self.place.chips[2], self.open
+        )
+
+    def came(self):
+        for wait in (self.waits[1], self.waits[2], *self.open):
+            wait()
 
     def finish(self):
         self.ready(0)
@@ -545,6 +577,7 @@
     out_in[0] = moves.load(out_chunk(0), out_block(f0, c0))
     spread_one = Spread(moves, place, own_one, rows_one)
     swap_pair(0)
+    swap_pair(1)
     seg_wait()
     pair_first = place.pair == 0
     own_seg, far_seg = seg[...].astype(F32), seg_in[...].astype(F32)
@@ -574,25 +607,26 @@
     qkv_gather.middle()
     spread_one.from_ctx()
     send_feed(0)
-    swap_pair(1)
     out_gather.relay()
     spread_one.from_both()
     spread_one.finish()
+    send_feed(1)
+    swap_pair(2)
     qkv_gather.finish()
     step = 2 * rows
 
-    @pl.loop(0, n_rows // step)
+    wide = min(256, w_qkv.shape[1])
+
+    @pl.loop(0, w_qkv.shape[1] // wide)
     def _(i):
-        at = lanes(i * step, step)
-        qkv[at] = dot(rows_one[at], w_qkv[...]).astype(BF16)
+        at = lanes(i * wide, wide)
+        qkv[:, at] = dot(rows_one[...], w_qkv[:, at]).astype(BF16)
 
     moves.store(qkv, qkv_out)
     normed_stored = moves.load(rows_one, normed_one)
     moves.store(w_qkv, qkv_weight)
-    spread_cot = Spread(moves, place, cot, rows_cot)
     out_gather.middle()
     feed[0][0].relay()
-    send_feed(1)
 
     @pl.loop(0, 2)
     def _(s):
@@ -600,11 +634,15 @@
 
     moves.store(att, att_out)
     out_gather.finish()
-    swap_pair(2)
-
-    @pl.loop(0, 8)
+
+    def columns_of(weight, at):
+        return (dot, weight[:, at]) if natural else (dot_cols, weight[at])
+
+    @pl.loop(0, width // 256)
     def _(i):
-        part[i] = (dot if natural else dot_cols)(att[lanes(i * rows, rows)], w_out[...]).astype(BF16)
+        at = lanes(i * 256, 256)
+        times, block = columns_of(w_out, at)
+        part[:, :, at] = times(att[...], block).astype(BF16).reshape(8, rows, 256)
 
     moves.store(w_out, out_weight)
     collect = Collect(
@@ -613,10 +651,9 @@
     collect.to_ctx()
     feed[0][0].middle()
     feed[1][0].relay()
-    spread_cot.from_pair()
     collect.to_pair()
     send_feed(2)
-    spread_cot.from_ctx()
+    feed[1][0].middle()
     collect.finish()
 
     def norm_two(at):
@@ -627,12 +664,12 @@
 
     row_loop(rows, norm_two)
     spread_two = Spread(moves, place, own_two, rows_two)
-    feed[1][0].middle()
+    spread_cot = Spread(moves, place, cot, rows_cot)
     feed[2][0].relay()
-    spread_cot.from_both()
     spread_two.from_pair()
     spread_two.from_ctx()
     spread_two.from_both()
+    feed[2][0].middle()
     spread_two.finish()
     moves.store(rows_two, normed_two)
     for wait in own_feed:
@@ -644,9 +681,8 @@
         at = lanes(i * step, step)
         gate[at] = dot(rows_two[at], w_gate[...])
 
-    spread_cot.finish()
-    moves.store(rows_cot, cot_out)
-    feed[2][0].middle()
+    spread_cot.from_pair()
+    spread_cot.from_ctx()
     feed[1][0].finish()
 
     @pl.loop(0, n_rows // step)
@@ -660,6 +696,9 @@
         mixed_t[:, at] = mix.T.astype(BF16)
 
     moves.store(mixed_t, mixed_out)
+    spread_cot.from_both()
+    spread_cot.finish()
+    moves.store(rows_cot, cot_out)
     normed_stored()
     feed[2][0].finish()
 
@@ -675,17 +714,19 @@
     moves.store(grad_gate, grad_gate_out)
     moves.store(grad_up, grad_up_out)
 
-    @pl.loop(0, 8)
+    @pl.loop(0, width // 256)
     def _(i):
-        at = lanes(i * rows, rows)
-        part[i] = (dot_cols(grad_gate[at], w_gate[...]) + dot_cols(grad_up[at], w_up[...])).astype(BF16)
+        at = lanes(i * 256, 256)
+        both = dot_cols(grad_gate[...], w_gate[at]) + dot_cols(grad_up[...], w_up[at])
+        part[:, :, at] = both.astype(BF16).reshape(8, rows, 256)
 
     moves.store(part, part_out)
 
-    @pl.loop(0, 8)
+    @pl.loop(0, width // 256)
     def _(i):
-        at = lanes(i * rows, rows)
-        rows_one[at] = (dot if natural else dot_cols)(mixed[at], w_down[...]).astype(BF16)
+        at = lanes(i * 256, 256)
+        times, block = columns_of(w_down, at)
+        rows_one[:, at] = times(mixed[...], block).astype(BF16)
 
     moves.store(rows_one, down_out)
     moves.close()
@@ -752,9 +793,9 @@
 
 
 class Scatter:
-    def __init__(self, moves, place, product, out0, in0, out1, in1, acc, spare):
+    def __init__(self, moves, place, product, out0, in0, out1, in1, acc, acc_pair, spare):
         self.moves, self.place, self.product, self.spare = moves, place, product, spare
-        self.out0, self.in0, self.out1, self.in1, self.acc = out0, in0, out1, in1, acc
+        self.out0, self.in0, self.out1, self.in1, self.acc, self.acc_pair = out0, in0, out1, in1, acc, acc_pair
         self.low, self.high = place.bits[1], place.bits[0]
         self.order = [self.high, self.high | PAIR, 0, PAIR]
         self.first, self.second, self.leaving = {}, {}, {}
@@ -780,8 +821,10 @@
             value = value + self.in0[(i, *at)].astype(F32)
             if i < 2:
                 self.out1[(i, *at)] = value.astype(BF16)
+            elif i == 2:
+                self.acc[at] = value
             else:
-                self.acc[(i - 2, *at)] = value
+                self.acc_pair[at] = value.astype(BF16)
 
         self.product(self.order[i], emit)
         if i < 2:
@@ -795,13 +838,13 @@
 
     def take_high(self, i):
         self.second[i].arrive()
-        rows = self.acc.shape[1]
+        total = self.acc_pair if i else self.acc
         step = 64
 
-        @pl.loop(0, rows // step)
+        @pl.loop(0, total.shape[0] // step)
         def _(k):
             at = pl.ds(pl.multiple_of(k * step, step), step)
-            self.acc[i, at] += self.in1[i, at].astype(F32)
+            total[at] = (total[at].astype(F32) + self.in1[i, at].astype(F32)).astype(total.dtype)
 
     def close(self):
         for waits in self.leaving.values():
@@ -833,20 +876,20 @@
 
 def backward_kernel(
     bits, groups,
-    mid, hidden, cot, gain_attn, gain_mlp, starts, cos, sin, gain_q, gain_k,
-    part_two, part_hidden, normed_one, normed_two, cot_rows, qkv_in, att_in, qkv_weight, out_weight, grad_gate, grad_up,
+    cot, gain_attn, gain_mlp, starts, cos, sin, gain_q, gain_k,
+    mid, hidden, part_two, part_hidden, normed_one, normed_two, cot_rows, qkv_in, att_in, qkv_weight, out_weight, grad_gate, grad_up,
     mixed_t,
     grad_in, hidden_out, gains, feed_own, feed_other, down_own, down_other, qkv_own, qkv_other, out_own, out_other,
     spare_feed, spare_down, spare_qkv, spare_out,
     own, rows_mid, feed, mixed, lhs, lhs_t, part, w_qkv, w_out, qkv, att, datt, dqkv,
-    first, ctx_in, pair_in, sending, gain_a, gain_m, gain_h, tree, tree_in,
-    f_out0, f_in0, f_out1, f_in1, f_acc, d_out0, d_in0, d_out1, d_in1, d_acc,
-    q_out0, q_in0, q_out1, q_in1, q_acc, o_out0, o_in0, o_out1, o_in1, o_acc,
+    first, ctx_in, pair_in, sending, first_h, ctx_h, pair_h, sending_h, gain_a, gain_m, gain_h, tree, tree_in,
+    f_out0, f_in0, f_out1, f_in1, f_acc, f_pair, d_out0, d_in0, d_out1, d_in1, d_acc, d_pair,
+    q_out0, q_in0, q_out1, q_in1, q_acc, q_pair, o_out0, o_in0, o_out1, o_in1, o_acc, o_pair,
     send, recv, local,
 ):
     place = Place(bits)
     moves = Moves(send, recv, local)
-    rows, width = hidden.shape
+    rows, width = cot.shape
     cols = mixed.shape[0]
     tile = lhs.shape[2]
     half = tile // 2
@@ -856,6 +899,7 @@
     def lanes(start, size):
         return pl.ds(pl.multiple_of(start, size), size)
 
+    ready_mid = moves.load(mid, hidden_out)
     ready_feed = [
         moves.load(grad_gate, feed.at[:, pl.ds(0, cols)]),
         moves.load(grad_up, feed.at[:, pl.ds(cols, cols)]),
@@ -865,14 +909,14 @@
     )
     masks = [high, high | PAIR, 0, PAIR]
     sends = [m | low for m in masks]
+    a, b, c, e = range(4)
     order = [
-        (cot_rows, sends[0]), (cot_rows, sends[1]), (normed_two, sends[0]), (cot_rows, masks[0]),
-        (normed_two, sends[1]), (cot_rows, masks[1]), (normed_two, masks[0]),
-        (cot_rows, sends[2]), (cot_rows, sends[3]), (normed_two, sends[2]), (normed_two, sends[3]),
-        (normed_two, masks[1]),
-        (normed_one, sends[0]), (normed_one, sends[1]), (cot_rows, masks[2]), (cot_rows, masks[3]),
-        (normed_one, sends[2]), (normed_one, sends[3]), (normed_two, masks[2]), (normed_two, masks[3]),
-        *[(normed_one, m) for m in masks],
+        (cot_rows, sends[a]), (cot_rows, sends[b]), (normed_two, sends[a]), (cot_rows, masks[a]),
+        (normed_two, sends[b]), (cot_rows, masks[b]), (normed_two, masks[a]), (cot_rows, sends[e]),
+        (cot_rows, sends[c]), (normed_two, sends[e]), (normed_two, masks[b]), (normed_one, sends[a]),
+        (normed_one, sends[b]), (normed_one, sends[e]), (cot_rows, masks[e]), (cot_rows, masks[c]),
+        (normed_two, masks[e]), (normed_two, sends[c]), (normed_one, sends[c]), (normed_one, masks[a]),
+        (normed_one, masks[b]), (normed_one, masks[e]), (normed_two, masks[c]), (normed_one, masks[c]),
     ]
     blocks = Blocks(moves, place, lhs, order)
     ready_mixed = moves.load(mixed_t, mixed)
@@ -908,156 +952,184 @@
         at = lanes(place.block(mask) * tile, tile)
         emit((slice(None), slice(None)), dot_rows(att[...], rows_mid[:, at]))
 
-    feed_s = Scatter(moves, place, by_rows(normed_two, feed), f_out0, f_in0, f_out1, f_in1, f_acc, spare_feed)
-    down_s = Scatter(moves, place, down_product, d_out0, d_in0, d_out1, d_in1, d_acc, spare_down)
-    qkv_s = Scatter(moves, place, by_rows(normed_one, dqkv), q_out0, q_in0, q_out1, q_in1, q_acc, spare_qkv)
-    out_s = Scatter(moves, place, out_product, o_out0, o_in0, o_out1, o_in1, o_acc, spare_out)
+    feed_s = Scatter(moves, place, by_rows(normed_two, feed), f_out0, f_in0, f_out1, f_in1, f_acc, f_pair, spare_feed)
+    down_s = Scatter(moves, place, down_product, d_out0, d_in0, d_out1, d_in1, d_acc, d_pair, spare_down)
+    qkv_s = Scatter(moves, place, by_rows(normed_one, dqkv), q_out0, q_in0, q_out1, q_in1, q_acc, q_pair, spare_qkv)
+    out_s = Scatter(moves, place, out_product, o_out0, o_in0, o_out1, o_in1, o_acc, o_pair, spare_out)
 
     ready_mixed()
-    down_s.send(0)
-    down_s.send(1)
+    down_s.send(a)
+    down_s.send(b)
     collect_two.to_ctx()
     for wait in ready_feed:
         wait()
-    feed_s.send(0)
-    down_s.take(0)
+    feed_s.send(a)
+    down_s.take(a)
+    feed_s.send(b)
     collect_two.to_pair()
-    feed_s.send(1)
-    down_s.relay(0)
-    down_s.take(1)
+    collect_hidden = Collect(
+        moves, place, lambda j, t: part_hidden.at[place.rows_of[j] + t], part.at[pl.ds(4, 4)],
+        first_h, ctx_h, pair_h, sending_h, True,
+    )
+    down_s.relay(a)
+    down_s.take(b)
+
+    collect_hidden.fold()
+    ready_mid()
     collect_two.finish()
     gain_m[...] = jnp.zeros_like(gain_m)
     gain_a[...] = jnp.zeros_like(gain_a)
     gain_h[...] = jnp.zeros_like(gain_h)
 
     def back_two(at):
-        g = cot[at].astype(F32) + norm_back(collect_two.total(at), mid[at], gain_mlp[...], gain_m)
+        x = hidden_out[at]
+        g = cot[at].astype(F32) + norm_back(collect_two.total(at), x, gain_mlp[...], gain_m)
+        hidden_out[at] = x + collect_hidden.two(0, at)
         grad_in[at] = g
         own[at] = g.astype(BF16)
 
     row_loop(rows, back_two)
     spread = Spread(moves, place, own, rows_mid)
-    feed_s.take(0)
-    down_s.relay(1)
+    down_s.relay(b)
+    feed_s.take(a)
+    down_s.send(e)
     spread.from_pair()
-    down_s.send(2)
-    down_s.send(3)
+    down_s.send(c)
     spread.from_ctx()
-    feed_s.send(2)
-    feed_s.send(3)
+    feed_s.send(e)
+    feed_s.relay(a)
     spread.from_both()
-    feed_s.relay(0)
     for wait in ready_late:
         wait()
     spread.finish()
-
-    @pl.loop(0, 8 // 2)
+    ready_hidden = moves.load(hidden, own)
+    collect_hidden.post_ctx()
+
+    @pl.loop(0, 4)
     def _(i):
         at = lanes(i * 2 * rows, 2 * rows)
         datt[at] = dot_cols(rows_mid[at], w_out[...]).astype(BF16)
 
-    feed_s.take(1)
+    feed_s.take(b)
 
     @pl.loop(0, 2)
     def _(s):
         attend_back_one(groups, s, qkv, att, datt, starts, cos, sin, gain_q, gain_k, dqkv, gain_h)
 
-    @pl.loop(0, 8)
+    @pl.loop(0, width // tile)
     def _(i):
-        part[i] = dot_cols(dqkv[lanes(i * rows, rows)], w_qkv[...]).astype(BF16)
+        at = lanes(i * tile, tile)
+        part[:, :, at] = dot_cols(dqkv[...], w_qkv[at]).astype(BF16).reshape(8, rows, tile)
 
     collect_one = Collect(
         moves, place, lambda j, t: part.at[place.rows_of[j] + t], None, first, ctx_in, pair_in, sending, False
     )
-    qkv_s.send(0)
-    qkv_s.send(1)
-    out_s.send(0)
-    out_s.send(1)
+    qkv_s.send(a)
+    qkv_s.send(b)
+    out_s.send(a)
+    out_s.send(b)
     collect_one.to_ctx()
-    feed_s.relay(1)
-    down_s.take(2)
-    down_s.take(3)
+    feed_s.relay(b)
+    collect_hidden.post_pair()
+    qkv_s.send(e)
+    out_s.send(e)
+    down_s.take(e)
+    down_s.take(c)
+    feed_s.take(e)
     collect_one.to_pair()
-    qkv_s.send(2)
-    qkv_s.send(3)
-    out_s.send(2)
-    out_s.send(3)
+    feed_s.send(c)
+    qkv_s.send(c)
+    out_s.send(c)
+    qkv_s.take(a)
+    qkv_s.take(b)
+    out_s.take(a)
+    out_s.take(b)
     collect_one.finish()
 
+    ready_hidden()
+
     def back_one(at):
-        grad_in[at] += norm_back(collect_one.total(at), hidden[at].astype(F32), gain_attn[...], gain_a)
+        grad_in[at] += norm_back(collect_one.total(at), own[at].astype(F32), gain_attn[...], gain_a)
 
     row_loop(rows, back_one)
-    feed_s.take(2)
-    feed_s.take(3)
-    qkv_s.take(0)
-    qkv_s.take(1)
-    out_s.take(0)
-    out_s.take(1)
-    qkv_s.relay(0)
-    qkv_s.relay(1)
-    out_s.relay(0)
-    out_s.relay(1)
 
     d = gain_q.shape[1]
     tree[0, :, 0:width] = jnp.sum(gain_a[...], axis=0, keepdims=True)
     tree[0, :, width : 2 * width] = jnp.sum(gain_m[...], axis=0, keepdims=True)
     tree[0, :, 2 * width : 2 * width + d] = jnp.sum(gain_h[0], axis=0, keepdims=True)
     tree[0, :, 2 * width + d : 2 * width + 2 * d] = jnp.sum(gain_h[1], axis=0, keepdims=True)
-    for k, device in enumerate([place.sibling, place.chips[1], place.chips[2], *[place.along(b) for b in bits]]):
-        moves.swap(tree.at[k], tree_in.at[k], tree_in.at[k], device)()
-        tree[k + 1] = tree[k] + tree_in[k]
-    gains[...] = tree[3 + len(bits)]
-    collect_hidden = Collect(
-        moves, place, lambda j, t: part_hidden.at[place.rows_of[j] + t], part, first, ctx_in, pair_in, sending, True
-    )
-    collect_hidden.to_ctx()
+    partners = [place.sibling, place.chips[1], *[place.along(x) for x in bits], place.chips[2]]
+    tree_waits = []
+
+    def climb():
+        k = len(tree_waits)
+        if k:
+            tree_waits[-1]()
+            tree[k] = tree[k - 1] + tree_in[k - 1]
+        if k < len(partners):
+            tree_waits.append(moves.swap(tree.at[k], tree_in.at[k], tree_in.at[k], partners[k]))
+
     finals = []
 
-    def feed_final(scatter, mine, other):
+    def pair_final(scatter, other):
         scatter.take_high(1)
-        pair_out = scatter.in0.at[0]
-        n, step = pair_out.shape[0], 64
-
-        @pl.loop(0, n // step)
-        def _(k):
-            at = lanes(k * step, step)
-            pair_out[at] = scatter.acc[1, at].astype(BF16)
-
-        finals.append(moves.swap(pair_out, other, other, place.chips[2]))
+        finals.append(moves.swap(scatter.acc_pair, other, other, place.chips[2]))
+
+    def own_final(scatter, mine):
         scatter.take_high(0)
-        moves.store(scatter.acc.at[0], mine)
-
-    def mates_final(scatter, piece, spare, mine, other):
-        scatter.take_high(1)
-        scatter.take_high(0)
-        for j in (3, 2, 1):
+        moves.store(scatter.acc, mine)
+
+    def mates_final(scatter, slot, piece, spare, other):
+        scatter.take_high(slot)
+        for j in (3, 2) if slot else (1,):
             out = spare(j)
-            out[...] = piece(j // 2, place.at[j][1]).astype(BF16)
+            out[...] = piece(slot, place.at[j][1]).astype(BF16)
             finals.append(moves.swap(out, other.at[j - 1], other.at[j - 1], place.chips[j]))
-        mine[...] = piece(0, place.c)
-
-    feed_final(down_s, down_own, down_other)
-    collect_hidden.to_pair()
-    qkv_s.take(2)
-    qkv_s.take(3)
-    out_s.take(2)
-    out_s.take(3)
-    collect_hidden.finish()
-
-    def add_hidden(at):
-        hidden_out[at] = mid[at] + collect_hidden.total(at)
-
-    row_loop(rows, add_hidden)
-    feed_final(feed_s, feed_own, feed_other)
-    mates_final(
-        qkv_s, lambda slot, c: q_acc[slot, lanes(c * half, half)],
-        lambda j: q_in0.at[j, pl.ds(0, half)], qkv_own, qkv_other,
-    )
-    mates_final(
-        out_s, lambda slot, c: o_acc[slot, :, lanes(c * half, half)],
-        lambda j: o_in0.at[j, :, pl.ds(0, half)], out_own, out_other,
-    )
+
+    def qkv_piece(slot, c):
+        return (q_pair if slot else q_acc)[lanes(c * half, half)]
+
+    def out_piece(slot, c):
+        return (o_pair if slot else o_acc)[:, lanes(c * half, half)]
+
+    def qkv_spare(j):
+        return q_in0.at[j, pl.ds(0, half)]
+
+    def out_spare(j):
+        return o_in0.at[j, :, pl.ds(0, half)]
+
+    climb()
+    qkv_s.relay(a)
+    qkv_s.relay(b)
+    out_s.relay(a)
+    out_s.relay(b)
+    climb()
+    pair_final(down_s, down_other)
+    climb()
+    own_final(down_s, down_own)
+    qkv_s.take(e)
+    out_s.take(e)
+    climb()
+    collect_hidden.came()
+
+    def end_hidden(at):
+        hidden_out[at] += ctx_h[1, at].astype(F32) + pair_h[at].astype(F32)
+
+    row_loop(rows, end_hidden)
+    pair_final(feed_s, feed_other)
+    climb()
+    feed_s.take(c)
+    qkv_s.take(c)
+    out_s.take(c)
+    mates_final(qkv_s, 1, qkv_piece, qkv_spare, qkv_other)
+    mates_final(out_s, 1, out_piece, out_spare, out_other)
+    own_final(feed_s, feed_own)
+    mates_final(qkv_s, 0, qkv_piece, qkv_spare, qkv_other)
+    mates_final(out_s, 0, out_piece, out_spare, out_other)
+    qkv_own[...] = qkv_piece(0, place.c)
+    out_own[...] = out_piece(0, place.c)
+    climb()
+    gains[...] = tree[len(partners)]
     for scatter in (feed_s, down_s, qkv_s, out_s):
         scatter.close()
     for wait in finals:
@@ -1258,7 +1330,7 @@
             return pltpu.VMEM(dims, dtype)
 
         def scatter(*block):
-            return [v(2, *block), v(4, *block), v(2, *block), v(2, *block), v(2, *block, dtype=F32)]
+            return [v(2, *block), v(4, *block), v(2, *block), v(2, *block), v(*block, dtype=F32), v(*block)]
 
         n_gain = 2 * width + 2 * d
         nbytes = n_rows * width * 20
@@ -1267,10 +1339,10 @@
             out_other, *_,
         ) = comm_call(
             backward_kernel, spread_bits, 2,
-            (residual_mid, hidden_in, cotangent, gain_attn[None], gain_mlp[None], *common, norm_two_part,
+            (cotangent, gain_attn[None], gain_mlp[None], *common, residual_mid, hidden_in, norm_two_part,
              down_part.reshape(8, rows, width), normed_one, normed_two, grad_rows, qkv, attended, full_qkv, full_out,
              grad_gate, grad_up, mixed_t),
-            [VMEM_SPEC] * 10 + [ANY_SPEC] * 12,
+            [VMEM_SPEC] * 8 + [ANY_SPEC] * 14,
             (out(F32, rows, width), out(F32, rows, width), out(F32, 1, n_gain), out(F32, ff_rows, 2 * cols),
              out(BF16, ff_rows, 2 * cols), out(F32, cols, ff_rows), out(BF16, cols, ff_rows),
              out(F32, at_rows, qkv_cols), out(BF16, 3, at_rows, qkv_cols), out(F32, q_cols, at_rows),
@@ -1281,7 +1353,7 @@
             [v(rows, width), v(n_rows, width), v(n_rows, 2 * cols), v(cols, n_rows), v(2, n_rows, ff_rows),
              v(ff_rows, n_rows), v(8, rows, width), v(width, qkv_cols), v(q_cols, width), v(n_rows, qkv_cols),
              v(n_rows, q_cols), v(n_rows, q_cols), v(n_rows, qkv_cols),
-             *collect_buffers(rows, width), v(8, width, dtype=F32), v(8, width, dtype=F32), v(2, 8, d, dtype=F32),
+             *collect_buffers(rows, width), *collect_buffers(rows, width), v(8, width, dtype=F32), v(8, width, dtype=F32), v(2, 8, d, dtype=F32),
              v(4 + len(spread_bits), 1, n_gain, dtype=F32), v(3 + len(spread_bits), 1, n_gain, dtype=F32),
              *scatter(ff_rows, 2 * cols), *scatter(cols, ff_rows), *scatter(ff_rows, qkv_cols),
              *scatter(q_cols, ff_rows)],
@@ -1297,7 +1369,7 @@
         pieces = pl.pallas_call(
             join_kernel,
             out_shape=made,
-            compiler_params=pltpu.CompilerParams(vmem_limit_bytes=40 << 20),
+            compiler_params=pltpu.CompilerParams(vmem_limit_bytes=61 << 20),
             name="join_kernel",
         )(feed_own, feed_other, down_own, down_other, qkv_own, qkv_other, out_own, out_other, grad_input, hidden_out, gains)
         grads, (grad_input, hidden_out), gains = pieces[:7], pieces[7:9], pieces[9:]

time: 475 us -> 434 us (0.914)
  Pallas kernels: 460 us -> 431 us
  local copies, waits for them, and re-layouts: 11.6 us -> 0 us
    pallas_call x2, Pallas kernels: 456 us -> 424 us  [comm_call(): pl.pallas_call(functools.partial(kernel, bits, *more), out_shape=outs, in...]
    unnamed x22 -> x0, local copies, waits for them, and re-layouts: 11.6 us -> none
where the time goes in v5:
time: 434 us
  Pallas kernels  431 us (99%)
    pallas_call x2, Pallas kernels, comm_call(): pl.pallas_call(functools.partial(kernel, bits, *more), out_shape=outs, in...  424 us

profile of v5, /device:TPU:0, one launch (start us, length us, event | category | flops | bytes accessed | tf_op | source)
XLA Modules:
  0.0 433.9 jit_solution(7419191692350896649)
XLA Ops:
  0.7 1.0 multiply_cosine_fusion
  1.7 1.1 pad_maximum_fusion.table
  2.7 217.6 %forward_kernel.1 = (f32[128,2048]{1,0:T(8,128)}, bf16[1024,2048]{1,0:T(8,128)(2,1)}, bf16[1024,2048]{1,0:T(8,128)(2,1)}, bf16[1024,2048]{1,0:T(8,128)(2,1)}, bf...) custom-call(bf16[128,2048]{1,0:T(8,128)(2,1)} %hidden.3, ...), custom_call_target="tpu_custom_call" | custom-call | flops 1342177280 | bytes 67108864 | tf_op jit(solution)/shard_map/forward_kernel/pallas_call | solution.py:1180
  220.3 206.8 %backward_kernel.1 = (f32[128,2048]{1,0:T(8,128)}, f32[128,2048]{1,0:T(8,128)}, f32[1,4352]{1,0:T(1,128)}, f32[256,1536]{1,0:T(8,128)}, bf16[256,1536]{1,0:T(8,1...) custom-call(bf16[128,2048]{1,0:T(8,128)(2,1)} %cot.3, ...), custom_call_target="tpu_custom_call" | custom-call | flops 838860800 | bytes 41943040 | tf_op jit(solution)/shard_map/backward_kernel/pallas_call | solution.py:1180
  427.1 6.6 %join_kernel.1 = (f32[128,1024]{1,0:T(8,128)}, f32[128,512]{1,0:T(8,128)}, f32[128,512]{1,0:T(8,128)}, f32[1024,128]{1,0:T(8,128)}, f32[256,1536]{1,0:T(8,128)},...) custom-call(f32[256,1536]{1,0:T(8,128)} %get-tuple-element.69.feed_o, ...), custom_call_target="tpu_custom_call" | custom-call | tf_op jit(solution)/shard_map/join_kernel/pallas_call | solution.py:1369
  (2 shorter events, 0.0 us)

commit v6 on v5

--- a/solution.py
+++ b/solution.py
@@ -340,16 +340,21 @@
             out += [m | b for m in out]
         return [m | self.place.bits[stage] for m in out]
 
-    def relay(self):
-        for m in list(self.crosses):
-            self.crosses.pop(m).relay()
+    def relay(self, m):
+        if self.place.relay:
+            self.crosses[m].relay()
+
+    def hop(self, m):
+        if self.place.relay:
+            self.pass_on(m | self.place.bits[0])
+        elif m == PAIR:
+            self.middle()
 
     def pass_on(self, m):
         self.waits.pop(m)()
         self.forward(m)
 
     def middle(self):
-        self.relay()
         for stage in range(len(self.place.bits) - 1):
             for m in self.masks(stage):
                 if m in self.waits:
@@ -510,6 +515,81 @@
     )
     f0, c0, _ = place.at[0]
     qkv_in, out_in = {}, {}
+
+    def rows_block(w):
+        return lambda f: w.at[lanes(f * ff_rows, ff_rows)]
+
+    def cols_block(w):
+        return lambda f: w.at[:, lanes(f * ff_rows, ff_rows)]
+
+    mine, theirs = lanes(place.pair * ff_cols, ff_cols), lanes((1 - place.pair) * ff_cols, ff_cols)
+    feed = [
+        (Gather(moves, place, rows_block(w_gate), spare_gate), wg.at[:, mine], wg.at[:, theirs]),
+        (Gather(moves, place, rows_block(w_up), spare_up), wu.at[:, mine], wu.at[:, theirs]),
+        (Gather(moves, place, cols_block(w_down), spare_down), wd.at[mine], wd.at[theirs])
+        if natural
+        else (Gather(moves, place, rows_block(w_down), spare_down), wd.at[:, mine], wd.at[:, theirs]),
+    ]
+    own_feed = [moves.load(own, gather.block(place.f)) for gather, own, _ in feed]
+
+    def swap_pair(i):
+        gather, _, other = feed[i]
+        gather.waits[PAIR] = moves.swap(
+            other, gather.block(place.f), gather.block(place.block(PAIR)), place.along(PAIR)
+        )
+
+    def send_feed(i):
+        gather, own, _ = feed[i]
+        gather.forward(0, own)
+        gather.pass_on(PAIR)
+
+    step = 2 * rows
+    wide = min(256, w_qkv.shape[1])
+    qkv_gather = Gather(moves, place, lambda f: w_qkv.at[qkv_rows(f)], spare_qkv)
+    out_gather = Gather(moves, place, out_block, spare_out)
+
+    def norm_one(at):
+        unit, _ = unit_and_scale(hidden[at].astype(F32))
+        own_one[at] = (unit * gain_attn[...]).astype(BF16)
+
+    def norm_two(at):
+        x = hidden[at].astype(F32) + collect.total(at)
+        mid[at] = x
+        unit, _ = unit_and_scale(x)
+        own_two[at] = (unit * gain_mlp[...]).astype(BF16)
+
+    def columns_of(weight, at):
+        return (dot, weight[:, at]) if natural else (dot_cols, weight[at])
+
+    def attend_part(s):
+        attend_one(groups, s, qkv, starts, cos, sin, gain_q, gain_k, att)
+
+    def gate_part(i):
+        at = pl.ds(i * step, step)
+        gate[at] = dot(rows_two[at], w_gate[...])
+
+    def up_part(i):
+        at = pl.ds(i * step, step)
+        u = dot(rows_two[at], w_up[...])
+        up[at] = u
+        g = gate[at]
+        mix = g * jax.nn.sigmoid(g) * u
+        mixed[at] = mix.astype(BF16)
+        mixed_t[:, at] = mix.T.astype(BF16)
+
+    def back_part(i):
+        at = pl.ds(i * step, step)
+        m = (dot_cols if natural else dot)(rows_cot[at], w_down[...])
+        g = gate[at]
+        s = jax.nn.sigmoid(g)
+        grad_gate[at] = (m * up[at] * s * (1.0 + g * (1.0 - s))).astype(BF16)
+        grad_up[at] = (m * (g * s)).astype(BF16)
+
+    for j in (3, 2, 1):
+        fj, cj, _ = place.at[j]
+        out_in[j] = moves.swap(out_chunk(j), out_block(f0, c0), out_block(fj, cj), place.chips[j])
+    out_in[0] = moves.load(out_chunk(0), out_block(f0, c0))
+    row_loop(rows, norm_one)
     for j in (1, 3, 2):
         fj, cj, _ = place.at[j]
         qkv_in[j] = [
@@ -525,59 +605,37 @@
         moves.load(w.at[:, lanes(place.chunk_of[0] * size, size)], w_qkv.at[qkv_rows(f0, c0), to])
         for w, size, to in pieces
     ]
+    out_in[0]()
+    out_in[1]()
+    out_gather.forward(0)
+    for wait in (*qkv_in[0], *qkv_in[1]):
+        wait()
+    qkv_gather.forward(0)
+    spread_one = Spread(moves, place, own_one, rows_one)
+    qkv_gather.relay(0)
+    spread_one.from_ctx()
+    out_gather.relay(0)
+    out_in[2]()
+    out_in[3]()
+    out_gather.forward(PAIR)
+    for wait in (*qkv_in[2], *qkv_in[3]):
+        wait()
+    qkv_gather.forward(PAIR)
+    feed[0][0].forward(0, feed[0][1])
+    out_gather.hop(0)
+    spread_cot = Spread(moves, place, cot, rows_cot)
     seg_wait = moves.swap(seg, seg_in, seg_in, place.chips[2])
-
-    def norm_one(at):
-        unit, _ = unit_and_scale(hidden[at].astype(F32))
-        own_one[at] = (unit * gain_attn[...]).astype(BF16)
-
-    row_loop(rows, norm_one)
-    def rows_block(w):
-        return lambda f: w.at[lanes(f * ff_rows, ff_rows)]
-
-    def cols_block(w):
-        return lambda f: w.at[:, lanes(f * ff_rows, ff_rows)]
-
-    mine, theirs = lanes(place.pair * ff_cols, ff_cols), lanes((1 - place.pair) * ff_cols, ff_cols)
-    feed = [
-        (Gather(moves, place, rows_block(w_gate), spare_gate), wg.at[:, mine], wg.at[:, theirs]),
-        (Gather(moves, place, rows_block(w_up), spare_up), wu.at[:, mine], wu.at[:, theirs]),
-        (Gather(moves, place, cols_block(w_down), spare_down), wd.at[mine], wd.at[theirs])
-        if natural
-        else (Gather(moves, place, rows_block(w_down), spare_down), wd.at[:, mine], wd.at[:, theirs]),
-    ]
-    own_feed = [moves.load(own, gather.block(place.f)) for gather, own, _ in feed]
-
-    def swap_pair(i):
-        gather, _, other = feed[i]
-        gather.waits[PAIR] = moves.swap(
-            other, gather.block(place.f), gather.block(place.block(PAIR)), place.along(PAIR)
-        )
-
-    def send_feed(i):
-        gather, own, _ = feed[i]
-        gather.forward(0, own)
-        gather.pass_on(PAIR)
-
-    qkv_gather = Gather(moves, place, lambda f: w_qkv.at[qkv_rows(f)], spare_qkv)
-    out_gather = Gather(moves, place, out_block, spare_out)
-
-    def send_attn(gather, arrivals):
-        for wait in (*arrivals[0], *arrivals[1]):
-            wait()
-        gather.forward(0)
-        for wait in (*arrivals[2], *arrivals[3]):
-            wait()
-        gather.forward(PAIR)
-
-    send_attn(qkv_gather, qkv_in)
-    for j in (3, 2, 1):
-        fj, cj, _ = place.at[j]
-        out_in[j] = moves.swap(out_chunk(j), out_block(f0, c0), out_block(fj, cj), place.chips[j])
-    out_in[0] = moves.load(out_chunk(0), out_block(f0, c0))
-    spread_one = Spread(moves, place, own_one, rows_one)
+    spread_one.from_pair()
+    out_gather.relay(PAIR)
+    qkv_gather.hop(0)
+    qkv_gather.relay(PAIR)
+    feed[0][0].relay(0)
+    out_gather.hop(PAIR)
+    qkv_gather.hop(PAIR)
     swap_pair(0)
-    swap_pair(1)
+    spread_one.from_both()
+    spread_cot.from_pair()
+    feed[1][0].forward(0, feed[1][1])
     seg_wait()
     pair_first = place.pair == 0
     own_seg, far_seg = seg[...].astype(F32), seg_in[...].astype(F32)
@@ -601,119 +659,91 @@
     moves.store(starts, starts_out)
     moves.store(cos, cos_out)
     moves.store(sin, sin_out)
-    qkv_gather.relay()
-    spread_one.from_pair()
-    send_attn(out_gather, {j: [w] for j, w in out_in.items()})
-    qkv_gather.middle()
-    spread_one.from_ctx()
-    send_feed(0)
-    out_gather.relay()
-    spread_one.from_both()
+    swap_pair(1)
     spread_one.finish()
-    send_feed(1)
-    swap_pair(2)
+    normed_stored = moves.load(rows_one, normed_one)
+    out_gather.finish()
+    moves.store(w_out, out_weight)
     qkv_gather.finish()
-    step = 2 * rows
-
-    wide = min(256, w_qkv.shape[1])
-
+    moves.store(w_qkv, qkv_weight)
     @pl.loop(0, w_qkv.shape[1] // wide)
     def _(i):
         at = lanes(i * wide, wide)
         qkv[:, at] = dot(rows_one[...], w_qkv[:, at]).astype(BF16)
 
     moves.store(qkv, qkv_out)
-    normed_stored = moves.load(rows_one, normed_one)
-    moves.store(w_qkv, qkv_weight)
-    out_gather.middle()
-    feed[0][0].relay()
-
-    @pl.loop(0, 2)
-    def _(s):
-        attend_one(groups, s, qkv, starts, cos, sin, gain_q, gain_k, att)
-
+    attend_part(0)
+    attend_part(1)
     moves.store(att, att_out)
-    out_gather.finish()
-
-    def columns_of(weight, at):
-        return (dot, weight[:, at]) if natural else (dot_cols, weight[at])
-
+    feed[0][0].pass_on(PAIR)
+    feed[1][0].relay(0)
     @pl.loop(0, width // 256)
     def _(i):
         at = lanes(i * 256, 256)
         times, block = columns_of(w_out, at)
         part[:, :, at] = times(att[...], block).astype(BF16).reshape(8, rows, 256)
 
-    moves.store(w_out, out_weight)
     collect = Collect(
         moves, place, lambda j, t: part.at[place.rows_of[j] + t], None, first, ctx_in, pair_in, sending, False
     )
+    feed[0][0].hop(0)
     collect.to_ctx()
-    feed[0][0].middle()
-    feed[1][0].relay()
+    feed[0][0].relay(PAIR)
+    feed[2][0].forward(0, feed[2][1])
     collect.to_pair()
-    send_feed(2)
-    feed[1][0].middle()
+    spread_cot.from_ctx()
+    feed[1][0].pass_on(PAIR)
+    feed[0][0].hop(PAIR)
+    swap_pair(2)
     collect.finish()
-
-    def norm_two(at):
-        x = hidden[at].astype(F32) + collect.total(at)
-        mid[at] = x
-        unit, _ = unit_and_scale(x)
-        own_two[at] = (unit * gain_mlp[...]).astype(BF16)
-
+    feed[2][0].relay(0)
     row_loop(rows, norm_two)
     spread_two = Spread(moves, place, own_two, rows_two)
-    spread_cot = Spread(moves, place, cot, rows_cot)
-    feed[2][0].relay()
-    spread_two.from_pair()
-    spread_two.from_ctx()
-    spread_two.from_both()
-    feed[2][0].middle()
-    spread_two.finish()
-    moves.store(rows_two, normed_two)
-    for wait in own_feed:
-        wait()
-    feed[0][0].finish()
-
-    @pl.loop(0, n_rows // step)
-    def _(i):
-        at = lanes(i * step, step)
-        gate[at] = dot(rows_two[at], w_gate[...])
-
-    spread_cot.from_pair()
-    spread_cot.from_ctx()
-    feed[1][0].finish()
-
-    @pl.loop(0, n_rows // step)
-    def _(i):
-        at = lanes(i * step, step)
-        u = dot(rows_two[at], w_up[...])
-        up[at] = u
-        g = gate[at]
-        mix = g * jax.nn.sigmoid(g) * u
-        mixed[at] = mix.astype(BF16)
-        mixed_t[:, at] = mix.T.astype(BF16)
-
-    moves.store(mixed_t, mixed_out)
     spread_cot.from_both()
     spread_cot.finish()
     moves.store(rows_cot, cot_out)
+    feed[1][0].hop(0)
+    spread_two.from_ctx()
+    feed[2][0].pass_on(PAIR)
+    feed[2][0].hop(0)
+    feed[1][0].relay(PAIR)
+    spread_two.from_pair()
+    feed[2][0].relay(PAIR)
+    own_feed[0]()
+    feed[0][0].finish()
+    feed[1][0].hop(PAIR)
+    spread_two.from_both()
+    feed[2][0].hop(PAIR)
+    spread_two.finish()
+    moves.store(rows_two, normed_two)
+    gate_part(0)
+    gate_part(1)
+    own_feed[1]()
+    feed[1][0].finish()
+    up_part(0)
+    gate_part(2)
+    up_part(1)
+    gate_part(3)
+    up_part(2)
+    up_part(3)
+    moves.store(mixed_t, mixed_out)
+    own_feed[2]()
+    feed[2][0].finish()
     normed_stored()
-    feed[2][0].finish()
-
-    @pl.loop(0, n_rows // step)
+
+    @pl.loop(0, width // 256)
     def _(i):
-        at = lanes(i * step, step)
-        m = (dot_cols if natural else dot)(rows_cot[at], w_down[...])
-        g = gate[at]
-        s = jax.nn.sigmoid(g)
-        grad_gate[at] = (m * up[at] * s * (1.0 + g * (1.0 - s))).astype(BF16)
-        grad_up[at] = (m * (g * s)).astype(BF16)
-
+        at = lanes(i * 256, 256)
+        times, block = columns_of(w_down, at)
+        rows_one[:, at] = times(mixed[...], block).astype(BF16)
+
+    moves.store(rows_one, down_out)
+    back_part(0)
+    back_part(1)
+    back_part(2)
+    back_part(3)
     moves.store(grad_gate, grad_gate_out)
     moves.store(grad_up, grad_up_out)
-
     @pl.loop(0, width // 256)
     def _(i):
         at = lanes(i * 256, 256)
@@ -721,14 +751,6 @@
         part[:, :, at] = both.astype(BF16).reshape(8, rows, 256)
 
     moves.store(part, part_out)
-
-    @pl.loop(0, width // 256)
-    def _(i):
-        at = lanes(i * 256, 256)
-        times, block = columns_of(w_down, at)
-        rows_one[:, at] = times(mixed[...], block).astype(BF16)
-
-    moves.store(rows_one, down_out)
     moves.close()
 
 
@@ -904,19 +926,16 @@
         moves.load(grad_gate, feed.at[:, pl.ds(0, cols)]),
         moves.load(grad_up, feed.at[:, pl.ds(cols, cols)]),
     ]
-    collect_two = Collect(
-        moves, place, lambda j, t: part_two.at[place.rows_of[j] + t], part, first, ctx_in, pair_in, sending, True
-    )
     masks = [high, high | PAIR, 0, PAIR]
     sends = [m | low for m in masks]
     a, b, c, e = range(4)
     order = [
-        (cot_rows, sends[a]), (cot_rows, sends[b]), (normed_two, sends[a]), (cot_rows, masks[a]),
-        (normed_two, sends[b]), (cot_rows, masks[b]), (normed_two, masks[a]), (cot_rows, sends[e]),
-        (cot_rows, sends[c]), (normed_two, sends[e]), (normed_two, masks[b]), (normed_one, sends[a]),
-        (normed_one, sends[b]), (normed_one, sends[e]), (cot_rows, masks[e]), (cot_rows, masks[c]),
-        (normed_two, masks[e]), (normed_two, sends[c]), (normed_one, sends[c]), (normed_one, masks[a]),
-        (normed_one, masks[b]), (normed_one, masks[e]), (normed_two, masks[c]), (normed_one, masks[c]),
+        (cot_rows, sends[a]), (cot_rows, sends[b]), (cot_rows, masks[a]), (normed_two, sends[a]),
+        (cot_rows, sends[e]), (cot_rows, masks[b]), (normed_two, sends[b]), (cot_rows, masks[e]),
+        (normed_two, masks[a]), (cot_rows, sends[c]), (normed_two, masks[b]), (normed_one, sends[a]),
+        (normed_one, sends[b]), (normed_two, sends[e]), (normed_one, masks[b]), (normed_two, sends[c]),
+        (cot_rows, masks[c]), (normed_one, masks[a]), (normed_two, masks[e]), (normed_one, sends[e]),
+        (normed_two, masks[c]), (normed_one, sends[c]), (normed_one, masks[e]), (normed_one, masks[c]),
     ]
     blocks = Blocks(moves, place, lhs, order)
     ready_mixed = moves.load(mixed_t, mixed)
@@ -957,26 +976,7 @@
     qkv_s = Scatter(moves, place, by_rows(normed_one, dqkv), q_out0, q_in0, q_out1, q_in1, q_acc, q_pair, spare_qkv)
     out_s = Scatter(moves, place, out_product, o_out0, o_in0, o_out1, o_in1, o_acc, o_pair, spare_out)
 
-    ready_mixed()
-    down_s.send(a)
-    down_s.send(b)
-    collect_two.to_ctx()
-    for wait in ready_feed:
-        wait()
-    feed_s.send(a)
-    down_s.take(a)
-    feed_s.send(b)
-    collect_two.to_pair()
-    collect_hidden = Collect(
-        moves, place, lambda j, t: part_hidden.at[place.rows_of[j] + t], part.at[pl.ds(4, 4)],
-        first_h, ctx_h, pair_h, sending_h, True,
-    )
-    down_s.relay(a)
-    down_s.take(b)
-
-    collect_hidden.fold()
-    ready_mid()
-    collect_two.finish()
+    d = gain_q.shape[1]
     gain_m[...] = jnp.zeros_like(gain_m)
     gain_a[...] = jnp.zeros_like(gain_a)
     gain_h[...] = jnp.zeros_like(gain_h)
@@ -988,76 +988,12 @@
         grad_in[at] = g
         own[at] = g.astype(BF16)
 
-    row_loop(rows, back_two)
-    spread = Spread(moves, place, own, rows_mid)
-    down_s.relay(b)
-    feed_s.take(a)
-    down_s.send(e)
-    spread.from_pair()
-    down_s.send(c)
-    spread.from_ctx()
-    feed_s.send(e)
-    feed_s.relay(a)
-    spread.from_both()
-    for wait in ready_late:
-        wait()
-    spread.finish()
-    ready_hidden = moves.load(hidden, own)
-    collect_hidden.post_ctx()
-
-    @pl.loop(0, 4)
-    def _(i):
-        at = lanes(i * 2 * rows, 2 * rows)
-        datt[at] = dot_cols(rows_mid[at], w_out[...]).astype(BF16)
-
-    feed_s.take(b)
-
-    @pl.loop(0, 2)
-    def _(s):
-        attend_back_one(groups, s, qkv, att, datt, starts, cos, sin, gain_q, gain_k, dqkv, gain_h)
-
-    @pl.loop(0, width // tile)
-    def _(i):
-        at = lanes(i * tile, tile)
-        part[:, :, at] = dot_cols(dqkv[...], w_qkv[at]).astype(BF16).reshape(8, rows, tile)
-
-    collect_one = Collect(
-        moves, place, lambda j, t: part.at[place.rows_of[j] + t], None, first, ctx_in, pair_in, sending, False
-    )
-    qkv_s.send(a)
-    qkv_s.send(b)
-    out_s.send(a)
-    out_s.send(b)
-    collect_one.to_ctx()
-    feed_s.relay(b)
-    collect_hidden.post_pair()
-    qkv_s.send(e)
-    out_s.send(e)
-    down_s.take(e)
-    down_s.take(c)
-    feed_s.take(e)
-    collect_one.to_pair()
-    feed_s.send(c)
-    qkv_s.send(c)
-    out_s.send(c)
-    qkv_s.take(a)
-    qkv_s.take(b)
-    out_s.take(a)
-    out_s.take(b)
-    collect_one.finish()
-
-    ready_hidden()
-
     def back_one(at):
         grad_in[at] += norm_back(collect_one.total(at), own[at].astype(F32), gain_attn[...], gain_a)
 
-    row_loop(rows, back_one)
-
-    d = gain_q.shape[1]
-    tree[0, :, 0:width] = jnp.sum(gain_a[...], axis=0, keepdims=True)
-    tree[0, :, width : 2 * width] = jnp.sum(gain_m[...], axis=0, keepdims=True)
-    tree[0, :, 2 * width : 2 * width + d] = jnp.sum(gain_h[0], axis=0, keepdims=True)
-    tree[0, :, 2 * width + d : 2 * width + 2 * d] = jnp.sum(gain_h[1], axis=0, keepdims=True)
+    def end_hidden(at):
+        hidden_out[at] += ctx_h[1, at].astype(F32) + pair_h[at].astype(F32)
+
     partners = [place.sibling, place.chips[1], *[place.along(x) for x in bits], place.chips[2]]
     tree_waits = []
 
@@ -1098,38 +1034,118 @@
     def out_spare(j):
         return o_in0.at[j, :, pl.ds(0, half)]
 
+    def attend_part(s):
+        attend_back_one(groups, s, qkv, att, datt, starts, cos, sin, gain_q, gain_k, dqkv, gain_h)
+
+    ready_mixed()
+    down_s.send(a)
+    for wait in ready_feed:
+        wait()
+    down_s.send(b)
+    collect_two = Collect(
+        moves, place, lambda j, t: part_two.at[place.rows_of[j] + t], part, first, ctx_in, pair_in, sending, True
+    )
+    collect_two.to_ctx()
+    down_s.take(a)
+    collect_hidden = Collect(
+        moves, place, lambda j, t: part_hidden.at[place.rows_of[j] + t], part.at[pl.ds(4, 4)],
+        first_h, ctx_h, pair_h, sending_h, True,
+    )
+    feed_s.send(a)
+    collect_hidden.fold()
+    collect_two.to_pair()
+    down_s.send(e)
+    down_s.relay(a)
+    for wait in ready_late:
+        wait()
+    down_s.take(b)
+    collect_two.finish()
+    ready_mid()
+    row_loop(rows, back_two)
+    spread = Spread(moves, place, own, rows_mid)
+    down_s.relay(b)
+    feed_s.send(b)
+    down_s.take(e)
+    feed_s.take(a)
+    down_s.send(c)
+    spread.from_pair()
+    collect_hidden.post_ctx()
+    spread.from_ctx()
+    pair_final(down_s, down_other)
+    spread.from_both()
+    feed_s.take(b)
+    feed_s.relay(a)
+    spread.finish()
+    ready_hidden = moves.load(hidden, own)
+    @pl.loop(0, 4)
+    def _(i):
+        at = lanes(i * 2 * rows, 2 * rows)
+        datt[at] = dot_cols(rows_mid[at], w_out[...]).astype(BF16)
+
+    attend_part(0)
+    collect_hidden.post_pair()
+    attend_part(1)
+    out_s.send(a)
+    out_s.send(b)
+    @pl.loop(0, width // tile)
+    def _(i):
+        at = lanes(i * tile, tile)
+        part[:, :, at] = dot_cols(dqkv[...], w_qkv[at]).astype(BF16).reshape(8, rows, tile)
+
+    collect_one = Collect(
+        moves, place, lambda j, t: part.at[place.rows_of[j] + t], None, first, ctx_in, pair_in, sending, False
+    )
+    qkv_s.send(a)
+    qkv_s.send(b)
+    out_s.send(e)
+    feed_s.relay(b)
+    feed_s.send(e)
+    out_s.take(b)
+    collect_one.to_ctx()
+    qkv_s.take(b)
+    feed_s.send(c)
+    collect_one.to_pair()
+    out_s.take(e)
+    down_s.take(c)
+    out_s.send(c)
+    qkv_s.take(a)
+    feed_s.take(e)
+    pair_final(feed_s, feed_other)
+    collect_one.finish()
+    qkv_s.send(e)
+    ready_hidden()
+    row_loop(rows, back_one)
+    tree[0, :, 0:width] = jnp.sum(gain_a[...], axis=0, keepdims=True)
+    tree[0, :, width : 2 * width] = jnp.sum(gain_m[...], axis=0, keepdims=True)
+    tree[0, :, 2 * width : 2 * width + d] = jnp.sum(gain_h[0], axis=0, keepdims=True)
+    tree[0, :, 2 * width + d : 2 * width + 2 * d] = jnp.sum(gain_h[1], axis=0, keepdims=True)
     climb()
+    out_s.relay(b)
     qkv_s.relay(a)
+    climb()
+    out_s.take(a)
     qkv_s.relay(b)
-    out_s.relay(a)
-    out_s.relay(b)
-    climb()
-    pair_final(down_s, down_other)
-    climb()
-    own_final(down_s, down_own)
-    qkv_s.take(e)
-    out_s.take(e)
-    climb()
-    collect_hidden.came()
-
-    def end_hidden(at):
-        hidden_out[at] += ctx_h[1, at].astype(F32) + pair_h[at].astype(F32)
-
-    row_loop(rows, end_hidden)
-    pair_final(feed_s, feed_other)
     climb()
     feed_s.take(c)
-    qkv_s.take(c)
+    qkv_s.send(c)
+    collect_hidden.came()
+    row_loop(rows, end_hidden)
+    own_final(down_s, down_own)
+    climb()
+    own_final(feed_s, feed_own)
     out_s.take(c)
-    mates_final(qkv_s, 1, qkv_piece, qkv_spare, qkv_other)
     mates_final(out_s, 1, out_piece, out_spare, out_other)
-    own_final(feed_s, feed_own)
-    mates_final(qkv_s, 0, qkv_piece, qkv_spare, qkv_other)
-    mates_final(out_s, 0, out_piece, out_spare, out_other)
-    qkv_own[...] = qkv_piece(0, place.c)
-    out_own[...] = out_piece(0, place.c)
+    climb()
     climb()
     gains[...] = tree[len(partners)]
+    qkv_s.take(e)
+    qkv_s.take(c)
+    mates_final(qkv_s, 0, qkv_piece, qkv_spare, qkv_other)
+    qkv_own[...] = qkv_piece(0, place.c)
+    out_s.relay(a)
+    mates_final(qkv_s, 1, qkv_piece, qkv_spare, qkv_other)
+    mates_final(out_s, 0, out_piece, out_spare, out_other)
+    out_own[...] = out_piece(0, place.c)
     for scatter in (feed_s, down_s, qkv_s, out_s):
         scatter.close()
     for wait in finals:

time: 434 us -> 398 us (0.917); the launches traced: 434 us -> 390 us
  Pallas kernels: 431 us -> 387 us
    pallas_call x2, Pallas kernels: 424 us -> 380 us  [comm_call(): pl.pallas_call(functools.partial(kernel, bits, *more), out_shape=outs, in...]
where the time goes in v6:
time: 398 us; the launch traced here: 390 us
  Pallas kernels  387 us (97%)
    pallas_call x2, Pallas kernels, comm_call(): pl.pallas_call(functools.partial(kernel, bits, *more), out_shape=outs, in...  380 us

profile of v6, /device:TPU:0, one launch (start us, length us, event | category | flops | bytes accessed | tf_op | source)
XLA Modules:
  0.0 389.9 jit_solution(9696496398208863337)
XLA Ops:
  0.7 1.0 multiply_cosine_fusion
  1.7 1.1 pad_maximum_fusion.table
  2.7 198.7 %forward_kernel.1 = (f32[128,2048]{1,0:T(8,128)}, bf16[1024,2048]{1,0:T(8,128)(2,1)}, bf16[1024,2048]{1,0:T(8,128)(2,1)}, bf16[1024,2048]{1,0:T(8,128)(2,1)}, bf...) custom-call(bf16[128,2048]{1,0:T(8,128)(2,1)} %hidden.3, ...), custom_call_target="tpu_custom_call" | custom-call | flops 1342177280 | bytes 67108864 | tf_op jit(solution)/shard_map/forward_kernel/pallas_call | solution.py:1196
  201.5 181.3 %backward_kernel.1 = (f32[128,2048]{1,0:T(8,128)}, f32[128,2048]{1,0:T(8,128)}, f32[1,4352]{1,0:T(1,128)}, f32[256,1536]{1,0:T(8,128)}, bf16[256,1536]{1,0:T(8,1...) custom-call(bf16[128,2048]{1,0:T(8,128)(2,1)} %cot.3, ...), custom_call_target="tpu_custom_call" | custom-call | flops 838860800 | bytes 41943040 | tf_op jit(solution)/shard_map/backward_kernel/pallas_call | solution.py:1196
  382.8 6.6 %join_kernel.1 = (f32[128,1024]{1,0:T(8,128)}, f32[128,512]{1,0:T(8,128)}, f32[128,512]{1,0:T(8,128)}, f32[1024,128]{1,0:T(8,128)}, f32[256,1536]{1,0:T(8,128)},...) custom-call(f32[256,1536]{1,0:T(8,128)} %get-tuple-element.69.feed_o, ...), custom_call_target="tpu_custom_call" | custom-call | tf_op jit(solution)/shard_map/join_kernel/pallas_call | solution.py:1385
  (2 shorter events, 0.0 us)
